TPU v7x, 32 devices: a whole 2x2x4 slice. The times are simulated.
32 devices in a mesh: trade: 4 (over y, core), scen: 8 (over z, x).
Axes of the slice: x: 2, y: 2, z: 4, core: 2. Of those that a mesh axis runs over, the one named last changes fastest.
Arguments:
- factors: float32 [2048, 64], P('scen'), may hold values from -1 to 1
- feat_factor: int32 [1024], replicated, may hold values from 0 to 63
- feat_degree: int32 [1024], replicated, may hold values from 1 to 12
- coefficients: float32 [1024, 8192], P(None, 'trade'), may hold values from -0.1875 to 0.1875
- set_of_trade: int32 [8192], P('trade'), may hold values from 0 to 511, as said below
- party_of_set: int32 [512], P('trade'), may hold values from 0 to 511
- threshold: float32 [512], replicated, may hold values from 0 to 4
- weight: float32 [512], replicated, may hold values from 0.5 to 2
Outputs:
- xva: float32 [512], P('trade')
- coef_sens: float32 [1024, 8192], P('scen', 'trade')
- feature_sens: float32 [1024, 2048], P('trade', 'scen')
Inputs may be any that keep to these rules, and one draw needn't show every extreme that they name: `set_of_trade`: each netting set holds exactly 16 trades; the trades of aligned block b of 2048 trades belong to sets b * 128 to (b + 1) * 128 - 1.
All inputs are finite; a program needn't handle non-finite values.
Results may differ from a plain program's by a relative error of at most 0.000073.
Values sent between devices are 32-bit elements; how exact they have to be, the bound alone decides.
No kernel may reach another device: no remote copies, remote signals or barrier semaphores. Data moves between devices by JAX's collectives and lax.ppermute only.
A program may use at most 64 MiB of HBM per device.

v0:
```python
import jax
import jax.numpy as jnp
from jax import lax
from jax.sharding import PartitionSpec as P

MAXDEG = 12
SET_SIZE = 16


highest = lax.Precision.HIGHEST


def chebyshev(points, degrees):
    before = jnp.ones_like(points)
    current = points
    result = jnp.where(degrees[None, :] == 1, current, jnp.zeros_like(points))
    for order in range(2, MAXDEG + 1):
        before, current = (current, 2.0 * points * current - before)
        result = jnp.where(degrees[None, :] == order, current, result)
    return result


def contract(left, right, left_dim, right_dim):
    return lax.dot_general(left, right, (((left_dim,), (right_dim,)), ((), ())), precision=highest)


def local(
    factors, feat_factor, feat_degree, coefficients, set_of_trade, party_of_set, threshold, weight
):
    scen_rows = factors.shape[0]
    scen_total = scen_rows * lax.axis_size("scen")
    width = coefficients.shape[0]
    trade_cols = coefficients.shape[1]
    set_count = trade_cols // SET_SIZE
    party_total = threshold.shape[0]
    party_own = party_total // lax.axis_size("trade")
    lookup = (
        lax.broadcasted_iota(jnp.int32, (factors.shape[1], width), 0) == feat_factor[None, :]
    ).astype(jnp.float32)
    points = jnp.dot(factors, lookup, precision=highest)
    phi = chebyshev(points, feat_degree)
    member = (
        set_of_trade[:, None] % set_count
        == lax.broadcasted_iota(jnp.int32, (trade_cols, set_count), 1)
    ).astype(jnp.float32)
    assign = (
        party_of_set[:, None] == lax.broadcasted_iota(jnp.int32, (set_count, party_total), 1)
    ).astype(jnp.float32)
    folded = jnp.dot(coefficients, member, precision=highest)
    exposure = jnp.dot(phi, folded, precision=highest)
    partial_value = jnp.dot(exposure, assign, precision=highest)
    first = lax.axis_index("trade") * party_own
    own_weight = lax.dynamic_slice_in_dim(weight, first, party_own, 0)
    own_sum = lax.psum_scatter(partial_value, "trade", scatter_dimension=1, tiled=True)
    own_shift = own_sum - lax.dynamic_slice_in_dim(threshold, first, party_own, 0)[None, :]
    own_adj = own_weight[None, :] * jax.nn.sigmoid(own_shift)
    party_adj = lax.all_gather(own_adj, "trade", axis=1, tiled=True)
    local_total = own_weight * jnp.sum(jax.nn.softplus(own_shift), axis=0)
    xva = lax.psum(local_total, "scen") / scen_total
    set_adj = contract(party_adj, assign, 1, 1)
    block = phi
    set_grad = lax.psum_scatter(
        contract(block, set_adj, 0, 0) / scen_total, "scen", scatter_dimension=0, tiled=True
    )
    coef_sens = contract(set_grad, member, 1, 1)
    block = folded
    feature_sens = lax.psum_scatter(
        contract(block, set_adj, 1, 1), "trade", scatter_dimension=0, tiled=True
    )
    return (xva, coef_sens, feature_sens)


def solution(mesh):
    in_specs = (P("scen", None), P(), P(), P(None, "trade"), P("trade"), P("trade"), P(), P())
    out_specs = (P("trade"), P("scen", "trade"), P("trade", "scen"))
    return jax.shard_map(local, mesh=mesh, in_specs=in_specs, out_specs=out_specs, check_vma=False)
```

profile of v0, /device:TPU:0, one launch (start us, length us, event | category | flops | bytes accessed | tf_op | source)
XLA Modules:
  0.0 156.8 jit_solution(4807160725196838700)
XLA Ops:
  7.2 0.0 copy-start
  7.2 0.0 copy-start.2
  7.2 0.0 reduce-scatter.4.cloned.1.call-start
  7.2 0.7 add_select_fusion
  7.9 0.7 broadcast_compare_fusion.11
  8.6 8.1 %fusion.9 = f32[128,1024]{1,0:T(8,128)S(1)} fusion(f32[1024,2048]{1,0:T(8,128)} %param.11, s32[2048]{0:T(1024)S(1)} %add_select_fusion), kind=kOutput, calls=%fused_computation.22 | convolution fusion | flops 3221749760 | bytes 8921088 | tf_op jit(solution)/shard_map/dot_general | solution.py:49
  16.7 0.0 copy-start.1
  16.7 0.0 copy-done
  16.7 0.0 copy-done.2
  16.7 3.9 %select_select_fusion = f32[256,1024]{0,1:T(8,128)S(1)} fusion(f32[256,64]{0,1:T(8,128)S(1)} %copy-done, pred[1024]{0:T(1024)(128)(4,1)S(1)} %get-tuple-element.15, pred[1024]{0:T(1024)(128)(4,1)S(1)} %get-tuple-element.16, pred[1024]{0:T(1024)(128)(4,1)S(1)} %get-tuple-element.6, pred[1024]{0:T(1024)(128)(4,1)S(1)} %get-tuple-element.7, ...), kind=kOutput, calls=%fused_computation.5 | convolution fusion | flops 210567168 | bytes 1130496 | tf_op jit(solution)/shard_map/dot_general | solution.py:40
  20.7 1.8 %fusion.21 = f32[256,128]{1,0:T(8,128)S(1)} fusion(f32[256,1024]{0,1:T(8,128)S(1)} %select_select_fusion, f32[128,1024]{1,0:T(8,128)S(1)} %fusion.9), kind=kOutput, calls=%fused_computation.53 | convolution fusion | flops 402653184 | bytes 1703936 | tf_op jit(solution)/shard_map/dot_general | solution.py:50
  22.5 0.0 copy-done.1
  22.5 1.2 fusion.14
  23.8 0.0 reduce-scatter.4.cloned.1.call-update
  23.8 0.0 reduce-scatter.6.cloned.1.call-start
  23.9 0.8 dynamic_slice.7
  24.6 23.7 %reduce-scatter.4.cloned.1.call-done = f32[256,128]{1,0:T(8,128)} async-done(((f32[256,512]{1,0:T(8,128)}), f32[256,128]{1,0:T(8,128)}) %reduce-scatter.4.cloned.1.call-update) | async-done | bytes 131088 | tf_op jit(solution)/shard_map/reduce_scatter | solution.py:54
  48.3 1.0 fusion.15
  49.3 0.8 fusion.20
  50.1 0.9 divide_multiply_fusion
  51.0 6.6 %all_gather.3 = f32[256,512]{1,0:T(8,128)S(1)} all-gather(f32[256,128]{1,0:T(8,128)S(1)} %divide_multiply_fusion), channel_id=1, replica_groups=mesh['trade'=4,'scen'=8] {'trade'}, dimensions={1}, use_global_device_ids=true | all-gather | bytes 655360 | tf_op jit(solution)/shard_map/all_gather | solution.py:57
  57.6 0.5 fusion.13
  58.1 1.8 %convolution_multiply_fusion = f32[1024,128]{1,0:T(8,128)} fusion(f32[256,1024]{0,1:T(8,128)S(1)} %select_select_fusion, f32[256,128]{1,0:T(8,128)S(1)} %fusion.13), kind=kOutput, calls=%fused_computation.1 | convolution fusion | flops 402784256 | bytes 1703936 | tf_op jit(solution)/shard_map/dot_general | solution.py:24
  59.9 0.0 reduce-scatter.6.cloned.1.call-update
  59.9 0.0 reduce-scatter.8.cloned.1.call-start
  59.9 2.0 %fusion.22 = f32[1024,256]{1,0:T(8,128)} fusion(f32[128,1024]{1,0:T(8,128)S(1)} %fusion.9, f32[256,128]{1,0:T(8,128)S(1)} %fusion.13), kind=kOutput, calls=%fused_computation.54 | convolution fusion | flops 402653184 | bytes 1703936 | tf_op jit(solution)/shard_map/dot_general | solution.py:24
  62.0 0.0 reduce-scatter.8.cloned.1.call-update
  62.0 21.5 %psum.7 = f32[128]{0:T(128)S(1)} all-reduce(f32[128]{0:T(128)S(1)} %get-tuple-element.3), channel_id=1, replica_groups=mesh['trade'=4,'scen'=8] {'scen'}, use_global_device_ids=true, to_apply=%region_2.3 | all-reduce | flops 128 | bytes 1024 | tf_op jit(solution)/shard_map/psum | solution.py:59
  83.5 0.5 broadcast_multiply_fusion
  84.0 39.3 %reduce-scatter.6.cloned.1.call-done = f32[128,128]{1,0:T(8,128)} async-done(((f32[1024,128]{1,0:T(8,128)}), f32[128,128]{1,0:T(8,128)}) %reduce-scatter.6.cloned.1.call-update) | async-done | bytes 65552 | tf_op jit(solution)/shard_map/reduce_scatter | solution.py:62
  123.3 2.6 %fusion = f32[128,2048]{1,0:T(8,128)} fusion(f32[128,128]{1,0:T(8,128)} %reduce-scatter.6.cloned.1.call-done, s32[2048]{0:T(1024)S(1)} %add_select_fusion), kind=kOutput, calls=%fused_computation.3 | convolution fusion | flops 402915328 | bytes 1122304 | tf_op jit(solution)/shard_map/dot_general | solution.py:24
  125.9 24.3 %reduce-scatter.8.cloned.1.call-done = f32[256,256]{1,0:T(8,128)} async-done(((f32[1024,256]{1,0:T(8,128)}), f32[256,256]{1,0:T(8,128)}) %reduce-scatter.8.cloned.1.call-update) | async-done | bytes 262160 | tf_op jit(solution)/shard_map/reduce_scatter | solution.py:67
Async XLA Ops:
  7.2 9.6 %copy-start = (f32[256,64]{0,1:T(8,128)S(1)}, f32[256,64]{0,1:T(8,128)}, u32[]{:S(2)}) copy-start(f32[256,64]{0,1:T(8,128)} %param.8) | copy-start | bytes 196612
  7.2 9.5 %copy-start.2 = (s32[1024]{0:T(1024)S(1)}, s32[1024]{0:T(1024)}, u32[]{:S(2)}) copy-start(s32[1024]{0:T(1024)} %param.9) | copy-start | bytes 12292
  7.2 41.1 %reduce-scatter.4.cloned.1.call-start = ((), (), s32[]{:S(2)}) async-start(), calls=%async_computation.3 | async-start | bytes 655360 | tf_op jit(solution)/shard_map/reduce_scatter | solution.py:54
  16.7 5.8 %copy-start.1 = (s32[128]{0:T(128)S(1)}, s32[128]{0:T(128)}, u32[]{:S(2)}) copy-start(s32[128]{0:T(128)} %param.13) | copy-start | bytes 1540
  23.8 99.5 %reduce-scatter.6.cloned.1.call-start = ((), (), s32[]{:S(2)}) async-start(), calls=%async_computation.4 | async-start | bytes 589824 | tf_op jit(solution)/shard_map/reduce_scatter | solution.py:62
  59.9 90.3 %reduce-scatter.8.cloned.1.call-start = ((), (), s32[]{:S(2)}) async-start(), calls=%async_computation.5 | async-start | bytes 1310720 | tf_op jit(solution)/shard_map/reduce_scatter | solution.py:67
Sparse Core Ops, SparseCore 0:
  23.9 24.3 reduce-scatter.3
  60.0 63.1 reduce-scatter.5
  126.4 23.8 reduce-scatter.7
where the time goes:
time: 157 us
  waiting for transfers between devices  87.4 us (56%)
  blocking collectives  28 us (18%)
  matrix products  22 us (14%)
  between operations  13.8 us (9%)
  other arithmetic  4.63 us (3%)
    reduce_scatter x1, waiting for transfers between devices, local(): lax.psum_scatter(contract(block, set_adj, 0, 0) / scen_total, 'scen', sca...  39.3 us
    reduce_scatter x1, waiting for transfers between devices, local(): lax.psum_scatter(contract(block, set_adj, 1, 1), 'trade', scatter_dimensi...  24.3 us
    reduce_scatter x1, waiting for transfers between devices, local(): lax.psum_scatter(partial_value, 'trade', scatter_dimension=1, tiled=True)  23.7 us
    psum x1, blocking collectives, local(): xva = lax.psum(local_total, 'scen') / scen_total  21.5 us
    dot_general x1, matrix products, local(): folded = jnp.dot(coefficients, member, precision=highest)  8.05 us
    dot_general x4, matrix products, contract(): lax.dot_general(left, right, (((left_dim,), (right_dim,)), ((), ())), pre...  6.91 us
    all_gather x1, blocking collectives, local(): party_adj = lax.all_gather(own_adj, 'trade', axis=1, tiled=True)  6.59 us
    dot_general x1, matrix products, local(): points = jnp.dot(factors, lookup, precision=highest)  3.94 us
  transfers between devices with their start and end apart: 3, of which 3 were waited for; matrix products, arithmetic and copies ran while one was open for 4% of the time, Pallas kernels for 0%

commit v1 on v0

v1 whole, which is shorter than its diff:
```python
import functools

import jax
import jax.numpy as jnp
from jax import lax
from jax.experimental import pallas as pl
from jax.experimental.pallas import tpu as pltpu
from jax.sharding import PartitionSpec as P

MAXDEG = 12
SET_SIZE = 16
INFO = 8

f32 = jnp.float32
bf16 = jnp.bfloat16
VMEM = pl.BlockSpec(memory_space=pltpu.VMEM)
ANY = pl.BlockSpec(memory_space=pl.ANY)


def split(value):
    high = value.astype(bf16)
    low = (value - high.astype(f32)).astype(bf16)
    return high, low


def nn(left, right):
    return lax.dot_general(left, right, (((1,), (0,)), ((), ())), preferred_element_type=f32)


def nt(left, right):
    return lax.dot_general(left, right, (((1,), (1,)), ((), ())), preferred_element_type=f32)


def iota(shape, dim):
    return lax.broadcasted_iota(jnp.int32, shape, dim)


def column(row):
    n = row.shape[1]
    return jnp.transpose(jnp.broadcast_to(row.astype(f32), (n, n)))


def one_hot(test):
    return jnp.where(test, jnp.float32(1), jnp.float32(0)).astype(bf16)


def pick(table, ids, rows):
    lanes = table.shape[1]
    total = jnp.zeros((1, ids.shape[1]), f32)
    for r in range(rows):
        here = column(table[r : r + 1, :])
        where = iota((lanes, ids.shape[1]), 0) + r * lanes == ids
        total = total + jnp.sum(jnp.where(where, here[:, : ids.shape[1]], 0.0), axis=0, keepdims=True)
    return total


def first_kernel(n_trade, fact_ref, factor_ref, degree_ref, coef_hbm, set_ref, party_ref, thr_ref, wgt_ref, *rest):
    folded_refs = rest[:n_trade]
    expo_ref, high_ref, low_ref, coef_buf, sems = rest[n_trade:]
    me = lax.axis_index("trade")
    width, cols = coef_hbm.shape
    sets = cols // SET_SIZE
    nfac, scen = fact_ref.shape
    block = 128
    own = width // n_trade
    steps = width // block
    per = own // block

    def start_row(step):
        return pl.multiple_of((me ^ (step // per)) * own + (step % per) * block, block)

    def copy(step):
        return pltpu.make_async_copy(
            coef_hbm.at[pl.ds(start_row(step), block), :], coef_buf.at[step], sems.at[step]
        )

    for step in range(steps):
        copy(step).start()
    points = fact_ref[...]
    before, current = jnp.ones_like(points), points
    high, low = [], []
    for order in range(1, MAXDEG + 1):
        if order > 1:
            before, current = current, 2.0 * points * current - before
        a, b = split(current)
        high.append(a)
        low.append(b)
    high = jnp.concatenate(high, axis=0)
    low = jnp.concatenate(low, axis=0)
    member = one_hot(set_ref[...] - me * sets == iota((sets, cols), 0))
    party = party_ref[...]
    rows = thr_ref.shape[0]
    thr_row = pick(thr_ref[...], party, rows)
    wgt_row = pick(wgt_ref[...], party, rows)
    info = jnp.where(
        iota((INFO, sets), 0) == 0,
        party.astype(f32),
        jnp.where(iota((INFO, sets), 0) == 1, thr_row, wgt_row),
    )
    expo_ref[sets:, :] = jnp.zeros((INFO, scen), f32)
    expo_ref[sets:, :sets] = info
    exposure = jnp.zeros((sets, scen), f32)
    for step in range(steps):
        row = start_row(step)
        line = lax.div(row, block)
        key = factor_ref[pl.ds(line, 1), :] + nfac * (degree_ref[pl.ds(line, 1), :] - 1)
        key = column(key)
        key = jnp.concatenate([key] * (MAXDEG * nfac // block), axis=1).astype(jnp.int32)
        chosen = one_hot(key == iota(key.shape, 1))
        phi_high = nn(chosen, high).astype(bf16)
        phi_low = nn(chosen, low).astype(bf16)
        high_ref[pl.ds(row, block), :] = phi_high
        low_ref[pl.ds(row, block), :] = phi_low
        copy(step).wait()
        coef_high, coef_low = split(coef_buf[step])
        folded = nt(coef_high, member) + nt(coef_low, member)
        folded_refs[step // per][pl.ds((step % per) * block, block), :] = folded
        turned_high, turned_low = split(jnp.transpose(folded))
        exposure = exposure + nn(turned_high, phi_high) + nn(turned_low, phi_high) + nn(turned_high, phi_low)
    expo_ref[:sets, :] = exposure


def second_kernel(n_trade, n_scen, all_ref, high_ref, low_ref, thr_ref, wgt_ref, adj_ref, *chunk_refs):
    trade, scen = lax.axis_index("trade"), lax.axis_index("scen")
    stride = all_ref.shape[0] // n_trade
    sets = stride - INFO
    chunk = high_ref.shape[0] // n_scen
    infos = [all_ref[a * stride + sets : (a + 1) * stride, :sets] for a in range(n_trade)]
    party_row = jnp.concatenate([info[0:1, :] for info in infos], axis=1).astype(jnp.int32)
    expo = [split(all_ref[a * stride : a * stride + sets, :]) for a in range(n_trade)]
    expo_high = jnp.concatenate([e[0] for e in expo], axis=0)
    expo_low = jnp.concatenate([e[1] for e in expo], axis=0)
    total = party_row.shape[1]
    for a in range(n_trade):
        turned = jnp.transpose(infos[a])
        same = one_hot(turned[:, 0:1].astype(jnp.int32) == party_row)
        netted = nn(same, expo_high) + nn(same, expo_low)
        adj_ref[a * sets : (a + 1) * sets, :] = turned[:, 2:3] * jax.nn.sigmoid(netted - turned[:, 1:2])
    own = one_hot(iota((sets, total), 0) + trade * sets == party_row)
    netted = nn(own, expo_high) + nn(own, expo_low)
    thr_own = column(thr_ref[pl.ds(trade, 1), :])
    soft = jax.nn.softplus(netted - thr_own[:, 0:1])
    summed = jnp.sum(soft, axis=1, keepdims=True)
    xva = jnp.transpose(jnp.broadcast_to(summed, (sets, sets)))[0:INFO, :] * wgt_ref[pl.ds(trade, 1), :]
    mine = adj_ref[pl.ds(pl.multiple_of(trade * sets, sets), sets), :]
    adj_high, adj_low = split(mine)
    for k in range(n_scen):
        rows = pl.ds(pl.multiple_of((scen ^ k) * chunk, chunk), chunk)
        phi_high, phi_low = high_ref[rows, :], low_ref[rows, :]
        part = nt(phi_high, adj_high) + nt(phi_high, adj_low) + nt(phi_low, adj_high)
        chunk_refs[k][:chunk, :] = part
        chunk_refs[k][chunk:, :] = xva


def feature_kernel(n_trade, adj_ref, *refs):
    folded_refs, out_ref = refs[:n_trade], refs[n_trade]
    trade = lax.axis_index("trade")
    sets = folded_refs[0].shape[1]
    total = jnp.zeros(out_ref.shape, f32)
    for k in range(n_trade):
        adj_high, adj_low = split(adj_ref[pl.ds(pl.multiple_of((trade ^ k) * sets, sets), sets), :])
        high, low = split(folded_refs[k][...])
        total = total + nn(high, adj_high) + nn(low, adj_high) + nn(high, adj_low)
    out_ref[...] = total


def last_kernel(n_scen, scale, set_ref, *refs):
    chunk_refs, xva_ref, out_ref = refs[:n_scen], refs[n_scen], refs[n_scen + 1]
    trade = lax.axis_index("trade")
    rows, cols = out_ref.shape
    sets = cols // SET_SIZE
    member = one_hot(set_ref[...] - trade * sets == iota((sets, cols), 0))
    total = chunk_refs[0][...]
    for k in range(1, n_scen):
        total = total + chunk_refs[k][...]
    total = total * scale
    xva_ref[...] = total[rows : rows + 1, :]
    high, low = split(total[:rows, :])
    out_ref[...] = nn(high, member) + nn(low, member)


def call(kernel, out_shape, in_specs, scratch=(), flops=10**9, moved=10**6, name=None):
    return pl.pallas_call(
        kernel,
        out_shape=out_shape,
        in_specs=in_specs,
        out_specs=jax.tree.map(lambda _: VMEM, out_shape),
        scratch_shapes=scratch,
        cost_estimate=pl.CostEstimate(flops=flops, bytes_accessed=moved, transcendentals=0),
        name=name,
    )


def local(
    factors, feat_factor, feat_degree, coefficients, set_of_trade, party_of_set, threshold, weight
):
    n_trade, n_scen = lax.axis_size("trade"), lax.axis_size("scen")
    scen, nfac = factors.shape
    width, cols = coefficients.shape
    sets = cols // SET_SIZE
    lanes = threshold.shape[0] // n_trade
    struct = jax.ShapeDtypeStruct
    thr = threshold.reshape(n_trade, lanes)
    wgt = weight.reshape(n_trade, lanes)
    set_row = set_of_trade.reshape(1, cols)
    own = width // n_trade
    outs = call(
        functools.partial(first_kernel, n_trade),
        [struct((own, sets), f32)] * n_trade
        + [struct((sets + INFO, scen), f32), struct((width, scen), bf16), struct((width, scen), bf16)],
        [VMEM, VMEM, VMEM, ANY, VMEM, VMEM, VMEM, VMEM],
        [pltpu.VMEM((width // 128, 128, cols), f32), pltpu.SemaphoreType.DMA((width // 128,))],
        name="first",
    )(
        factors.T,
        feat_factor.reshape(width // 128, 128),
        feat_degree.reshape(width // 128, 128),
        coefficients,
        set_row,
        party_of_set.reshape(1, sets),
        thr,
        wgt,
    )
    folded, (expo, high, low) = outs[:n_trade], outs[n_trade:]
    everything = lax.all_gather(expo, "trade", axis=0, tiled=True)
    chunk = width // n_scen
    outs = call(
        functools.partial(second_kernel, n_trade, n_scen),
        [struct((n_trade * sets, scen), f32)] + [struct((chunk + INFO, sets), f32)] * n_scen,
        [VMEM] * 5,
        name="second",
    )(everything, high, low, thr, wgt)
    adj, chunks = outs[0], outs[1:]
    chunks = [chunks[0]] + [
        lax.ppermute(chunks[k], "scen", [(i, i ^ k) for i in range(n_scen)]) for k in range(1, n_scen)
    ]
    others = lax.optimization_barrier((adj, *folded[1:]))
    adj, later = others[0], others[1:]
    folded = [folded[0]] + [
        lax.ppermute(later[k - 1], "trade", [(i, i ^ k) for i in range(n_trade)])
        for k in range(1, n_trade)
    ]
    feature_sens = call(
        functools.partial(feature_kernel, n_trade), struct((own, scen), f32), [VMEM] * (n_trade + 1),
        name="feature",
    )(adj, *folded)
    xva, coef_sens = call(
        functools.partial(last_kernel, n_scen, 1.0 / (scen * n_scen)),
        [struct((1, sets), f32), struct((chunk, cols), f32)],
        [VMEM] * (n_scen + 1),
        name="last",
    )(set_row, *chunks)
    return (xva.reshape(sets), coef_sens, feature_sens)


def solution(mesh):
    in_specs = (P("scen", None), P(), P(), P(None, "trade"), P("trade"), P("trade"), P(), P())
    out_specs = (P("trade"), P("scen", "trade"), P("trade", "scen"))
    return jax.shard_map(local, mesh=mesh, in_specs=in_specs, out_specs=out_specs, check_vma=False)
```

time: 157 us -> 51.2 us (0.33)
  waiting for transfers between devices: 87.4 us -> 7.58 us
  matrix products: 22 us -> 0 us
  Pallas kernels: 0 us -> 19.2 us
  blocking collectives: 28 us -> 10.4 us
  between operations: 13.8 us -> 0.73 us
  starting transfers between devices: 0.12 us -> 11.6 us
  other arithmetic: 4.63 us -> 0 us
    reduce_scatter x3 -> x0, waiting for transfers between devices: 87.3 us -> none  [the longest x1 39.3 us: local(): lax.psum_scatter(contract(block, set_adj, 0, 0) / scen_total, 'scen', sca...]
    dot_general x8 -> x0, matrix products: 22 us -> none  [the longest x1 8.05 us: local(): folded = jnp.dot(coefficients, member, precision=highest)]
    psum x1 -> x0, blocking collectives: 21.5 us -> none  [local(): xva = lax.psum(local_total, 'scen') / scen_total]
    pallas_call x0 -> x4, Pallas kernels: none -> 19.2 us  [the longest x1 10.6 us: local(): call(functools.partial(first_kernel, n_trade), [struct((own, sets), f32)]...]
    ppermute x0 -> x10, starting transfers between devices: none -> 11.6 us  [the longest x7 11.1 us: local(): lax.ppermute(chunks[k], 'scen', [(i, i ^ k) for i in range(n_scen)])]
    ppermute x0 -> x10, waiting for transfers between devices: none -> 7.58 us  [the longest x7 6.64 us: local(): lax.ppermute(chunks[k], 'scen', [(i, i ^ k) for i in range(n_scen)])]
    all_gather x1, blocking collectives: 6.59 us -> 10.4 us  [local(): everything = lax.all_gather(expo, 'trade', axis=0, tiled=True)]
    mul x2 -> x0, other arithmetic: 1.7 us -> none  [the longest x1 0.95 us: local(): own_adj = own_weight[None, :] * jax.nn.sigmoid(own_shift)]
  transfers between devices with their start and end apart: 3 -> 10, of which waited for: 3 -> 3; matrix products, arithmetic and copies ran while one was open for 4% -> 0% of each run, Pallas kernels for 0% -> 5%
where the time goes in v1:
time: 51.2 us; the launch traced here: 50.8 us
  Pallas kernels  19.2 us (38%)
  starting transfers between devices  11.6 us (23%)
  blocking collectives  10.4 us (20%)
  waiting for transfers between devices  7.58 us (15%)
  local copies, waits for them, and re-layouts  1.27 us (2%)
  between operations  0.73 us (1%)
    ppermute x7, starting transfers between devices, local(): lax.ppermute(chunks[k], 'scen', [(i, i ^ k) for i in range(n_scen)])  11.1 us
    pallas_call x1, Pallas kernels, local(): call(functools.partial(first_kernel, n_trade), [struct((own, sets), f32)]...  10.6 us
    all_gather x1, blocking collectives, local(): everything = lax.all_gather(expo, 'trade', axis=0, tiled=True)  10.4 us
    ppermute x7, waiting for transfers between devices, local(): lax.ppermute(chunks[k], 'scen', [(i, i ^ k) for i in range(n_scen)])  6.64 us
    pallas_call x1, Pallas kernels, local(): call(functools.partial(second_kernel, n_trade, n_scen), [struct((n_trade...  3.57 us
    pallas_call x1, Pallas kernels, local(): call(functools.partial(last_kernel, n_scen, 1.0 / (scen * n_scen)), [stru...  2.57 us
    pallas_call x1, Pallas kernels, local(): call(functools.partial(feature_kernel, n_trade), struct((own, scen), f32)...  2.5 us
    unnamed x20, local copies, waits for them, and re-layouts  1.27 us
  transfers between devices with their start and end apart: 10, of which 3 were waited for; matrix products, arithmetic and copies ran while one was open for 0% of the time, Pallas kernels for 5%

profile of v1, /device:TPU:0, one launch (start us, length us, event | category | flops | bytes accessed | tf_op | source)
XLA Modules:
  0.0 50.8 jit_solution(4404342453172515401)
XLA Ops:
  0.6 10.6 %first.1 = (f32[256,128]{1,0:T(8,128)}, f32[256,128]{1,0:T(8,128)}, f32[256,128]{1,0:T(8,128)}, f32[256,128]{1,0:T(8,128)}, f32[136,256]{1,0:T(8,128)}, /*index=...) custom-call(f32[64,256]{1,0:T(8,128)} %bitcast.8, s32[8,128]{1,0:T(8,128)} %bitcast.11, s32[8,128]{1,0:T(8,128)} %bitcast.12, ...), custom_call_target="tpu_custom_call" | custom-call | flops 1000000000 | bytes 1000000 | tf_op jit(solution)/shard_map/first/pallas_call | solution.py:207
  11.2 10.4 %all_gather.3.all_ref = f32[544,256]{1,0:T(8,128)} all-gather(f32[136,256]{1,0:T(8,128)} %get-tuple-element.25), channel_id=1, replica_groups=mesh['trade'=4,'scen'=8] {'trade'}, dimensions={0}, use_global_device_ids=true | all-gather | bytes 696320 | tf_op jit(solution)/shard_map/all_gather | solution.py:225
  21.7 3.6 %second.1 = (f32[512,256]{1,0:T(8,128)}, f32[136,128]{1,0:T(8,128)}, f32[136,128]{1,0:T(8,128)}, f32[136,128]{1,0:T(8,128)}, f32[136,128]{1,0:T(8,128)}, /*index...) custom-call(f32[544,256]{1,0:T(8,128)} %all_gather.3.all_ref, ...), custom_call_target="tpu_custom_call" | custom-call | flops 1000000000 | bytes 1000000 | tf_op jit(solution)/shard_map/second/pallas_call | solution.py:227
  25.2 1.5 %collective-permute-start = (f32[136,128]{1,0:T(8,128)}, f32[136,128]{1,0:T(8,128)S(1)}, u32[]{:S(2)}, u32[]{:S(2)}) collective-permute-start(f32[136,128]{1,0:T(8,128)} %get-tuple-element.29), channel_id=1, source_target_pairs={{0,1},{1,0},{2,3},{3,2},{4,5},{5,4},{6,7},{7,6},{8,9},{9,8},{10,11... | collective-permute-start | bytes 208904 | tf_op jit(solution)/shard_map/ppermute | solution.py:235
  26.7 1.6 %collective-permute-start.1 = (f32[136,128]{1,0:T(8,128)}, f32[136,128]{1,0:T(8,128)S(1)}, u32[]{:S(2)}, u32[]{:S(2)}) collective-permute-start(f32[136,128]{1,0:T(8,128)} %get-tuple-element.30), channel_id=1, source_target_pairs={{0,2},{1,3},{2,0},{3,1},{4,6},{5,7},{6,4},{7,5},{8,10},{9,11},{10,... | collective-permute-start | bytes 208904 | tf_op jit(solution)/shard_map/ppermute | solution.py:235
  28.3 0.4 collective-permute-start.2
  28.7 2.6 %collective-permute-start.3 = (f32[136,128]{1,0:T(8,128)}, f32[136,128]{1,0:T(8,128)S(1)}, u32[]{:S(2)}, u32[]{:S(2)}) collective-permute-start(f32[136,128]{1,0:T(8,128)} %get-tuple-element.32), channel_id=1, source_target_pairs={{0,4},{1,5},{2,6},{3,7},{4,0},{5,1},{6,2},{7,3},{8,12},{9,13},{10,... | collective-permute-start | bytes 208904 | tf_op jit(solution)/shard_map/ppermute | solution.py:235
  31.3 1.3 %collective-permute-start.4 = (f32[136,128]{1,0:T(8,128)}, f32[136,128]{1,0:T(8,128)S(1)}, u32[]{:S(2)}, u32[]{:S(2)}) collective-permute-start(f32[136,128]{1,0:T(8,128)} %get-tuple-element.33), channel_id=1, source_target_pairs={{0,5},{1,4},{2,7},{3,6},{4,1},{5,0},{6,3},{7,2},{8,13},{9,12},{10,... | collective-permute-start | bytes 208904 | tf_op jit(solution)/shard_map/ppermute | solution.py:235
  32.6 0.0 collective-permute-done.refs_1_
  32.6 0.0 copy-start.3
  32.6 3.6 %collective-permute-start.5 = (f32[136,128]{1,0:T(8,128)}, f32[136,128]{1,0:T(8,128)S(1)}, u32[]{:S(2)}, u32[]{:S(2)}) collective-permute-start(f32[136,128]{1,0:T(8,128)} %get-tuple-element.34), channel_id=1, source_target_pairs={{0,6},{1,7},{2,4},{3,5},{4,2},{5,3},{6,0},{7,1},{8,14},{9,15},{10,... | collective-permute-start | bytes 208904 | tf_op jit(solution)/shard_map/ppermute | solution.py:235
  36.2 0.0 collective-permute-done.1.refs_2_
  36.2 0.0 copy-start.4
  36.2 0.2 collective-permute-start.6
  36.4 0.0 collective-permute-done.2.refs_3_
  36.4 0.0 copy-start.5
  36.4 0.0 collective-permute-start.7
  36.4 0.0 collective-permute-done.3.refs_4_
  36.4 0.0 copy-start.6
  36.4 0.4 collective-permute-start.8
  36.9 5.4 %collective-permute-done.4.refs_5_ = f32[136,128]{1,0:T(8,128)S(1)} collective-permute-done((f32[136,128]{1,0:T(8,128)}, f32[136,128]{1,0:T(8,128)S(1)}, u32[]{:S(2)}, u32[]{:S(2)}) %collective-permute-start.4) | collective-permute-done | bytes 69664 | tf_op jit(solution)/shard_map/ppermute | solution.py:235
  42.2 0.0 copy-start.7
  42.2 0.0 collective-permute-start.9
  42.2 0.0 collective-permute-done.5.refs_6_
  42.2 0.0 copy-start.8
  42.2 1.3 %collective-permute-done.6.refs_7_ = f32[136,128]{1,0:T(8,128)S(1)} collective-permute-done((f32[136,128]{1,0:T(8,128)}, f32[136,128]{1,0:T(8,128)S(1)}, u32[]{:S(2)}, u32[]{:S(2)}) %collective-permute-start.6) | collective-permute-done | bytes 69664 | tf_op jit(solution)/shard_map/ppermute | solution.py:235
  43.5 0.0 copy-start.9
  43.5 0.0 copy-done.3
  43.5 0.0 copy-done.4
  43.5 0.0 copy-done.5
  43.5 0.0 copy-done.6
  43.5 0.0 copy-done.7
  43.6 0.0 copy-done.8
  43.6 0.6 %copy-done.9 = f32[136,128]{1,0:T(8,128)} copy-done((f32[136,128]{1,0:T(8,128)}, f32[136,128]{1,0:T(8,128)S(1)}, u32[]{:S(2)}) %copy-start.9) | copy-done | bytes 69656
  44.1 2.6 %last.1 = (f32[1,128]{1,0:T(1,128)}, f32[128,2048]{1,0:T(8,128)}) custom-call(s32[1,2048]{1,0:T(1,128)} %bitcast.10, f32[136,128]{1,0:T(8,128)} %get-tuple-element.28.refs_0_, f32[136,128]{1,0:T(8,128)} %copy-done.3, f32[136,128]{1,0:T(8,128)} %copy-done.4, f32[136,128]{1,0:T(8,128)} %copy-done.5, f32[136,128]{1,0:T(8,128)} %copy-done.6, ...), custom_call_target="tpu_custom_call" | custom-call | flops 1000000000 | bytes 1000000 | tf_op jit(solution)/shard_map/last/pallas_call | solution.py:247
  46.7 0.0 collective-permute-done.7.refs_1_
  46.7 0.0 copy-start
  46.7 0.0 collective-permute-done.8.refs_2_
  46.7 0.0 copy-start.1
  46.7 0.9 %collective-permute-done.9.refs_3_ = f32[256,128]{1,0:T(8,128)S(1)} collective-permute-done((f32[256,128]{1,0:T(8,128)}, f32[256,128]{1,0:T(8,128)S(1)}, u32[]{:S(2)}, u32[]{:S(2)}) %collective-permute-start.9) | collective-permute-done | bytes 131104 | tf_op jit(solution)/shard_map/ppermute | solution.py:240
  47.7 0.0 copy-start.2
  47.7 0.0 copy-done
  47.7 0.0 copy-done.1
  47.7 0.7 %copy-done.2 = f32[256,128]{1,0:T(8,128)} copy-done((f32[256,128]{1,0:T(8,128)}, f32[256,128]{1,0:T(8,128)S(1)}, u32[]{:S(2)}) %copy-start.2) | copy-done | bytes 131096
  48.3 2.5 %feature.1 = f32[256,256]{1,0:T(8,128)} custom-call(f32[512,256]{1,0:T(8,128)} %get-tuple-element.42.adj_ref, f32[256,128]{1,0:T(8,128)} %get-tuple-element.43.refs_0_, f32[256,128]{1,0:T(8,128)} %copy-done, f32[256,128]{1,0:T(8,128)} %copy-done.1, f32[256,128]{1,0:T(8,128)} %copy-done.2), custom_call_target="tpu_custom_call" | custom-call | flops 1000000000 | bytes 1000000 | tf_op jit(solution)/shard_map/feature/pallas_call | solution.py:243
Async XLA Ops:
  25.2 7.4 %collective-permute-start = (f32[136,128]{1,0:T(8,128)}, f32[136,128]{1,0:T(8,128)S(1)}, u32[]{:S(2)}, u32[]{:S(2)}) collective-permute-start(f32[136,128]{1,0:T(8,128)} %get-tuple-element.29), channel_id=1, source_target_pairs={{0,1},{1,0},{2,3},{3,2},{4,5},{5,4},{6,7},{7,6},{8,9},{9,8},{10,11... | collective-permute-start | bytes 208904 | tf_op jit(solution)/shard_map/ppermute | solution.py:235
  26.7 9.5 %collective-permute-start.1 = (f32[136,128]{1,0:T(8,128)}, f32[136,128]{1,0:T(8,128)S(1)}, u32[]{:S(2)}, u32[]{:S(2)}) collective-permute-start(f32[136,128]{1,0:T(8,128)} %get-tuple-element.30), channel_id=1, source_target_pairs={{0,2},{1,3},{2,0},{3,1},{4,6},{5,7},{6,4},{7,5},{8,10},{9,11},{10,... | collective-permute-start | bytes 208904 | tf_op jit(solution)/shard_map/ppermute | solution.py:235
  28.3 8.1 %collective-permute-start.2 = (f32[136,128]{1,0:T(8,128)}, f32[136,128]{1,0:T(8,128)S(1)}, u32[]{:S(2)}, u32[]{:S(2)}) collective-permute-start(f32[136,128]{1,0:T(8,128)} %get-tuple-element.31), channel_id=1, source_target_pairs={{0,3},{1,2},{2,1},{3,0},{4,7},{5,6},{6,5},{7,4},{8,11},{9,10},{10,... | collective-permute-start | bytes 208904 | tf_op jit(solution)/shard_map/ppermute | solution.py:235
  28.7 7.7 %collective-permute-start.3 = (f32[136,128]{1,0:T(8,128)}, f32[136,128]{1,0:T(8,128)S(1)}, u32[]{:S(2)}, u32[]{:S(2)}) collective-permute-start(f32[136,128]{1,0:T(8,128)} %get-tuple-element.32), channel_id=1, source_target_pairs={{0,4},{1,5},{2,6},{3,7},{4,0},{5,1},{6,2},{7,3},{8,12},{9,13},{10,... | collective-permute-start | bytes 208904 | tf_op jit(solution)/shard_map/ppermute | solution.py:235
  31.3 10.9 %collective-permute-start.4 = (f32[136,128]{1,0:T(8,128)}, f32[136,128]{1,0:T(8,128)S(1)}, u32[]{:S(2)}, u32[]{:S(2)}) collective-permute-start(f32[136,128]{1,0:T(8,128)} %get-tuple-element.33), channel_id=1, source_target_pairs={{0,5},{1,4},{2,7},{3,6},{4,1},{5,0},{6,3},{7,2},{8,13},{9,12},{10,... | collective-permute-start | bytes 208904 | tf_op jit(solution)/shard_map/ppermute | solution.py:235
  32.6 10.9 %copy-start.3 = (f32[136,128]{1,0:T(8,128)}, f32[136,128]{1,0:T(8,128)S(1)}, u32[]{:S(2)}) copy-start(f32[136,128]{1,0:T(8,128)S(1)} %collective-permute-done.refs_1_) | copy-start | bytes 208900
  32.6 9.6 %collective-permute-start.5 = (f32[136,128]{1,0:T(8,128)}, f32[136,128]{1,0:T(8,128)S(1)}, u32[]{:S(2)}, u32[]{:S(2)}) collective-permute-start(f32[136,128]{1,0:T(8,128)} %get-tuple-element.34), channel_id=1, source_target_pairs={{0,6},{1,7},{2,4},{3,5},{4,2},{5,3},{6,0},{7,1},{8,14},{9,15},{10,... | collective-permute-start | bytes 208904 | tf_op jit(solution)/shard_map/ppermute | solution.py:235
  36.2 7.3 %copy-start.4 = (f32[136,128]{1,0:T(8,128)}, f32[136,128]{1,0:T(8,128)S(1)}, u32[]{:S(2)}) copy-start(f32[136,128]{1,0:T(8,128)S(1)} %collective-permute-done.1.refs_2_) | copy-start | bytes 208900
  36.2 7.3 %collective-permute-start.6 = (f32[136,128]{1,0:T(8,128)}, f32[136,128]{1,0:T(8,128)S(1)}, u32[]{:S(2)}, u32[]{:S(2)}) collective-permute-start(f32[136,128]{1,0:T(8,128)} %get-tuple-element.35), channel_id=1, source_target_pairs={{0,7},{1,6},{2,5},{3,4},{4,3},{5,2},{6,1},{7,0},{8,15},{9,14},{10,... | collective-permute-start | bytes 208904 | tf_op jit(solution)/shard_map/ppermute | solution.py:235
  36.4 7.1 %copy-start.5 = (f32[136,128]{1,0:T(8,128)}, f32[136,128]{1,0:T(8,128)S(1)}, u32[]{:S(2)}) copy-start(f32[136,128]{1,0:T(8,128)S(1)} %collective-permute-done.2.refs_3_) | copy-start | bytes 208900
  36.4 10.3 %collective-permute-start.7 = (f32[256,128]{1,0:T(8,128)}, f32[256,128]{1,0:T(8,128)S(1)}, u32[]{:S(2)}, u32[]{:S(2)}) collective-permute-start(f32[256,128]{1,0:T(8,128)} %get-tuple-element.44), channel_id=1, source_target_pairs={{0,8},{8,0},{16,24},{24,16},{1,9},{9,1},{17,25},{25,17},{2,10},{10... | collective-permute-start | bytes 393224 | tf_op jit(solution)/shard_map/ppermute | solution.py:240
  36.4 7.1 %copy-start.6 = (f32[136,128]{1,0:T(8,128)}, f32[136,128]{1,0:T(8,128)S(1)}, u32[]{:S(2)}) copy-start(f32[136,128]{1,0:T(8,128)S(1)} %collective-permute-done.3.refs_4_) | copy-start | bytes 208900
  36.4 10.3 %collective-permute-start.8 = (f32[256,128]{1,0:T(8,128)}, f32[256,128]{1,0:T(8,128)S(1)}, u32[]{:S(2)}, u32[]{:S(2)}) collective-permute-start(f32[256,128]{1,0:T(8,128)} %get-tuple-element.45), channel_id=1, source_target_pairs={{0,16},{8,24},{16,0},{24,8},{1,17},{9,25},{17,1},{25,9},{2,18},{10... | collective-permute-start | bytes 393224 | tf_op jit(solution)/shard_map/ppermute | solution.py:240
  42.2 1.3 %copy-start.7 = (f32[136,128]{1,0:T(8,128)}, f32[136,128]{1,0:T(8,128)S(1)}, u32[]{:S(2)}) copy-start(f32[136,128]{1,0:T(8,128)S(1)} %collective-permute-done.4.refs_5_) | copy-start | bytes 208900
  42.2 5.5 %collective-permute-start.9 = (f32[256,128]{1,0:T(8,128)}, f32[256,128]{1,0:T(8,128)S(1)}, u32[]{:S(2)}, u32[]{:S(2)}) collective-permute-start(f32[256,128]{1,0:T(8,128)} %get-tuple-element.46), channel_id=1, source_target_pairs={{0,24},{8,16},{16,8},{24,0},{1,25},{9,17},{17,9},{25,1},{2,26},{10... | collective-permute-start | bytes 393224 | tf_op jit(solution)/shard_map/ppermute | solution.py:240
  42.2 1.3 %copy-start.8 = (f32[136,128]{1,0:T(8,128)}, f32[136,128]{1,0:T(8,128)S(1)}, u32[]{:S(2)}) copy-start(f32[136,128]{1,0:T(8,128)S(1)} %collective-permute-done.5.refs_6_) | copy-start | bytes 208900
  43.5 0.6 %copy-start.9 = (f32[136,128]{1,0:T(8,128)}, f32[136,128]{1,0:T(8,128)S(1)}, u32[]{:S(2)}) copy-start(f32[136,128]{1,0:T(8,128)S(1)} %collective-permute-done.6.refs_7_) | copy-start | bytes 208900
  46.7 1.0 %copy-start = (f32[256,128]{1,0:T(8,128)}, f32[256,128]{1,0:T(8,128)S(1)}, u32[]{:S(2)}) copy-start(f32[256,128]{1,0:T(8,128)S(1)} %collective-permute-done.7.refs_1_) | copy-start | bytes 393220
  46.7 1.0 %copy-start.1 = (f32[256,128]{1,0:T(8,128)}, f32[256,128]{1,0:T(8,128)S(1)}, u32[]{:S(2)}) copy-start(f32[256,128]{1,0:T(8,128)S(1)} %collective-permute-done.8.refs_2_) | copy-start | bytes 393220
  47.7 0.7 %copy-start.2 = (f32[256,128]{1,0:T(8,128)}, f32[256,128]{1,0:T(8,128)S(1)}, u32[]{:S(2)}) copy-start(f32[256,128]{1,0:T(8,128)S(1)} %collective-permute-done.9.refs_3_) | copy-start | bytes 393220

commit v2 on v0

v2 whole, which is shorter than its diff:
```python
import functools

import jax
import jax.numpy as jnp
from jax import lax
from jax.experimental import pallas as pl
from jax.experimental.pallas import tpu as pltpu
from jax.sharding import PartitionSpec as P

MAXDEG = 12
SET_SIZE = 16
INFO = 8
BLOCK = 128

f32 = jnp.float32
bf16 = jnp.bfloat16
VMEM = pl.BlockSpec(memory_space=pltpu.VMEM)
ANY = pl.BlockSpec(memory_space=pl.ANY)


def split(value):
    high = value.astype(bf16)
    low = (value - high.astype(f32)).astype(bf16)
    return high, low


def nn(left, right):
    return lax.dot_general(left, right, (((1,), (0,)), ((), ())), preferred_element_type=f32)


def nt(left, right):
    return lax.dot_general(left, right, (((1,), (1,)), ((), ())), preferred_element_type=f32)


def pair_nn(left, right):
    cols = right[0].shape[1]
    both = nn(left[0], jnp.concatenate(right, axis=1))
    return both[:, :cols] + both[:, cols:] + nn(left[1], right[0])


def iota(shape, dim):
    return lax.broadcasted_iota(jnp.int32, shape, dim)


def column(row):
    n = row.shape[1]
    return jnp.transpose(jnp.broadcast_to(row.astype(f32), (n, n)))


def one_hot(test):
    return jnp.where(test, f32(1), f32(0)).astype(bf16)


def pick(table, ids):
    rows, lanes = table.shape
    total = jnp.zeros((1, ids.shape[1]), f32)
    for r in range(rows):
        here = column(table[r : r + 1, :])
        where = iota((lanes, ids.shape[1]), 0) + r * lanes == ids
        total = total + jnp.sum(jnp.where(where, here[:, : ids.shape[1]], 0.0), axis=0, keepdims=True)
    return total


def basis(points):
    before, current = jnp.ones_like(points), points
    rows = [current]
    for _ in range(2, MAXDEG + 1):
        before, current = current, 2.0 * points * current - before
        rows.append(current)
    return jnp.concatenate(rows, axis=0)


def first_kernel(n_trade, *refs):
    ins, rest = refs[:8], refs[8:]
    folded_refs, rest = rest[:n_trade], rest[n_trade:]
    expo_ref, fact_out, key_out, side_out, member_out = rest[:5]
    fact_ref, factor_ref, degree_ref, set_ref, party_ref, thr_ref, wgt_ref, coef_buf, grid_ref, small, sems = rest[5:]
    fact_hbm, factor_hbm, degree_hbm, coef_hbm, set_hbm, party_hbm, thr_hbm, wgt_hbm = ins
    me = lax.axis_index("trade")
    width, cols = coef_hbm.shape
    sets = cols // SET_SIZE
    nfac, scen = fact_ref.shape
    own = width // n_trade
    steps = width // BLOCK
    per = own // BLOCK

    loads = [
        pltpu.make_async_copy(source, target, small.at[i])
        for i, (source, target) in enumerate(
            [
                (fact_hbm, fact_ref),
                (set_hbm, set_ref),
                (factor_hbm, factor_ref),
                (degree_hbm, degree_ref),
                (party_hbm, party_ref),
                (thr_hbm, thr_ref),
                (wgt_hbm, wgt_ref),
            ]
        )
    ]

    def start_row(step):
        return pl.multiple_of((me ^ (step // per)) * own + (step % per) * BLOCK, BLOCK)

    def copy(step):
        return pltpu.make_async_copy(
            coef_hbm.at[pl.ds(start_row(step), BLOCK), :], coef_buf.at[step], sems.at[step]
        )

    for load in loads:
        load.start()
    for step in range(steps):
        copy(step).start()
    for load in loads:
        load.wait()
    member = jnp.where(set_ref[...] - me * sets == iota((sets, cols), 0), f32(1), f32(0))
    member_out[...] = member.astype(bf16)
    turned_member = jnp.transpose(member).astype(bf16)
    fact_out[...] = fact_ref[...]
    table = split(jnp.transpose(basis(fact_ref[...])))
    key_out[...] = factor_ref[...] + nfac * (degree_ref[...] - 1)
    party = party_ref[...]
    thr_row = pick(thr_ref[...], party)
    wgt_row = pick(wgt_ref[...], party)
    line = iota((INFO, sets), 0)
    expo_ref[scen:, :] = jnp.where(line == 0, party.astype(f32), jnp.where(line == 1, thr_row, wgt_row))
    side_out[...] = jnp.where(line == 0, thr_ref[pl.ds(me, 1), :], wgt_ref[pl.ds(me, 1), :])
    for pair in range(steps // 2):
        highs, lows, keys = [], [], []
        for step in (2 * pair, 2 * pair + 1):
            copy(step).wait()
            coef_high, coef_low = split(coef_buf[step])
            folded = nn(coef_high, turned_member) + nn(coef_low, turned_member)
            folded_refs[step // per][pl.ds((step % per) * BLOCK, BLOCK), :] = folded
            high, low = split(folded)
            highs.append(high)
            lows.append(low)
            keys.append(key_out[pl.ds(lax.div(start_row(step), BLOCK), 1), :])
        right = jnp.concatenate([jnp.concatenate(highs, axis=0), jnp.concatenate(lows, axis=0)], axis=1)
        chosen = one_hot(iota((MAXDEG * nfac, 2 * BLOCK), 0) == jnp.concatenate(keys, axis=1))
        part = nn(chosen, right)
        grid_ref[...] = part if pair == 0 else grid_ref[...] + part
    expo_ref[:scen, :] = pair_nn(table, split(grid_ref[:, :sets] + grid_ref[:, sets:]))


def blocks_of(all_ref, n_trade):
    stride = all_ref.shape[0] // n_trade
    scen = stride - INFO
    expo = [split(all_ref[a * stride : a * stride + scen, :]) for a in range(n_trade)]
    pieces = tuple(jnp.concatenate([e[i] for e in expo], axis=1) for i in range(2))
    columns = [column(all_ref[a * stride + scen : a * stride + scen + 1, :]) for a in range(n_trade)]
    return pieces, columns


def same_as(columns, row):
    return one_hot(jnp.concatenate([here == row for here in columns], axis=0))


def info_of(all_ref, n_trade, block):
    stride = all_ref.shape[0] // n_trade
    info = all_ref[pl.ds(pl.multiple_of(block * stride + stride - INFO, INFO), INFO), :]
    return info[0:1, :], info[1:2, :], info[2:3, :]


def second_kernel(n_trade, all_ref, side_ref, fact_ref, msg_ref):
    trade = lax.axis_index("trade")
    sets = all_ref.shape[1]
    scen = all_ref.shape[0] // n_trade - INFO
    (high, low), columns = blocks_of(all_ref, n_trade)
    party, thr, wgt = info_of(all_ref, n_trade, trade)
    mine = (iota((1, sets), 1) + trade * sets).astype(f32)
    right = jnp.concatenate([same_as(columns, party), same_as(columns, mine)], axis=1)
    netted = nn(high, right) + nn(low, right)
    msg_ref[:scen, :] = wgt * jax.nn.sigmoid(netted[:, :sets] - thr)
    soft = jax.nn.softplus(netted[:, sets:] - side_ref[0:1, :])
    msg_ref[scen : scen + INFO, :] = jnp.broadcast_to(
        jnp.sum(soft, axis=0, keepdims=True) * side_ref[1:2, :], (INFO, sets)
    )
    nfac, base = fact_ref.shape[0], scen + INFO
    for piece in range(scen // sets):
        msg_ref[base + piece * nfac : base + (piece + 1) * nfac, :] = fact_ref[:, piece * sets : (piece + 1) * sets]


def response(msg_ref, nfac, scen):
    base = scen + INFO
    pieces = (msg_ref.shape[0] - base) // nfac
    points = jnp.concatenate(
        [msg_ref[base + i * nfac : base + (i + 1) * nfac, :] for i in range(pieces)], axis=1
    )
    return pair_nn(split(basis(points)), split(msg_ref[:scen, :]))


def middle_kernel(n_scen, nfac, scen, msg_ref, key_ref, grid_ref, chosen_ref, column_ref):
    me = lax.axis_index("scen")
    lines = key_ref.shape[0]
    chunk = lines * BLOCK // n_scen
    for i in range(lines):
        column_ref[i * BLOCK : (i + 1) * BLOCK, :] = column(key_ref[i : i + 1, :])
    rows = grid_ref.shape[0]
    for j in range(n_scen // 2):
        here = column_ref[pl.ds(pl.multiple_of((me ^ (2 * j)) * chunk, chunk), chunk), :].astype(jnp.int32)
        for i in range(rows // BLOCK):
            chosen_ref[j * chunk : (j + 1) * chunk, i * BLOCK : (i + 1) * BLOCK] = one_hot(
                here == iota(here.shape, 1) + i * BLOCK
            )
    grid_ref[...] = response(msg_ref, nfac, scen)


def third_kernel(n_scen, nfac, scen, msg_ref, own_ref, grid_ref, chosen_ref, *chunk_refs):
    chunk = chosen_ref.shape[0] // len(chunk_refs)
    both = jnp.concatenate(split(grid_ref[...] + response(msg_ref, nfac, scen)), axis=1)
    xva = msg_ref[scen : scen + INFO, :] + own_ref[scen : scen + INFO, :]
    sets = msg_ref.shape[1]
    for j, ref in enumerate(chunk_refs):
        part = nn(chosen_ref[j * chunk : (j + 1) * chunk, :], both)
        ref[:chunk, :] = part[:, :sets] + part[:, sets:]
        ref[chunk:, :] = xva


def feature_kernel(n_trade, all_ref, *refs):
    folded_refs, out_ref = refs[:n_trade], refs[n_trade]
    trade = lax.axis_index("trade")
    (high, low), columns = blocks_of(all_ref, n_trade)
    total = jnp.zeros(out_ref.shape, f32)
    for k in range(n_trade):
        party, thr, wgt = info_of(all_ref, n_trade, trade ^ k)
        same = same_as(columns, party)
        netted = nn(high, same) + nn(low, same)
        adj_high, adj_low = split(wgt * jax.nn.sigmoid(netted - thr))
        fold_high, fold_low = split(folded_refs[k][...])
        total = total + nt(fold_high, adj_high) + nt(fold_low, adj_high) + nt(fold_high, adj_low)
    out_ref[...] = total


def last_kernel(n_chunks, scale, member_ref, *refs):
    chunk_refs, (xva_hbm, out_hbm, xva_ref, out_ref, sems) = refs[:n_chunks], refs[n_chunks:]
    rows, cols = out_hbm.shape
    total = chunk_refs[0][...]
    for ref in chunk_refs[1:]:
        total = total + ref[...]
    total = total * scale
    xva_ref[...] = total[rows : rows + 1, :]
    first = pltpu.make_async_copy(xva_ref, xva_hbm, sems.at[0])
    first.start()
    high, low = split(total[:rows, :])
    copies = [first]
    pieces = sems.shape[0] - 1
    wide = cols // pieces
    for i in range(pieces):
        part = member_ref[:, i * wide : (i + 1) * wide]
        out_ref[:, i * wide : (i + 1) * wide] = nn(high, part) + nn(low, part)
        copies.append(
            pltpu.make_async_copy(
                out_ref.at[:, pl.ds(i * wide, wide)], out_hbm.at[:, pl.ds(i * wide, wide)], sems.at[i + 1]
            )
        )
        copies[-1].start()
    for copy in copies:
        copy.wait()


def call(kernel, out_shape, in_specs, args, name, scratch=(), flops=5 * 10**8, limit=None):
    args = [
        pltpu.with_memory_space_constraint(arg, pltpu.VMEM) if spec is VMEM else arg
        for arg, spec in zip(args, in_specs)
    ]
    specs = [ANY if isinstance(shape, jax.ShapeDtypeStruct) else VMEM for shape in out_shape]
    return pl.pallas_call(
        kernel,
        out_shape=out_shape,
        in_specs=in_specs,
        out_specs=specs,
        scratch_shapes=scratch,
        cost_estimate=pl.CostEstimate(flops=flops, bytes_accessed=10**5, transcendentals=0),
        compiler_params=pltpu.CompilerParams(vmem_limit_bytes=limit),
        name=name,
    )(*args)


def local(
    factors, feat_factor, feat_degree, coefficients, set_of_trade, party_of_set, threshold, weight
):
    n_trade, n_scen = lax.axis_size("trade"), lax.axis_size("scen")
    scen, nfac = factors.shape
    width, cols = coefficients.shape
    sets = cols // SET_SIZE
    lines = width // BLOCK
    own, chunk, grid = width // n_trade, width // n_scen, MAXDEG * nfac
    struct, vmem, dma = jax.ShapeDtypeStruct, pltpu.VMEM, pltpu.SemaphoreType.DMA
    i32 = jnp.int32
    outs = call(
        functools.partial(first_kernel, n_trade),
        [vmem((own, sets), f32)] * n_trade
        + [vmem((scen + INFO, sets), f32), vmem((nfac, scen), f32), vmem((lines, BLOCK), i32)]
        + [vmem((INFO, sets), f32), vmem((sets, cols), bf16)],
        [ANY] * 8,
        [
            factors.T,
            feat_factor.reshape(lines, BLOCK),
            feat_degree.reshape(lines, BLOCK),
            coefficients,
            set_of_trade.reshape(1, cols),
            party_of_set.reshape(1, sets),
            threshold.reshape(n_trade, sets),
            weight.reshape(n_trade, sets),
        ],
        "first",
        [
            vmem((nfac, scen), f32),
            vmem((lines, BLOCK), i32),
            vmem((lines, BLOCK), i32),
            vmem((1, cols), i32),
            vmem((1, sets), i32),
            vmem((n_trade, sets), f32),
            vmem((n_trade, sets), f32),
            vmem((lines, BLOCK, cols), f32),
            vmem((grid, 2 * sets), f32),
            dma((7,)),
            dma((lines,)),
        ],
        limit=32 << 20,
    )
    folded, (expo, fact, key, side, member) = outs[:n_trade], outs[n_trade:]
    everything = lax.all_gather(expo, "trade", axis=0, tiled=True)
    (msg,) = call(
        functools.partial(second_kernel, n_trade),
        [vmem((scen + INFO + nfac * scen // sets, sets), f32)],
        [VMEM] * 3,
        [everything, side, fact],
        "second",
        limit=8 << 20,
    )
    peer = lax.ppermute(msg, "scen", [(i, i ^ 1) for i in range(n_scen)])
    half, chosen = call(
        functools.partial(middle_kernel, n_scen, nfac, scen),
        [vmem((grid, sets), f32), vmem((width // 2, grid), bf16)],
        [VMEM] * 2,
        [msg, key],
        "middle",
        [vmem((width, BLOCK), f32)],
        limit=8 << 20,
    )
    msg, *later = lax.optimization_barrier((msg, *folded[1:]))
    moved = [folded[0]] + [
        lax.ppermute(later[k - 1], "trade", [(i, i ^ k) for i in range(n_trade)])
        for k in range(1, n_trade)
    ]
    chunks = call(
        functools.partial(third_kernel, n_scen, nfac, scen),
        [vmem((chunk + INFO, sets), f32)] * (n_scen // 2),
        [VMEM] * 4,
        [peer, msg, half, chosen],
        "third",
        limit=8 << 20,
    )
    chunks = [chunks[0]] + [
        lax.ppermute(chunks[j], "scen", [(i, i ^ (2 * j)) for i in range(n_scen)])
        for j in range(n_scen // 2 - 1, 0, -1)
    ]
    (feature_sens,) = call(
        functools.partial(feature_kernel, n_trade),
        [vmem((own, scen), f32)],
        [VMEM] * (n_trade + 1),
        [everything, *moved],
        "feature",
        flops=2 * 10**9,
        limit=8 << 20,
    )
    xva, coef_sens = call(
        functools.partial(last_kernel, n_scen // 2, 1.0 / (scen * n_scen)),
        [struct((1, sets), f32), struct((chunk, cols), f32)],
        [VMEM] * (n_scen // 2 + 1),
        [member, *chunks],
        "last",
        [vmem((1, sets), f32), vmem((chunk, cols), f32), dma((5,))],
        limit=8 << 20,
    )
    return (xva.reshape(sets), coef_sens, feature_sens)


def solution(mesh):
    in_specs = (P("scen", None), P(), P(), P(None, "trade"), P("trade"), P("trade"), P(), P())
    out_specs = (P("trade"), P("scen", "trade"), P("trade", "scen"))
    return jax.shard_map(local, mesh=mesh, in_specs=in_specs, out_specs=out_specs, check_vma=False)
```

time: 157 us -> 43.8 us (0.28)
  waiting for transfers between devices: 87.4 us -> 5.55 us
  matrix products: 22 us -> 0 us
  blocking collectives: 28 us -> 8.78 us
  between operations: 13.8 us -> 0.69 us
  Pallas kernels: 0 us -> 11.6 us
  local copies, waits for them, and re-layouts: 0.78 us -> 9 us
  starting transfers between devices: 0.12 us -> 7.85 us
  other arithmetic: 4.63 us -> 0 us
    reduce_scatter x3 -> x0, waiting for transfers between devices: 87.3 us -> none  [the longest x1 39.3 us: local(): lax.psum_scatter(contract(block, set_adj, 0, 0) / scen_total, 'scen', sca...]
    dot_general x8 -> x0, matrix products: 22 us -> none  [the longest x1 8.05 us: local(): folded = jnp.dot(coefficients, member, precision=highest)]
    psum x1 -> x0, blocking collectives: 21.5 us -> none  [local(): xva = lax.psum(local_total, 'scen') / scen_total]
    pallas_call x0 -> x6, Pallas kernels: none -> 11.6 us  [call(): pl.pallas_call(kernel, out_shape=out_shape, in_specs=in_specs, out_specs=...]
    unnamed x6 -> x17, local copies, waits for them, and re-layouts: 0.02 us -> 9 us
    ppermute x0 -> x7, starting transfers between devices: none -> 7.85 us  [the longest x3 4.45 us: local(): lax.ppermute(chunks[j], 'scen', [(i, i ^ 2 * j) for i in range(n_scen)])]
    ppermute x0 -> x7, waiting for transfers between devices: none -> 5.55 us  [the longest x1 3.26 us: local(): peer = lax.ppermute(msg, 'scen', [(i, i ^ 1) for i in range(n_scen)])]
    all_gather x1, blocking collectives: 6.59 us -> 8.78 us  [local(): everything = lax.all_gather(expo, 'trade', axis=0, tiled=True)]
  transfers between devices with their start and end apart: 3 -> 7, of which waited for: 3 -> 3; matrix products, arithmetic and copies ran while one was open for 4% -> 2% of each run, Pallas kernels for 0% -> 7%
where the time goes in v2:
time: 43.8 us; the launch traced here: 43.4 us
  Pallas kernels  11.6 us (26%)
  local copies, waits for them, and re-layouts  9 us (21%)
  blocking collectives  8.78 us (20%)
  starting transfers between devices  7.85 us (18%)
  waiting for transfers between devices  5.55 us (13%)
  between operations  0.69 us (2%)
    pallas_call x6, Pallas kernels, call(): pl.pallas_call(kernel, out_shape=out_shape, in_specs=in_specs, out_specs=...  11.6 us
    unnamed x17, local copies, waits for them, and re-layouts  9 us
    all_gather x1, blocking collectives, local(): everything = lax.all_gather(expo, 'trade', axis=0, tiled=True)  8.78 us
    ppermute x3, starting transfers between devices, local(): lax.ppermute(chunks[j], 'scen', [(i, i ^ 2 * j) for i in range(n_scen)])  4.45 us
    ppermute x1, waiting for transfers between devices, local(): peer = lax.ppermute(msg, 'scen', [(i, i ^ 1) for i in range(n_scen)])  3.26 us
    ppermute x3, waiting for transfers between devices, local(): lax.ppermute(chunks[j], 'scen', [(i, i ^ 2 * j) for i in range(n_scen)])  2.28 us
    ppermute x3, starting transfers between devices, local(): lax.ppermute(later[k - 1], 'trade', [(i, i ^ k) for i in range(n_trade)])  1.86 us
    ppermute x1, starting transfers between devices, local(): peer = lax.ppermute(msg, 'scen', [(i, i ^ 1) for i in range(n_scen)])  1.54 us
  transfers between devices with their start and end apart: 7, of which 3 were waited for; matrix products, arithmetic and copies ran while one was open for 2% of the time, Pallas kernels for 7%

profile of v2, /device:TPU:0, one launch (start us, length us, event | category | flops | bytes accessed | tf_op | source)
XLA Modules:
  0.0 43.4 jit_solution(5856872890625129418)
XLA Ops:
  0.6 0.0 copy-start
  0.6 3.4 %copy-done = f32[1024,2048]{1,0:T(8,128)S(1)} copy-done((f32[1024,2048]{1,0:T(8,128)S(1)}, f32[1024,2048]{1,0:T(8,128)}, u32[]{:S(2)}) %copy-start) | copy-done | bytes 8388632
  4.0 0.0 copy-start.1
  4.0 0.8 %copy-done.1 = f32[256,64]{0,1:T(8,128)S(1)} copy-done((f32[256,64]{0,1:T(8,128)S(1)}, f32[256,64]{0,1:T(8,128)}, u32[]{:S(2)}) %copy-start.1) | copy-done | bytes 65560
  4.9 0.0 copy-start.2
  4.9 0.7 %copy-done.2 = s32[2048]{0:T(1024)S(1)} copy-done((s32[2048]{0:T(1024)S(1)}, s32[2048]{0:T(1024)}, u32[]{:S(2)}) %copy-start.2) | copy-done | bytes 8216
  5.6 0.0 copy-start.3
  5.6 0.7 %copy-done.3 = s32[1024]{0:T(1024)S(1)} copy-done((s32[1024]{0:T(1024)S(1)}, s32[1024]{0:T(1024)}, u32[]{:S(2)}) %copy-start.3) | copy-done | bytes 4120
  6.2 0.0 copy-start.4
  6.2 0.7 %copy-done.4 = s32[1024]{0:T(1024)S(1)} copy-done((s32[1024]{0:T(1024)S(1)}, s32[1024]{0:T(1024)}, u32[]{:S(2)}) %copy-start.4) | copy-done | bytes 4120
  6.9 0.0 copy-start.5
  6.9 0.7 %copy-done.5 = f32[512]{0:T(512)S(1)} copy-done((f32[512]{0:T(512)S(1)}, f32[512]{0:T(512)}, u32[]{:S(2)}) %copy-start.5) | copy-done | bytes 2072
  7.6 0.0 copy-start.6
  7.6 0.7 %copy-done.6 = f32[512]{0:T(512)S(1)} copy-done((f32[512]{0:T(512)S(1)}, f32[512]{0:T(512)}, u32[]{:S(2)}) %copy-start.6) | copy-done | bytes 2072
  8.3 0.0 copy-start.7
  8.3 0.7 %copy-done.7 = s32[128]{0:T(128)S(1)} copy-done((s32[128]{0:T(128)S(1)}, s32[128]{0:T(128)}, u32[]{:S(2)}) %copy-start.7) | copy-done | bytes 536
  8.9 6.7 %first.1 = (f32[256,128]{1,0:T(8,128)S(1)}, f32[256,128]{1,0:T(8,128)S(1)}, f32[256,128]{1,0:T(8,128)S(1)}, f32[256,128]{1,0:T(8,128)S(1)}, f32[264,128]{1,0:T(8...) custom-call(f32[64,256]{1,0:T(8,128)S(1)} %bitcast.8, ...), custom_call_target="tpu_custom_call" | custom-call | flops 500000000 | bytes 100000 | tf_op jit(solution)/shard_map/first/pallas_call | solution.py:268
  15.6 8.8 %all_gather.3.all_ref = f32[1056,128]{1,0:T(8,128)S(1)} all-gather(f32[264,128]{1,0:T(8,128)S(1)} %get-tuple-element.25), channel_id=1, replica_groups=mesh['trade'=4,'scen'=8] {'trade'}, dimensions={0}, use_global_device_ids=true | all-gather | bytes 675840 | tf_op jit(solution)/shard_map/all_gather | solution.py:324
  24.4 0.5 %second.1.msg_ref.own_ref = f32[392,128]{1,0:T(8,128)S(1)} custom-call(f32[1056,128]{1,0:T(8,128)S(1)} %all_gather.3.all_ref, f32[8,128]{1,0:T(8,128)S(1)} %get-tuple-element.26.side_ref, f32[64,256]{1,0:T(8,128)S(1)} %get-tuple-element.27.fact_ref), custom_call_target="tpu_custom_call" | custom-call | flops 500000000 | bytes 100000 | tf_op jit(solution)/shard_map/second/pallas_call | solution.py:268
  24.9 1.5 %collective-permute-start = (f32[392,128]{1,0:T(8,128)S(1)}, f32[392,128]{1,0:T(8,128)S(1)}, u32[]{:S(2)}, u32[]{:S(2)}) collective-permute-start(f32[392,128]{1,0:T(8,128)S(1)} %second.1.msg_ref.own_ref), channel_id=1, source_target_pairs={{0,1},{1,0},{2,3},{3,2},{4,5},{5,4},{6,7},{7,6},{8,9},{9,8},{10,11... | collective-permute-start | bytes 602120 | tf_op jit(solution)/shard_map/ppermute | solution.py:333
  26.4 0.1 collective-permute-start.4
  26.5 1.1 %collective-permute-start.5 = (f32[256,128]{1,0:T(8,128)S(1)}, f32[256,128]{1,0:T(8,128)S(1)}, u32[]{:S(2)}, u32[]{:S(2)}) collective-permute-start(f32[256,128]{1,0:T(8,128)S(1)} %get-tuple-element.43), channel_id=1, source_target_pairs={{0,16},{8,24},{16,0},{24,8},{1,17},{9,25},{17,1},{25,9},{2,18},{10... | collective-permute-start | bytes 393224 | tf_op jit(solution)/shard_map/ppermute | solution.py:345
  27.6 0.7 %collective-permute-start.6 = (f32[256,128]{1,0:T(8,128)S(1)}, f32[256,128]{1,0:T(8,128)S(1)}, u32[]{:S(2)}, u32[]{:S(2)}) collective-permute-start(f32[256,128]{1,0:T(8,128)S(1)} %get-tuple-element.44), channel_id=1, source_target_pairs={{0,24},{8,16},{16,8},{24,0},{1,25},{9,17},{17,9},{25,1},{2,26},{10... | collective-permute-start | bytes 393224 | tf_op jit(solution)/shard_map/ppermute | solution.py:345
  28.3 0.6 %middle.1 = (f32[768,128]{1,0:T(8,128)S(1)}, bf16[512,768]{1,0:T(8,128)(2,1)S(1)}) custom-call(f32[392,128]{1,0:T(8,128)S(1)} %second.1.msg_ref.own_ref, s32[8,128]{1,0:T(8,128)S(1)} %get-tuple-element.32.key_ref), custom_call_target="tpu_custom_call" | custom-call | flops 500000000 | bytes 100000 | tf_op jit(solution)/shard_map/middle/pallas_call | solution.py:268
  28.9 3.3 %collective-permute-done.msg_ref = f32[392,128]{1,0:T(8,128)S(1)} collective-permute-done((f32[392,128]{1,0:T(8,128)S(1)}, f32[392,128]{1,0:T(8,128)S(1)}, u32[]{:S(2)}, u32[]{:S(2)}) %collective-permute-start) | collective-permute-done | bytes 200736 | tf_op jit(solution)/shard_map/ppermute | solution.py:333
  32.2 0.7 %third.1 = (f32[136,128]{1,0:T(8,128)S(1)}, f32[136,128]{1,0:T(8,128)S(1)}, f32[136,128]{1,0:T(8,128)S(1)}, f32[136,128]{1,0:T(8,128)S(1)}) custom-call(f32[392,128]{1,0:T(8,128)S(1)} %collective-permute-done.msg_ref, f32[392,128]{1,0:T(8,128)S(1)} %second.1.msg_ref.own_ref, f32[768,128]{1,0:T(8,128)S(1)} %get-tuple-element.33.grid_ref, ...), custom_call_target="tpu_custom_call" | custom-call | flops 500000000 | bytes 100000 | tf_op jit(solution)/shard_map/third/pallas_call | solution.py:268
  32.9 3.7 %collective-permute-start.1 = (f32[136,128]{1,0:T(8,128)S(1)}, f32[136,128]{1,0:T(8,128)S(1)}, u32[]{:S(2)}, u32[]{:S(2)}) collective-permute-start(f32[136,128]{1,0:T(8,128)S(1)} %get-tuple-element.36), channel_id=1, source_target_pairs={{0,6},{1,7},{2,4},{3,5},{4,2},{5,3},{6,0},{7,1},{8,14},{9,15},{10,... | collective-permute-start | bytes 208904 | tf_op jit(solution)/shard_map/ppermute | solution.py:357
  36.5 0.0 collective-permute-start.2
  36.5 0.0 collective-permute-done.4.refs_1_
  36.5 0.8 %collective-permute-start.3 = (f32[136,128]{1,0:T(8,128)S(1)}, f32[136,128]{1,0:T(8,128)S(1)}, u32[]{:S(2)}, u32[]{:S(2)}) collective-permute-start(f32[136,128]{1,0:T(8,128)S(1)} %get-tuple-element.38), channel_id=1, source_target_pairs={{0,2},{1,3},{2,0},{3,1},{4,6},{5,7},{6,4},{7,5},{8,10},{9,11},{10,... | collective-permute-start | bytes 208904 | tf_op jit(solution)/shard_map/ppermute | solution.py:357
  37.3 0.0 collective-permute-done.5.refs_2_
  37.3 0.0 collective-permute-done.6.refs_3_
  37.3 1.9 %feature.1 = f32[256,256]{1,0:T(8,128)S(1)} custom-call(f32[1056,128]{1,0:T(8,128)S(1)} %all_gather.3.all_ref, f32[256,128]{1,0:T(8,128)S(1)} %get-tuple-element.41.refs_0_, f32[256,128]{1,0:T(8,128)S(1)} %collective-permute-done.4.refs_1_, f32[256,128]{1,0:T(8,128)S(1)} %collective-permute-done.5.refs_2_, f32[256,128]{1,0:T(8,128)S(1)} %collective-permute-done.6.refs_3_), custom_call_target="tpu_custom_call" | custom-call | flops 2000000000 | bytes 100000 | tf_op jit(solution)/shard_map/feature/pallas_call | solution.py:268
  39.2 0.7 %copy.11 = f32[256,256]{1,0:T(8,128)} copy(f32[256,256]{1,0:T(8,128)S(1)} %feature.1) | data formatting | bytes 524288
  39.9 0.0 collective-permute-done.1.refs_1_
  39.9 2.2 %collective-permute-done.2.refs_2_ = f32[136,128]{1,0:T(8,128)S(1)} collective-permute-done((f32[136,128]{1,0:T(8,128)S(1)}, f32[136,128]{1,0:T(8,128)S(1)}, u32[]{:S(2)}, u32[]{:S(2)}) %collective-permute-start.2) | collective-permute-done | bytes 69664 | tf_op jit(solution)/shard_map/ppermute | solution.py:357
  42.1 0.1 collective-permute-done.3.refs_3_
  42.2 1.2 %last.1 = (f32[1,128]{1,0:T(1,128)}, f32[128,2048]{1,0:T(8,128)}) custom-call(bf16[128,2048]{1,0:T(8,128)(2,1)S(1)} %get-tuple-element.24.member_ref, f32[136,128]{1,0:T(8,128)S(1)} %get-tuple-element.35.refs_0_, f32[136,128]{1,0:T(8,128)S(1)} %collective-permute-done.1.refs_1_, f32[136,128]{1,0:T(8,128)S(1)} %collective-permute-done.2.refs_2_, ...), custom_call_target="tpu_custom_call" | custom-call | flops 500000000 | bytes 100000 | tf_op jit(solution)/shard_map/last/pallas_call | solution.py:268
Async XLA Ops:
  0.6 3.4 %copy-start = (f32[1024,2048]{1,0:T(8,128)S(1)}, f32[1024,2048]{1,0:T(8,128)}, u32[]{:S(2)}) copy-start(f32[1024,2048]{1,0:T(8,128)} %refs_3_.1) | copy-start | bytes 25165828
  4.0 0.8 %copy-start.1 = (f32[256,64]{0,1:T(8,128)S(1)}, f32[256,64]{0,1:T(8,128)}, u32[]{:S(2)}) copy-start(f32[256,64]{0,1:T(8,128)} %param.8) | copy-start | bytes 196612
  4.9 0.7 %copy-start.2 = (s32[2048]{0:T(1024)S(1)}, s32[2048]{0:T(1024)}, u32[]{:S(2)}) copy-start(s32[2048]{0:T(1024)} %param.12) | copy-start | bytes 24580
  5.6 0.7 %copy-start.3 = (s32[1024]{0:T(1024)S(1)}, s32[1024]{0:T(1024)}, u32[]{:S(2)}) copy-start(s32[1024]{0:T(1024)} %param.9) | copy-start | bytes 12292
  6.2 0.7 %copy-start.4 = (s32[1024]{0:T(1024)S(1)}, s32[1024]{0:T(1024)}, u32[]{:S(2)}) copy-start(s32[1024]{0:T(1024)} %param.10) | copy-start | bytes 12292
  6.9 0.7 %copy-start.5 = (f32[512]{0:T(512)S(1)}, f32[512]{0:T(512)}, u32[]{:S(2)}) copy-start(f32[512]{0:T(512)} %param.14) | copy-start | bytes 6148
  7.6 0.7 %copy-start.6 = (f32[512]{0:T(512)S(1)}, f32[512]{0:T(512)}, u32[]{:S(2)}) copy-start(f32[512]{0:T(512)} %param.15) | copy-start | bytes 6148
  8.3 0.7 %copy-start.7 = (s32[128]{0:T(128)S(1)}, s32[128]{0:T(128)}, u32[]{:S(2)}) copy-start(s32[128]{0:T(128)} %param.13) | copy-start | bytes 1540
  24.9 7.3 %collective-permute-start = (f32[392,128]{1,0:T(8,128)S(1)}, f32[392,128]{1,0:T(8,128)S(1)}, u32[]{:S(2)}, u32[]{:S(2)}) collective-permute-start(f32[392,128]{1,0:T(8,128)S(1)} %second.1.msg_ref.own_ref), channel_id=1, source_target_pairs={{0,1},{1,0},{2,3},{3,2},{4,5},{5,4},{6,7},{7,6},{8,9},{9,8},{10,11... | collective-permute-start | bytes 602120 | tf_op jit(solution)/shard_map/ppermute | solution.py:333
  26.4 10.1 %collective-permute-start.4 = (f32[256,128]{1,0:T(8,128)S(1)}, f32[256,128]{1,0:T(8,128)S(1)}, u32[]{:S(2)}, u32[]{:S(2)}) collective-permute-start(f32[256,128]{1,0:T(8,128)S(1)} %get-tuple-element.42), channel_id=1, source_target_pairs={{0,8},{8,0},{16,24},{24,16},{1,9},{9,1},{17,25},{25,17},{2,10},{10... | collective-permute-start | bytes 393224 | tf_op jit(solution)/shard_map/ppermute | solution.py:345
  26.5 10.9 %collective-permute-start.5 = (f32[256,128]{1,0:T(8,128)S(1)}, f32[256,128]{1,0:T(8,128)S(1)}, u32[]{:S(2)}, u32[]{:S(2)}) collective-permute-start(f32[256,128]{1,0:T(8,128)S(1)} %get-tuple-element.43), channel_id=1, source_target_pairs={{0,16},{8,24},{16,0},{24,8},{1,17},{9,25},{17,1},{25,9},{2,18},{10... | collective-permute-start | bytes 393224 | tf_op jit(solution)/shard_map/ppermute | solution.py:345
  27.6 9.8 %collective-permute-start.6 = (f32[256,128]{1,0:T(8,128)S(1)}, f32[256,128]{1,0:T(8,128)S(1)}, u32[]{:S(2)}, u32[]{:S(2)}) collective-permute-start(f32[256,128]{1,0:T(8,128)S(1)} %get-tuple-element.44), channel_id=1, source_target_pairs={{0,24},{8,16},{16,8},{24,0},{1,25},{9,17},{17,9},{25,1},{2,26},{10... | collective-permute-start | bytes 393224 | tf_op jit(solution)/shard_map/ppermute | solution.py:345
  32.9 7.1 %collective-permute-start.1 = (f32[136,128]{1,0:T(8,128)S(1)}, f32[136,128]{1,0:T(8,128)S(1)}, u32[]{:S(2)}, u32[]{:S(2)}) collective-permute-start(f32[136,128]{1,0:T(8,128)S(1)} %get-tuple-element.36), channel_id=1, source_target_pairs={{0,6},{1,7},{2,4},{3,5},{4,2},{5,3},{6,0},{7,1},{8,14},{9,15},{10,... | collective-permute-start | bytes 208904 | tf_op jit(solution)/shard_map/ppermute | solution.py:357
  36.5 5.6 %collective-permute-start.2 = (f32[136,128]{1,0:T(8,128)S(1)}, f32[136,128]{1,0:T(8,128)S(1)}, u32[]{:S(2)}, u32[]{:S(2)}) collective-permute-start(f32[136,128]{1,0:T(8,128)S(1)} %get-tuple-element.37), channel_id=1, source_target_pairs={{0,4},{1,5},{2,6},{3,7},{4,0},{5,1},{6,2},{7,3},{8,12},{9,13},{10,... | collective-permute-start | bytes 208904 | tf_op jit(solution)/shard_map/ppermute | solution.py:357
  36.5 5.7 %collective-permute-start.3 = (f32[136,128]{1,0:T(8,128)S(1)}, f32[136,128]{1,0:T(8,128)S(1)}, u32[]{:S(2)}, u32[]{:S(2)}) collective-permute-start(f32[136,128]{1,0:T(8,128)S(1)} %get-tuple-element.38), channel_id=1, source_target_pairs={{0,2},{1,3},{2,0},{3,1},{4,6},{5,7},{6,4},{7,5},{8,10},{9,11},{10,... | collective-permute-start | bytes 208904 | tf_op jit(solution)/shard_map/ppermute | solution.py:357

commit v3 on v2

--- a/solution.py
+++ b/solution.py
@@ -15,7 +15,7 @@
 f32 = jnp.float32
 bf16 = jnp.bfloat16
 VMEM = pl.BlockSpec(memory_space=pltpu.VMEM)
-ANY = pl.BlockSpec(memory_space=pl.ANY)
+HBM = pl.BlockSpec(memory_space=pltpu.HBM)
 
 
 def split(value):
@@ -218,7 +218,7 @@
 
 
 def feature_kernel(n_trade, all_ref, *refs):
-    folded_refs, out_ref = refs[:n_trade], refs[n_trade]
+    folded_refs, (out_hbm, out_ref, sem) = refs[:n_trade], refs[n_trade:]
     trade = lax.axis_index("trade")
     (high, low), columns = blocks_of(all_ref, n_trade)
     total = jnp.zeros(out_ref.shape, f32)
@@ -230,6 +230,9 @@
         fold_high, fold_low = split(folded_refs[k][...])
         total = total + nt(fold_high, adj_high) + nt(fold_low, adj_high) + nt(fold_high, adj_low)
     out_ref[...] = total
+    copy = pltpu.make_async_copy(out_ref, out_hbm, sem)
+    copy.start()
+    copy.wait()
 
 
 def last_kernel(n_chunks, scale, member_ref, *refs):
@@ -261,10 +264,10 @@
 
 def call(kernel, out_shape, in_specs, args, name, scratch=(), flops=5 * 10**8, limit=None):
     args = [
-        pltpu.with_memory_space_constraint(arg, pltpu.VMEM) if spec is VMEM else arg
+        pltpu.with_memory_space_constraint(arg, pltpu.VMEM if spec is VMEM else pltpu.HBM)
         for arg, spec in zip(args, in_specs)
     ]
-    specs = [ANY if isinstance(shape, jax.ShapeDtypeStruct) else VMEM for shape in out_shape]
+    specs = [HBM if isinstance(shape, jax.ShapeDtypeStruct) else VMEM for shape in out_shape]
     return pl.pallas_call(
         kernel,
         out_shape=out_shape,
@@ -293,7 +296,7 @@
         [vmem((own, sets), f32)] * n_trade
         + [vmem((scen + INFO, sets), f32), vmem((nfac, scen), f32), vmem((lines, BLOCK), i32)]
         + [vmem((INFO, sets), f32), vmem((sets, cols), bf16)],
-        [ANY] * 8,
+        [HBM] * 8,
         [
             factors.T,
             feat_factor.reshape(lines, BLOCK),
@@ -359,10 +362,11 @@
     ]
     (feature_sens,) = call(
         functools.partial(feature_kernel, n_trade),
-        [vmem((own, scen), f32)],
+        [struct((own, scen), f32)],
         [VMEM] * (n_trade + 1),
         [everything, *moved],
         "feature",
+        [vmem((own, scen), f32), dma],
         flops=2 * 10**9,
         limit=8 << 20,
     )

time: 43.8 us -> 37.6 us (0.86)
  local copies, waits for them, and re-layouts: 9 us -> 0 us
  Pallas kernels: 11.6 us -> 14.6 us
    unnamed x17 -> x0, local copies, waits for them, and re-layouts: 9 us -> none
    pallas_call x6, Pallas kernels: 11.6 us -> 14.6 us  [call(): pl.pallas_call(kernel, out_shape=out_shape, in_specs=in_specs, out_specs=...]
  transfers between devices with their start and end apart: 7 -> 7, of which waited for: 3 -> 3; matrix products, arithmetic and copies ran while one was open for 2% -> 0% of each run, Pallas kernels for 7% -> 10%
where the time goes in v3:
time: 37.6 us; the launch traced here: 37.4 us
  Pallas kernels  14.6 us (39%)
  blocking collectives  8.75 us (23%)
  starting transfers between devices  7.87 us (21%)
  waiting for transfers between devices  5.54 us (15%)
  between operations  0.68 us (2%)
    pallas_call x6, Pallas kernels, call(): pl.pallas_call(kernel, out_shape=out_shape, in_specs=in_specs, out_specs=...  14.6 us
    all_gather x1, blocking collectives, local(): everything = lax.all_gather(expo, 'trade', axis=0, tiled=True)  8.75 us
    ppermute x3, starting transfers between devices, local(): lax.ppermute(chunks[j], 'scen', [(i, i ^ 2 * j) for i in range(n_scen)])  4.45 us
    ppermute x1, waiting for transfers between devices, local(): peer = lax.ppermute(msg, 'scen', [(i, i ^ 1) for i in range(n_scen)])  3.25 us
    ppermute x3, waiting for transfers between devices, local(): lax.ppermute(chunks[j], 'scen', [(i, i ^ 2 * j) for i in range(n_scen)])  2.28 us
    ppermute x3, starting transfers between devices, local(): lax.ppermute(later[k - 1], 'trade', [(i, i ^ k) for i in range(n_trade)])  1.86 us
    ppermute x1, starting transfers between devices, local(): peer = lax.ppermute(msg, 'scen', [(i, i ^ 1) for i in range(n_scen)])  1.55 us
  transfers between devices with their start and end apart: 7, of which 3 were waited for; matrix products, arithmetic and copies ran while one was open for 0% of the time, Pallas kernels for 10%

profile of v3, /device:TPU:0, one launch (start us, length us, event | category | flops | bytes accessed | tf_op | source)
XLA Modules:
  0.0 37.4 jit_solution(10236765668039628938)
XLA Ops:
  0.6 9.0 %first.1 = (f32[256,128]{1,0:T(8,128)S(1)}, f32[256,128]{1,0:T(8,128)S(1)}, f32[256,128]{1,0:T(8,128)S(1)}, f32[256,128]{1,0:T(8,128)S(1)}, f32[264,128]{1,0:T(8...) custom-call(f32[64,256]{1,0:T(8,128)} %bitcast.8, ...), custom_call_target="tpu_custom_call" | custom-call | flops 500000000 | bytes 100000 | tf_op jit(solution)/shard_map/first/pallas_call | solution.py:271
  9.6 8.7 %all_gather.3.all_ref = f32[1056,128]{1,0:T(8,128)S(1)} all-gather(f32[264,128]{1,0:T(8,128)S(1)} %get-tuple-element.25), channel_id=1, replica_groups=mesh['trade'=4,'scen'=8] {'trade'}, dimensions={0}, use_global_device_ids=true | all-gather | bytes 675840 | tf_op jit(solution)/shard_map/all_gather | solution.py:327
  18.4 0.5 %second.1.msg_ref.own_ref = f32[392,128]{1,0:T(8,128)S(1)} custom-call(f32[1056,128]{1,0:T(8,128)S(1)} %all_gather.3.all_ref, f32[8,128]{1,0:T(8,128)S(1)} %get-tuple-element.26.side_ref, f32[64,256]{1,0:T(8,128)S(1)} %get-tuple-element.27.fact_ref), custom_call_target="tpu_custom_call" | custom-call | flops 500000000 | bytes 100000 | tf_op jit(solution)/shard_map/second/pallas_call | solution.py:271
  18.8 1.6 %collective-permute-start = (f32[392,128]{1,0:T(8,128)S(1)}, f32[392,128]{1,0:T(8,128)S(1)}, u32[]{:S(2)}, u32[]{:S(2)}) collective-permute-start(f32[392,128]{1,0:T(8,128)S(1)} %second.1.msg_ref.own_ref), channel_id=1, source_target_pairs={{0,1},{1,0},{2,3},{3,2},{4,5},{5,4},{6,7},{7,6},{8,9},{9,8},{10,11... | collective-permute-start | bytes 602120 | tf_op jit(solution)/shard_map/ppermute | solution.py:336
  20.4 0.1 collective-permute-start.4
  20.4 1.1 %collective-permute-start.5 = (f32[256,128]{1,0:T(8,128)S(1)}, f32[256,128]{1,0:T(8,128)S(1)}, u32[]{:S(2)}, u32[]{:S(2)}) collective-permute-start(f32[256,128]{1,0:T(8,128)S(1)} %get-tuple-element.43), channel_id=1, source_target_pairs={{0,16},{8,24},{16,0},{24,8},{1,17},{9,25},{17,1},{25,9},{2,18},{10... | collective-permute-start | bytes 393224 | tf_op jit(solution)/shard_map/ppermute | solution.py:348
  21.5 0.7 %collective-permute-start.6 = (f32[256,128]{1,0:T(8,128)S(1)}, f32[256,128]{1,0:T(8,128)S(1)}, u32[]{:S(2)}, u32[]{:S(2)}) collective-permute-start(f32[256,128]{1,0:T(8,128)S(1)} %get-tuple-element.44), channel_id=1, source_target_pairs={{0,24},{8,16},{16,8},{24,0},{1,25},{9,17},{17,9},{25,1},{2,26},{10... | collective-permute-start | bytes 393224 | tf_op jit(solution)/shard_map/ppermute | solution.py:348
  22.2 0.6 %middle.1 = (f32[768,128]{1,0:T(8,128)S(1)}, bf16[512,768]{1,0:T(8,128)(2,1)S(1)}) custom-call(f32[392,128]{1,0:T(8,128)S(1)} %second.1.msg_ref.own_ref, s32[8,128]{1,0:T(8,128)S(1)} %get-tuple-element.32.key_ref), custom_call_target="tpu_custom_call" | custom-call | flops 500000000 | bytes 100000 | tf_op jit(solution)/shard_map/middle/pallas_call | solution.py:271
  22.9 3.3 %collective-permute-done.msg_ref = f32[392,128]{1,0:T(8,128)S(1)} collective-permute-done((f32[392,128]{1,0:T(8,128)S(1)}, f32[392,128]{1,0:T(8,128)S(1)}, u32[]{:S(2)}, u32[]{:S(2)}) %collective-permute-start) | collective-permute-done | bytes 200736 | tf_op jit(solution)/shard_map/ppermute | solution.py:336
  26.1 0.7 %third.1 = (f32[136,128]{1,0:T(8,128)S(1)}, f32[136,128]{1,0:T(8,128)S(1)}, f32[136,128]{1,0:T(8,128)S(1)}, f32[136,128]{1,0:T(8,128)S(1)}) custom-call(f32[392,128]{1,0:T(8,128)S(1)} %collective-permute-done.msg_ref, f32[392,128]{1,0:T(8,128)S(1)} %second.1.msg_ref.own_ref, f32[768,128]{1,0:T(8,128)S(1)} %get-tuple-element.33.grid_ref, ...), custom_call_target="tpu_custom_call" | custom-call | flops 500000000 | bytes 100000 | tf_op jit(solution)/shard_map/third/pallas_call | solution.py:271
  26.8 3.7 %collective-permute-start.1 = (f32[136,128]{1,0:T(8,128)S(1)}, f32[136,128]{1,0:T(8,128)S(1)}, u32[]{:S(2)}, u32[]{:S(2)}) collective-permute-start(f32[136,128]{1,0:T(8,128)S(1)} %get-tuple-element.36), channel_id=1, source_target_pairs={{0,6},{1,7},{2,4},{3,5},{4,2},{5,3},{6,0},{7,1},{8,14},{9,15},{10,... | collective-permute-start | bytes 208904 | tf_op jit(solution)/shard_map/ppermute | solution.py:360
  30.5 0.0 collective-permute-start.2
  30.5 0.0 collective-permute-done.4.refs_1_
  30.5 0.8 %collective-permute-start.3 = (f32[136,128]{1,0:T(8,128)S(1)}, f32[136,128]{1,0:T(8,128)S(1)}, u32[]{:S(2)}, u32[]{:S(2)}) collective-permute-start(f32[136,128]{1,0:T(8,128)S(1)} %get-tuple-element.38), channel_id=1, source_target_pairs={{0,2},{1,3},{2,0},{3,1},{4,6},{5,7},{6,4},{7,5},{8,10},{9,11},{10,... | collective-permute-start | bytes 208904 | tf_op jit(solution)/shard_map/ppermute | solution.py:360
  31.3 0.0 collective-permute-done.5.refs_2_
  31.3 0.0 collective-permute-done.6.refs_3_
  31.3 2.6 %feature.1 = f32[256,256]{1,0:T(8,128)} custom-call(f32[1056,128]{1,0:T(8,128)S(1)} %all_gather.3.all_ref, f32[256,128]{1,0:T(8,128)S(1)} %get-tuple-element.41.refs_0_, f32[256,128]{1,0:T(8,128)S(1)} %collective-permute-done.4.refs_1_, f32[256,128]{1,0:T(8,128)S(1)} %collective-permute-done.5.refs_2_, f32[256,128]{1,0:T(8,128)S(1)} %collective-permute-done.6.refs_3_), custom_call_target="tpu_custom_call" | custom-call | flops 2000000000 | bytes 100000 | tf_op jit(solution)/shard_map/feature/pallas_call | solution.py:271
  33.9 0.0 collective-permute-done.1.refs_1_
  33.9 2.2 %collective-permute-done.2.refs_2_ = f32[136,128]{1,0:T(8,128)S(1)} collective-permute-done((f32[136,128]{1,0:T(8,128)S(1)}, f32[136,128]{1,0:T(8,128)S(1)}, u32[]{:S(2)}, u32[]{:S(2)}) %collective-permute-start.2) | collective-permute-done | bytes 69664 | tf_op jit(solution)/shard_map/ppermute | solution.py:360
  36.1 0.1 collective-permute-done.3.refs_3_
  36.2 1.2 %last.1 = (f32[1,128]{1,0:T(1,128)}, f32[128,2048]{1,0:T(8,128)}) custom-call(bf16[128,2048]{1,0:T(8,128)(2,1)S(1)} %get-tuple-element.24.member_ref, f32[136,128]{1,0:T(8,128)S(1)} %get-tuple-element.35.refs_0_, f32[136,128]{1,0:T(8,128)S(1)} %collective-permute-done.1.refs_1_, f32[136,128]{1,0:T(8,128)S(1)} %collective-permute-done.2.refs_2_, ...), custom_call_target="tpu_custom_call" | custom-call | flops 500000000 | bytes 100000 | tf_op jit(solution)/shard_map/last/pallas_call | solution.py:271
Async XLA Ops:
  18.8 7.3 %collective-permute-start = (f32[392,128]{1,0:T(8,128)S(1)}, f32[392,128]{1,0:T(8,128)S(1)}, u32[]{:S(2)}, u32[]{:S(2)}) collective-permute-start(f32[392,128]{1,0:T(8,128)S(1)} %second.1.msg_ref.own_ref), channel_id=1, source_target_pairs={{0,1},{1,0},{2,3},{3,2},{4,5},{5,4},{6,7},{7,6},{8,9},{9,8},{10,11... | collective-permute-start | bytes 602120 | tf_op jit(solution)/shard_map/ppermute | solution.py:336
  20.4 10.1 %collective-permute-start.4 = (f32[256,128]{1,0:T(8,128)S(1)}, f32[256,128]{1,0:T(8,128)S(1)}, u32[]{:S(2)}, u32[]{:S(2)}) collective-permute-start(f32[256,128]{1,0:T(8,128)S(1)} %get-tuple-element.42), channel_id=1, source_target_pairs={{0,8},{8,0},{16,24},{24,16},{1,9},{9,1},{17,25},{25,17},{2,10},{10... | collective-permute-start | bytes 393224 | tf_op jit(solution)/shard_map/ppermute | solution.py:348
  20.4 10.8 %collective-permute-start.5 = (f32[256,128]{1,0:T(8,128)S(1)}, f32[256,128]{1,0:T(8,128)S(1)}, u32[]{:S(2)}, u32[]{:S(2)}) collective-permute-start(f32[256,128]{1,0:T(8,128)S(1)} %get-tuple-element.43), channel_id=1, source_target_pairs={{0,16},{8,24},{16,0},{24,8},{1,17},{9,25},{17,1},{25,9},{2,18},{10... | collective-permute-start | bytes 393224 | tf_op jit(solution)/shard_map/ppermute | solution.py:348
  21.5 9.8 %collective-permute-start.6 = (f32[256,128]{1,0:T(8,128)S(1)}, f32[256,128]{1,0:T(8,128)S(1)}, u32[]{:S(2)}, u32[]{:S(2)}) collective-permute-start(f32[256,128]{1,0:T(8,128)S(1)} %get-tuple-element.44), channel_id=1, source_target_pairs={{0,24},{8,16},{16,8},{24,0},{1,25},{9,17},{17,9},{25,1},{2,26},{10... | collective-permute-start | bytes 393224 | tf_op jit(solution)/shard_map/ppermute | solution.py:348
  26.8 7.1 %collective-permute-start.1 = (f32[136,128]{1,0:T(8,128)S(1)}, f32[136,128]{1,0:T(8,128)S(1)}, u32[]{:S(2)}, u32[]{:S(2)}) collective-permute-start(f32[136,128]{1,0:T(8,128)S(1)} %get-tuple-element.36), channel_id=1, source_target_pairs={{0,6},{1,7},{2,4},{3,5},{4,2},{5,3},{6,0},{7,1},{8,14},{9,15},{10,... | collective-permute-start | bytes 208904 | tf_op jit(solution)/shard_map/ppermute | solution.py:360
  30.5 5.6 %collective-permute-start.2 = (f32[136,128]{1,0:T(8,128)S(1)}, f32[136,128]{1,0:T(8,128)S(1)}, u32[]{:S(2)}, u32[]{:S(2)}) collective-permute-start(f32[136,128]{1,0:T(8,128)S(1)} %get-tuple-element.37), channel_id=1, source_target_pairs={{0,4},{1,5},{2,6},{3,7},{4,0},{5,1},{6,2},{7,3},{8,12},{9,13},{10,... | collective-permute-start | bytes 208904 | tf_op jit(solution)/shard_map/ppermute | solution.py:360
  30.5 5.7 %collective-permute-start.3 = (f32[136,128]{1,0:T(8,128)S(1)}, f32[136,128]{1,0:T(8,128)S(1)}, u32[]{:S(2)}, u32[]{:S(2)}) collective-permute-start(f32[136,128]{1,0:T(8,128)S(1)} %get-tuple-element.38), channel_id=1, source_target_pairs={{0,2},{1,3},{2,0},{3,1},{4,6},{5,7},{6,4},{7,5},{8,10},{9,11},{10,... | collective-permute-start | bytes 208904 | tf_op jit(solution)/shard_map/ppermute | solution.py:360

commit v4 on v3

--- a/solution.py
+++ b/solution.py
@@ -74,7 +74,7 @@
     ins, rest = refs[:8], refs[8:]
     folded_refs, rest = rest[:n_trade], rest[n_trade:]
     expo_ref, fact_out, key_out, side_out, member_out = rest[:5]
-    fact_ref, factor_ref, degree_ref, set_ref, party_ref, thr_ref, wgt_ref, coef_buf, grid_ref, small, sems = rest[5:]
+    fact_ref, factor_ref, degree_ref, set_ref, party_ref, thr_ref, wgt_ref, coef_buf, small, sems = rest[5:]
     fact_hbm, factor_hbm, degree_hbm, coef_hbm, set_hbm, party_hbm, thr_hbm, wgt_hbm = ins
     me = lax.axis_index("trade")
     width, cols = coef_hbm.shape
@@ -110,7 +110,7 @@
     for load in loads:
         load.start()
     for step in range(steps):
-        copy(step).start()
+        copy(step).start(priority=1)
     for load in loads:
         load.wait()
     member = jnp.where(set_ref[...] - me * sets == iota((sets, cols), 0), f32(1), f32(0))
@@ -125,22 +125,30 @@
     line = iota((INFO, sets), 0)
     expo_ref[scen:, :] = jnp.where(line == 0, party.astype(f32), jnp.where(line == 1, thr_row, wgt_row))
     side_out[...] = jnp.where(line == 0, thr_ref[pl.ds(me, 1), :], wgt_ref[pl.ds(me, 1), :])
-    for pair in range(steps // 2):
-        highs, lows, keys = [], [], []
-        for step in (2 * pair, 2 * pair + 1):
+    keys = [key_out[pl.ds(lax.div(start_row(step), BLOCK), 1), :] for step in range(steps)]
+    chosen = one_hot(iota((MAXDEG * nfac, width), 0) == jnp.concatenate(keys, axis=1))
+    phi = [nn(part, chosen).astype(bf16) for part in table]
+    done, total = 0, None
+    for size in (steps // 2, steps - steps // 2):
+        group = range(done, done + size)
+        for step in group:
             copy(step).wait()
+        highs, lows = [], []
+        for step in group:
             coef_high, coef_low = split(coef_buf[step])
             folded = nn(coef_high, turned_member) + nn(coef_low, turned_member)
             folded_refs[step // per][pl.ds((step % per) * BLOCK, BLOCK), :] = folded
             high, low = split(folded)
             highs.append(high)
             lows.append(low)
-            keys.append(key_out[pl.ds(lax.div(start_row(step), BLOCK), 1), :])
-        right = jnp.concatenate([jnp.concatenate(highs, axis=0), jnp.concatenate(lows, axis=0)], axis=1)
-        chosen = one_hot(iota((MAXDEG * nfac, 2 * BLOCK), 0) == jnp.concatenate(keys, axis=1))
-        part = nn(chosen, right)
-        grid_ref[...] = part if pair == 0 else grid_ref[...] + part
-    expo_ref[:scen, :] = pair_nn(table, split(grid_ref[:, :sets] + grid_ref[:, sets:]))
+        here = slice(done * BLOCK, (done + size) * BLOCK)
+        part = pair_nn(
+            [piece[:, here] for piece in phi],
+            [jnp.concatenate(highs, axis=0), jnp.concatenate(lows, axis=0)],
+        )
+        total = part if total is None else total + part
+        done += size
+    expo_ref[:scen, :] = total
 
 
 def blocks_of(all_ref, n_trade):
@@ -317,7 +325,6 @@
             vmem((n_trade, sets), f32),
             vmem((n_trade, sets), f32),
             vmem((lines, BLOCK, cols), f32),
-            vmem((grid, 2 * sets), f32),
             dma((7,)),
             dma((lines,)),
         ],
@@ -358,7 +365,7 @@
     )
     chunks = [chunks[0]] + [
         lax.ppermute(chunks[j], "scen", [(i, i ^ (2 * j)) for i in range(n_scen)])
-        for j in range(n_scen // 2 - 1, 0, -1)
+        for j in [*range(n_scen // 4, n_scen // 2), *range(1, n_scen // 4)]
     ]
     (feature_sens,) = call(
         functools.partial(feature_kernel, n_trade),

time: 37.6 us -> 33.7 us (0.90)
  Pallas kernels: 14.6 us -> 11 us
    pallas_call x6, Pallas kernels: 14.6 us -> 11 us  [call(): pl.pallas_call(kernel, out_shape=out_shape, in_specs=in_specs, out_specs=...]
  transfers between devices with their start and end apart: 7 -> 7, of which waited for: 3 -> 4; matrix products, arithmetic and copies ran while one was open for 0% -> 0% of each run, Pallas kernels for 10% -> 12%
where the time goes in v4:
time: 33.7 us; the launch traced here: 33.6 us
  Pallas kernels  11 us (33%)
  blocking collectives  8.76 us (26%)
  starting transfers between devices  7.65 us (23%)
  waiting for transfers between devices  5.48 us (16%)
  between operations  0.67 us (2%)
    pallas_call x6, Pallas kernels, call(): pl.pallas_call(kernel, out_shape=out_shape, in_specs=in_specs, out_specs=...  11 us
    all_gather x1, blocking collectives, local(): everything = lax.all_gather(expo, 'trade', axis=0, tiled=True)  8.76 us
    ppermute x3, starting transfers between devices, local(): lax.ppermute(chunks[j], 'scen', [(i, i ^ 2 * j) for i in range(n_scen)])  4.23 us
    ppermute x1, waiting for transfers between devices, local(): peer = lax.ppermute(msg, 'scen', [(i, i ^ 1) for i in range(n_scen)])  3.25 us
    ppermute x3, waiting for transfers between devices, local(): lax.ppermute(chunks[j], 'scen', [(i, i ^ 2 * j) for i in range(n_scen)])  2.22 us
    ppermute x3, starting transfers between devices, local(): lax.ppermute(later[k - 1], 'trade', [(i, i ^ k) for i in range(n_trade)])  1.86 us
    ppermute x1, starting transfers between devices, local(): peer = lax.ppermute(msg, 'scen', [(i, i ^ 1) for i in range(n_scen)])  1.56 us
  transfers between devices with their start and end apart: 7, of which 4 were waited for; matrix products, arithmetic and copies ran while one was open for 0% of the time, Pallas kernels for 12%

profile of v4, /device:TPU:0, one launch (start us, length us, event | category | flops | bytes accessed | tf_op | source)
XLA Modules:
  0.0 33.6 jit_solution(7451095508492596252)
XLA Ops:
  0.6 5.4 %first.1 = (f32[256,128]{1,0:T(8,128)S(1)}, f32[256,128]{1,0:T(8,128)S(1)}, f32[256,128]{1,0:T(8,128)S(1)}, f32[256,128]{1,0:T(8,128)S(1)}, f32[264,128]{1,0:T(8...) custom-call(f32[64,256]{1,0:T(8,128)} %bitcast.8, ...), custom_call_target="tpu_custom_call" | custom-call | flops 500000000 | bytes 100000 | tf_op jit(solution)/shard_map/first/pallas_call | solution.py:279
  6.0 8.8 %all_gather.3.all_ref = f32[1056,128]{1,0:T(8,128)S(1)} all-gather(f32[264,128]{1,0:T(8,128)S(1)} %get-tuple-element.25), channel_id=1, replica_groups=mesh['trade'=4,'scen'=8] {'trade'}, dimensions={0}, use_global_device_ids=true | all-gather | bytes 675840 | tf_op jit(solution)/shard_map/all_gather | solution.py:334
  14.8 0.5 %second.1.msg_ref.own_ref = f32[392,128]{1,0:T(8,128)S(1)} custom-call(f32[1056,128]{1,0:T(8,128)S(1)} %all_gather.3.all_ref, f32[8,128]{1,0:T(8,128)S(1)} %get-tuple-element.26.side_ref, f32[64,256]{1,0:T(8,128)S(1)} %get-tuple-element.27.fact_ref), custom_call_target="tpu_custom_call" | custom-call | flops 500000000 | bytes 100000 | tf_op jit(solution)/shard_map/second/pallas_call | solution.py:279
  15.3 1.6 %collective-permute-start = (f32[392,128]{1,0:T(8,128)S(1)}, f32[392,128]{1,0:T(8,128)S(1)}, u32[]{:S(2)}, u32[]{:S(2)}) collective-permute-start(f32[392,128]{1,0:T(8,128)S(1)} %second.1.msg_ref.own_ref), channel_id=1, source_target_pairs={{0,1},{1,0},{2,3},{3,2},{4,5},{5,4},{6,7},{7,6},{8,9},{9,8},{10,11... | collective-permute-start | bytes 602120 | tf_op jit(solution)/shard_map/ppermute | solution.py:343
  16.8 0.1 collective-permute-start.4
  16.9 1.1 %collective-permute-start.5 = (f32[256,128]{1,0:T(8,128)S(1)}, f32[256,128]{1,0:T(8,128)S(1)}, u32[]{:S(2)}, u32[]{:S(2)}) collective-permute-start(f32[256,128]{1,0:T(8,128)S(1)} %get-tuple-element.43), channel_id=1, source_target_pairs={{0,16},{8,24},{16,0},{24,8},{1,17},{9,25},{17,1},{25,9},{2,18},{10... | collective-permute-start | bytes 393224 | tf_op jit(solution)/shard_map/ppermute | solution.py:355
  18.0 0.7 %collective-permute-start.6 = (f32[256,128]{1,0:T(8,128)S(1)}, f32[256,128]{1,0:T(8,128)S(1)}, u32[]{:S(2)}, u32[]{:S(2)}) collective-permute-start(f32[256,128]{1,0:T(8,128)S(1)} %get-tuple-element.44), channel_id=1, source_target_pairs={{0,24},{8,16},{16,8},{24,0},{1,25},{9,17},{17,9},{25,1},{2,26},{10... | collective-permute-start | bytes 393224 | tf_op jit(solution)/shard_map/ppermute | solution.py:355
  18.7 0.6 %middle.1 = (f32[768,128]{1,0:T(8,128)S(1)}, bf16[512,768]{1,0:T(8,128)(2,1)S(1)}) custom-call(f32[392,128]{1,0:T(8,128)S(1)} %second.1.msg_ref.own_ref, s32[8,128]{1,0:T(8,128)S(1)} %get-tuple-element.32.key_ref), custom_call_target="tpu_custom_call" | custom-call | flops 500000000 | bytes 100000 | tf_op jit(solution)/shard_map/middle/pallas_call | solution.py:279
  19.3 3.3 %collective-permute-done.msg_ref = f32[392,128]{1,0:T(8,128)S(1)} collective-permute-done((f32[392,128]{1,0:T(8,128)S(1)}, f32[392,128]{1,0:T(8,128)S(1)}, u32[]{:S(2)}, u32[]{:S(2)}) %collective-permute-start) | collective-permute-done | bytes 200736 | tf_op jit(solution)/shard_map/ppermute | solution.py:343
  22.6 0.7 %third.1 = (f32[136,128]{1,0:T(8,128)S(1)}, f32[136,128]{1,0:T(8,128)S(1)}, f32[136,128]{1,0:T(8,128)S(1)}, f32[136,128]{1,0:T(8,128)S(1)}) custom-call(f32[392,128]{1,0:T(8,128)S(1)} %collective-permute-done.msg_ref, f32[392,128]{1,0:T(8,128)S(1)} %second.1.msg_ref.own_ref, f32[768,128]{1,0:T(8,128)S(1)} %get-tuple-element.33.grid_ref, ...), custom_call_target="tpu_custom_call" | custom-call | flops 500000000 | bytes 100000 | tf_op jit(solution)/shard_map/third/pallas_call | solution.py:279
  23.3 2.7 %collective-permute-start.1 = (f32[136,128]{1,0:T(8,128)S(1)}, f32[136,128]{1,0:T(8,128)S(1)}, u32[]{:S(2)}, u32[]{:S(2)}) collective-permute-start(f32[136,128]{1,0:T(8,128)S(1)} %get-tuple-element.36), channel_id=1, source_target_pairs={{0,4},{1,5},{2,6},{3,7},{4,0},{5,1},{6,2},{7,3},{8,12},{9,13},{10,... | collective-permute-start | bytes 208904 | tf_op jit(solution)/shard_map/ppermute | solution.py:367
  25.9 1.4 %collective-permute-start.2 = (f32[136,128]{1,0:T(8,128)S(1)}, f32[136,128]{1,0:T(8,128)S(1)}, u32[]{:S(2)}, u32[]{:S(2)}) collective-permute-start(f32[136,128]{1,0:T(8,128)S(1)} %get-tuple-element.37), channel_id=1, source_target_pairs={{0,6},{1,7},{2,4},{3,5},{4,2},{5,3},{6,0},{7,1},{8,14},{9,15},{10,... | collective-permute-start | bytes 208904 | tf_op jit(solution)/shard_map/ppermute | solution.py:367
  27.3 0.0 collective-permute-done.4.refs_1_
  27.3 0.2 collective-permute-start.3
  27.5 0.0 collective-permute-done.5.refs_2_
  27.5 0.0 collective-permute-done.6.refs_3_
  27.5 2.6 %feature.1 = f32[256,256]{1,0:T(8,128)} custom-call(f32[1056,128]{1,0:T(8,128)S(1)} %all_gather.3.all_ref, f32[256,128]{1,0:T(8,128)S(1)} %get-tuple-element.41.refs_0_, f32[256,128]{1,0:T(8,128)S(1)} %collective-permute-done.4.refs_1_, f32[256,128]{1,0:T(8,128)S(1)} %collective-permute-done.5.refs_2_, f32[256,128]{1,0:T(8,128)S(1)} %collective-permute-done.6.refs_3_), custom_call_target="tpu_custom_call" | custom-call | flops 2000000000 | bytes 100000 | tf_op jit(solution)/shard_map/feature/pallas_call | solution.py:279
  30.1 0.3 collective-permute-done.1.refs_1_
  30.4 1.7 %collective-permute-done.2.refs_2_ = f32[136,128]{1,0:T(8,128)S(1)} collective-permute-done((f32[136,128]{1,0:T(8,128)S(1)}, f32[136,128]{1,0:T(8,128)S(1)}, u32[]{:S(2)}, u32[]{:S(2)}) %collective-permute-start.2) | collective-permute-done | bytes 69664 | tf_op jit(solution)/shard_map/ppermute | solution.py:367
  32.1 0.2 collective-permute-done.3.refs_3_
  32.3 1.2 %last.1 = (f32[1,128]{1,0:T(1,128)}, f32[128,2048]{1,0:T(8,128)}) custom-call(bf16[128,2048]{1,0:T(8,128)(2,1)S(1)} %get-tuple-element.24.member_ref, f32[136,128]{1,0:T(8,128)S(1)} %get-tuple-element.35.refs_0_, f32[136,128]{1,0:T(8,128)S(1)} %collective-permute-done.1.refs_1_, f32[136,128]{1,0:T(8,128)S(1)} %collective-permute-done.2.refs_2_, ...), custom_call_target="tpu_custom_call" | custom-call | flops 500000000 | bytes 100000 | tf_op jit(solution)/shard_map/last/pallas_call | solution.py:279
Async XLA Ops:
  15.3 7.3 %collective-permute-start = (f32[392,128]{1,0:T(8,128)S(1)}, f32[392,128]{1,0:T(8,128)S(1)}, u32[]{:S(2)}, u32[]{:S(2)}) collective-permute-start(f32[392,128]{1,0:T(8,128)S(1)} %second.1.msg_ref.own_ref), channel_id=1, source_target_pairs={{0,1},{1,0},{2,3},{3,2},{4,5},{5,4},{6,7},{7,6},{8,9},{9,8},{10,11... | collective-permute-start | bytes 602120 | tf_op jit(solution)/shard_map/ppermute | solution.py:343
  16.8 10.5 %collective-permute-start.4 = (f32[256,128]{1,0:T(8,128)S(1)}, f32[256,128]{1,0:T(8,128)S(1)}, u32[]{:S(2)}, u32[]{:S(2)}) collective-permute-start(f32[256,128]{1,0:T(8,128)S(1)} %get-tuple-element.42), channel_id=1, source_target_pairs={{0,8},{8,0},{16,24},{24,16},{1,9},{9,1},{17,25},{25,17},{2,10},{10... | collective-permute-start | bytes 393224 | tf_op jit(solution)/shard_map/ppermute | solution.py:355
  16.9 10.6 %collective-permute-start.5 = (f32[256,128]{1,0:T(8,128)S(1)}, f32[256,128]{1,0:T(8,128)S(1)}, u32[]{:S(2)}, u32[]{:S(2)}) collective-permute-start(f32[256,128]{1,0:T(8,128)S(1)} %get-tuple-element.43), channel_id=1, source_target_pairs={{0,16},{8,24},{16,0},{24,8},{1,17},{9,25},{17,1},{25,9},{2,18},{10... | collective-permute-start | bytes 393224 | tf_op jit(solution)/shard_map/ppermute | solution.py:355
  18.0 9.5 %collective-permute-start.6 = (f32[256,128]{1,0:T(8,128)S(1)}, f32[256,128]{1,0:T(8,128)S(1)}, u32[]{:S(2)}, u32[]{:S(2)}) collective-permute-start(f32[256,128]{1,0:T(8,128)S(1)} %get-tuple-element.44), channel_id=1, source_target_pairs={{0,24},{8,16},{16,8},{24,0},{1,25},{9,17},{17,9},{25,1},{2,26},{10... | collective-permute-start | bytes 393224 | tf_op jit(solution)/shard_map/ppermute | solution.py:355
  23.3 7.2 %collective-permute-start.1 = (f32[136,128]{1,0:T(8,128)S(1)}, f32[136,128]{1,0:T(8,128)S(1)}, u32[]{:S(2)}, u32[]{:S(2)}) collective-permute-start(f32[136,128]{1,0:T(8,128)S(1)} %get-tuple-element.36), channel_id=1, source_target_pairs={{0,4},{1,5},{2,6},{3,7},{4,0},{5,1},{6,2},{7,3},{8,12},{9,13},{10,... | collective-permute-start | bytes 208904 | tf_op jit(solution)/shard_map/ppermute | solution.py:367
  25.9 6.2 %collective-permute-start.2 = (f32[136,128]{1,0:T(8,128)S(1)}, f32[136,128]{1,0:T(8,128)S(1)}, u32[]{:S(2)}, u32[]{:S(2)}) collective-permute-start(f32[136,128]{1,0:T(8,128)S(1)} %get-tuple-element.37), channel_id=1, source_target_pairs={{0,6},{1,7},{2,4},{3,5},{4,2},{5,3},{6,0},{7,1},{8,14},{9,15},{10,... | collective-permute-start | bytes 208904 | tf_op jit(solution)/shard_map/ppermute | solution.py:367
  27.3 5.1 %collective-permute-start.3 = (f32[136,128]{1,0:T(8,128)S(1)}, f32[136,128]{1,0:T(8,128)S(1)}, u32[]{:S(2)}, u32[]{:S(2)}) collective-permute-start(f32[136,128]{1,0:T(8,128)S(1)} %get-tuple-element.38), channel_id=1, source_target_pairs={{0,2},{1,3},{2,0},{3,1},{4,6},{5,7},{6,4},{7,5},{8,10},{9,11},{10,... | collective-permute-start | bytes 208904 | tf_op jit(solution)/shard_map/ppermute | solution.py:367

commit v5 on v4

--- a/solution.py
+++ b/solution.py
@@ -6,6 +6,7 @@
 from jax.experimental import pallas as pl
 from jax.experimental.pallas import tpu as pltpu
 from jax.sharding import PartitionSpec as P
+
 
 MAXDEG = 12
 SET_SIZE = 16
@@ -151,54 +152,43 @@
     expo_ref[:scen, :] = total
 
 
-def blocks_of(all_ref, n_trade):
-    stride = all_ref.shape[0] // n_trade
-    scen = stride - INFO
-    expo = [split(all_ref[a * stride : a * stride + scen, :]) for a in range(n_trade)]
-    pieces = tuple(jnp.concatenate([e[i] for e in expo], axis=1) for i in range(2))
-    columns = [column(all_ref[a * stride + scen : a * stride + scen + 1, :]) for a in range(n_trade)]
-    return pieces, columns
+def blocks_of(refs):
+    scen = refs[0].shape[0] - INFO
+    expo = [split(ref[:scen, :]) for ref in refs]
+    pieces = [jnp.concatenate([e[i] for e in expo], axis=1) for i in range(2)]
+    return pieces, [column(ref[scen : scen + 1, :]) for ref in refs]
 
 
 def same_as(columns, row):
     return one_hot(jnp.concatenate([here == row for here in columns], axis=0))
 
 
-def info_of(all_ref, n_trade, block):
-    stride = all_ref.shape[0] // n_trade
-    info = all_ref[pl.ds(pl.multiple_of(block * stride + stride - INFO, INFO), INFO), :]
+def info_of(ref):
+    info = ref[ref.shape[0] - INFO :, :]
     return info[0:1, :], info[1:2, :], info[2:3, :]
 
 
-def second_kernel(n_trade, all_ref, side_ref, fact_ref, msg_ref):
+def second_kernel(n_trade, *refs):
+    blocks, (side_ref, _, msg_ref) = refs[:n_trade], refs[n_trade:]
     trade = lax.axis_index("trade")
-    sets = all_ref.shape[1]
-    scen = all_ref.shape[0] // n_trade - INFO
-    (high, low), columns = blocks_of(all_ref, n_trade)
-    party, thr, wgt = info_of(all_ref, n_trade, trade)
+    scen, sets = blocks[0].shape[0] - INFO, blocks[0].shape[1]
+    (high, low), columns = blocks_of(blocks)
+    party, thr, wgt = info_of(blocks[0])
     mine = (iota((1, sets), 1) + trade * sets).astype(f32)
     right = jnp.concatenate([same_as(columns, party), same_as(columns, mine)], axis=1)
     netted = nn(high, right) + nn(low, right)
     msg_ref[:scen, :] = wgt * jax.nn.sigmoid(netted[:, :sets] - thr)
     soft = jax.nn.softplus(netted[:, sets:] - side_ref[0:1, :])
-    msg_ref[scen : scen + INFO, :] = jnp.broadcast_to(
+    msg_ref[scen:, :] = jnp.broadcast_to(
         jnp.sum(soft, axis=0, keepdims=True) * side_ref[1:2, :], (INFO, sets)
     )
-    nfac, base = fact_ref.shape[0], scen + INFO
-    for piece in range(scen // sets):
-        msg_ref[base + piece * nfac : base + (piece + 1) * nfac, :] = fact_ref[:, piece * sets : (piece + 1) * sets]
-
-
-def response(msg_ref, nfac, scen):
-    base = scen + INFO
-    pieces = (msg_ref.shape[0] - base) // nfac
-    points = jnp.concatenate(
-        [msg_ref[base + i * nfac : base + (i + 1) * nfac, :] for i in range(pieces)], axis=1
-    )
-    return pair_nn(split(basis(points)), split(msg_ref[:scen, :]))
-
-
-def middle_kernel(n_scen, nfac, scen, msg_ref, key_ref, grid_ref, chosen_ref, column_ref):
+
+
+def response(table, msg_ref):
+    return pair_nn(table, split(msg_ref[: msg_ref.shape[0] - INFO, :]))
+
+
+def middle_kernel(n_scen, msg_ref, fact_ref, peer_ref, key_ref, grid_ref, chosen_ref, high_ref, low_ref, column_ref):
     me = lax.axis_index("scen")
     lines = key_ref.shape[0]
     chunk = lines * BLOCK // n_scen
@@ -211,27 +201,27 @@
             chosen_ref[j * chunk : (j + 1) * chunk, i * BLOCK : (i + 1) * BLOCK] = one_hot(
                 here == iota(here.shape, 1) + i * BLOCK
             )
-    grid_ref[...] = response(msg_ref, nfac, scen)
-
-
-def third_kernel(n_scen, nfac, scen, msg_ref, own_ref, grid_ref, chosen_ref, *chunk_refs):
+    grid_ref[...] = response(split(basis(fact_ref[...])), msg_ref)
+    high_ref[...], low_ref[...] = split(basis(peer_ref[...]))
+
+
+def third_kernel(msg_ref, high_ref, low_ref, own_ref, grid_ref, chosen_ref, *chunk_refs):
     chunk = chosen_ref.shape[0] // len(chunk_refs)
-    both = jnp.concatenate(split(grid_ref[...] + response(msg_ref, nfac, scen)), axis=1)
-    xva = msg_ref[scen : scen + INFO, :] + own_ref[scen : scen + INFO, :]
-    sets = msg_ref.shape[1]
+    both = jnp.concatenate(split(grid_ref[...] + response((high_ref[...], low_ref[...]), msg_ref)), axis=1)
+    scen, sets = msg_ref.shape[0] - INFO, msg_ref.shape[1]
+    xva = msg_ref[scen:, :] + own_ref[scen:, :]
     for j, ref in enumerate(chunk_refs):
         part = nn(chosen_ref[j * chunk : (j + 1) * chunk, :], both)
         ref[:chunk, :] = part[:, :sets] + part[:, sets:]
         ref[chunk:, :] = xva
 
 
-def feature_kernel(n_trade, all_ref, *refs):
-    folded_refs, (out_hbm, out_ref, sem) = refs[:n_trade], refs[n_trade:]
-    trade = lax.axis_index("trade")
-    (high, low), columns = blocks_of(all_ref, n_trade)
+def feature_kernel(n_trade, *refs):
+    blocks, folded_refs, (out_hbm, out_ref, sem) = refs[:n_trade], refs[n_trade : 2 * n_trade], refs[2 * n_trade :]
+    (high, low), columns = blocks_of(blocks)
     total = jnp.zeros(out_ref.shape, f32)
     for k in range(n_trade):
-        party, thr, wgt = info_of(all_ref, n_trade, trade ^ k)
+        party, thr, wgt = info_of(blocks[k])
         same = same_as(columns, party)
         netted = nn(high, same) + nn(low, same)
         adj_high, adj_low = split(wgt * jax.nn.sigmoid(netted - thr))
@@ -270,7 +260,7 @@
         copy.wait()
 
 
-def call(kernel, out_shape, in_specs, args, name, scratch=(), flops=5 * 10**8, limit=None):
+def call(kernel, out_shape, in_specs, args, scratch=(), flops=5 * 10**8, limit=None):
     args = [
         pltpu.with_memory_space_constraint(arg, pltpu.VMEM if spec is VMEM else pltpu.HBM)
         for arg, spec in zip(args, in_specs)
@@ -284,8 +274,11 @@
         scratch_shapes=scratch,
         cost_estimate=pl.CostEstimate(flops=flops, bytes_accessed=10**5, transcendentals=0),
         compiler_params=pltpu.CompilerParams(vmem_limit_bytes=limit),
-        name=name,
     )(*args)
+
+
+def send(value, axis, k):
+    return lax.ppermute(value, axis, [(i, i ^ k) for i in range(lax.axis_size(axis))])
 
 
 def local(
@@ -315,7 +308,6 @@
             threshold.reshape(n_trade, sets),
             weight.reshape(n_trade, sets),
         ],
-        "first",
         [
             vmem((nfac, scen), f32),
             vmem((lines, BLOCK), i32),
@@ -331,48 +323,47 @@
         limit=32 << 20,
     )
     folded, (expo, fact, key, side, member) = outs[:n_trade], outs[n_trade:]
-    everything = lax.all_gather(expo, "trade", axis=0, tiled=True)
+    blocks = [expo] + [None] * (n_trade - 1)
+    for k in range(2, n_trade, 2):
+        blocks[k] = send(expo, "trade", k)
+    blocks[1] = send(expo, "trade", 1)
+    for k in range(2, n_trade, 2):
+        blocks[k + 1] = send(blocks[k], "trade", 1)
+    peer_fact = send(fact, "scen", 1)
     (msg,) = call(
         functools.partial(second_kernel, n_trade),
-        [vmem((scen + INFO + nfac * scen // sets, sets), f32)],
-        [VMEM] * 3,
-        [everything, side, fact],
-        "second",
-        limit=8 << 20,
-    )
-    peer = lax.ppermute(msg, "scen", [(i, i ^ 1) for i in range(n_scen)])
-    half, chosen = call(
-        functools.partial(middle_kernel, n_scen, nfac, scen),
-        [vmem((grid, sets), f32), vmem((width // 2, grid), bf16)],
-        [VMEM] * 2,
-        [msg, key],
-        "middle",
+        [vmem((scen + INFO, sets), f32)],
+        [VMEM] * (n_trade + 2),
+        [*blocks, side, peer_fact],
+        limit=8 << 20,
+    )
+    peer = send(msg, "scen", 1)
+    half, chosen, *peer_table = call(
+        functools.partial(middle_kernel, n_scen),
+        [vmem((grid, sets), f32), vmem((width // 2, grid), bf16)] + [vmem((grid, scen), bf16)] * 2,
+        [VMEM] * 4,
+        [msg, fact, peer_fact, key],
         [vmem((width, BLOCK), f32)],
         limit=8 << 20,
     )
     msg, *later = lax.optimization_barrier((msg, *folded[1:]))
-    moved = [folded[0]] + [
-        lax.ppermute(later[k - 1], "trade", [(i, i ^ k) for i in range(n_trade)])
-        for k in range(1, n_trade)
-    ]
+    moved = [folded[0]] + [send(later[k - 1], "trade", k) for k in range(1, n_trade)]
     chunks = call(
-        functools.partial(third_kernel, n_scen, nfac, scen),
+        third_kernel,
         [vmem((chunk + INFO, sets), f32)] * (n_scen // 2),
-        [VMEM] * 4,
-        [peer, msg, half, chosen],
-        "third",
+        [VMEM] * 6,
+        [peer, *peer_table, msg, half, chosen],
         limit=8 << 20,
     )
     chunks = [chunks[0]] + [
-        lax.ppermute(chunks[j], "scen", [(i, i ^ (2 * j)) for i in range(n_scen)])
+        send(chunks[j], "scen", 2 * j)
         for j in [*range(n_scen // 4, n_scen // 2), *range(1, n_scen // 4)]
     ]
     (feature_sens,) = call(
         functools.partial(feature_kernel, n_trade),
         [struct((own, scen), f32)],
-        [VMEM] * (n_trade + 1),
-        [everything, *moved],
-        "feature",
+        [VMEM] * (2 * n_trade),
+        [*blocks, *moved],
         [vmem((own, scen), f32), dma],
         flops=2 * 10**9,
         limit=8 << 20,
@@ -382,7 +373,6 @@
         [struct((1, sets), f32), struct((chunk, cols), f32)],
         [VMEM] * (n_scen // 2 + 1),
         [member, *chunks],
-        "last",
         [vmem((1, sets), f32), vmem((chunk, cols), f32), dma((5,))],
         limit=8 << 20,
     )

time: 33.7 us -> 34.2 us (1.015)
  blocking collectives: 8.76 us -> 0 us
  starting transfers between devices: 7.65 us -> 12.8 us
  waiting for transfers between devices: 5.48 us -> 9.39 us
    all_gather x1 -> x0, blocking collectives: 8.76 us -> none  [local(): everything = lax.all_gather(expo, 'trade', axis=0, tiled=True)]
    ppermute x7 -> x11, starting transfers between devices: 7.65 us -> 12.8 us  [send(): lax.ppermute(value, axis, [(i, i ^ k) for i in range(lax.axis_size(axis))])]
    ppermute x7 -> x11, waiting for transfers between devices: 5.48 us -> 9.39 us  [send(): lax.ppermute(value, axis, [(i, i ^ k) for i in range(lax.axis_size(axis))])]
  transfers between devices with their start and end apart: 7 -> 11, of which waited for: 4 -> 5; matrix products, arithmetic and copies ran while one was open for 0% -> 0% of each run, Pallas kernels for 12% -> 12%
where the time goes in v5:
time: 34.2 us; the launch traced here: 34 us
  starting transfers between devices  12.8 us (37%)
  Pallas kernels  11.1 us (32%)
  waiting for transfers between devices  9.39 us (27%)
  between operations  0.69 us (2%)
    ppermute x11, starting transfers between devices, send(): lax.ppermute(value, axis, [(i, i ^ k) for i in range(lax.axis_size(axis))])  12.8 us
    pallas_call x6, Pallas kernels, call(): pl.pallas_call(kernel, out_shape=out_shape, in_specs=in_specs, out_specs=...  11.1 us
    ppermute x11, waiting for transfers between devices, send(): lax.ppermute(value, axis, [(i, i ^ k) for i in range(lax.axis_size(axis))])  9.39 us
  transfers between devices with their start and end apart: 11, of which 5 were waited for; matrix products, arithmetic and copies ran while one was open for 0% of the time, Pallas kernels for 12%

profile of v5, /device:TPU:0, one launch (start us, length us, event | category | flops | bytes accessed | tf_op | source)
XLA Modules:
  0.0 34.0 jit_solution(13143291204734594345)
XLA Ops:
  0.6 5.4 %shard_map.103 = (f32[256,128]{1,0:T(8,128)S(1)}, f32[256,128]{1,0:T(8,128)S(1)}, f32[256,128]{1,0:T(8,128)S(1)}, f32[256,128]{1,0:T(8,128)S(1)}, f32[264,128]{1...) custom-call(f32[64,256]{1,0:T(8,128)} %bitcast.8, ...), custom_call_target="tpu_custom_call" | custom-call | flops 500000000 | bytes 100000 | tf_op jit(solution)/shard_map/pallas_call | solution.py:269
  6.0 3.1 %collective-permute-start.1 = (f32[264,128]{1,0:T(8,128)S(1)}, f32[264,128]{1,0:T(8,128)S(1)}, u32[]{:S(2)}, u32[]{:S(2)}) collective-permute-start(f32[264,128]{1,0:T(8,128)S(1)} %get-tuple-element.27.refs_0_), channel_id=1, source_target_pairs={{0,16},{8,24},{16,0},{24,8},{1,17},{9,25},{17,1},{25,9},{2,18},{10... | collective-permute-start | bytes 405512 | tf_op jit(solution)/shard_map/ppermute | solution.py:281
  9.1 0.0 collective-permute-start
  9.1 3.6 %collective-permute-done.1.refs_2_ = f32[264,128]{1,0:T(8,128)S(1)} collective-permute-done((f32[264,128]{1,0:T(8,128)S(1)}, f32[264,128]{1,0:T(8,128)S(1)}, u32[]{:S(2)}, u32[]{:S(2)}) %collective-permute-start.1) | collective-permute-done | bytes 135200 | tf_op jit(solution)/shard_map/ppermute | solution.py:281
  12.7 0.0 collective-permute-start.2
  12.7 1.7 %collective-permute-start.3 = (f32[64,256]{1,0:T(8,128)S(1)}, f32[64,256]{1,0:T(8,128)S(1)}, u32[]{:S(2)}, u32[]{:S(2)}) collective-permute-start(f32[64,256]{1,0:T(8,128)S(1)} %get-tuple-element.29.fact_ref), channel_id=1, source_target_pairs={{0,1},{1,0},{2,3},{3,2},{4,5},{5,4},{6,7},{7,6},{8,9},{9,8},{10,11... | collective-permute-start | bytes 196616 | tf_op jit(solution)/shard_map/ppermute | solution.py:281
  14.4 2.8 %collective-permute-done.3.refs_5_.peer_ref = f32[64,256]{1,0:T(8,128)S(1)} collective-permute-done((f32[64,256]{1,0:T(8,128)S(1)}, f32[64,256]{1,0:T(8,128)S(1)}, u32[]{:S(2)}, u32[]{:S(2)}) %collective-permute-start.3) | collective-permute-done | bytes 65568 | tf_op jit(solution)/shard_map/ppermute | solution.py:281
  17.2 0.0 collective-permute-done.refs_1_
  17.2 0.0 collective-permute-done.2.refs_3_
  17.2 0.5 %shard_map.104.msg_ref.own_ref = f32[264,128]{1,0:T(8,128)S(1)} custom-call(f32[264,128]{1,0:T(8,128)S(1)} %get-tuple-element.27.refs_0_, f32[264,128]{1,0:T(8,128)S(1)} %collective-permute-done.refs_1_, f32[264,128]{1,0:T(8,128)S(1)} %collective-permute-done.1.refs_2_, f32[264,128]{1,0:T(8,128)S(1)} %collective-permute-done.2.refs_3_, ...), custom_call_target="tpu_custom_call" | custom-call | flops 500000000 | bytes 100000 | tf_op jit(solution)/shard_map/pallas_call | solution.py:269
  17.7 1.8 %collective-permute-start.4 = (f32[264,128]{1,0:T(8,128)S(1)}, f32[264,128]{1,0:T(8,128)S(1)}, u32[]{:S(2)}, u32[]{:S(2)}) collective-permute-start(f32[264,128]{1,0:T(8,128)S(1)} %shard_map.104.msg_ref.own_ref), channel_id=1, source_target_pairs={{0,1},{1,0},{2,3},{3,2},{4,5},{5,4},{6,7},{7,6},{8,9},{9,8},{10,11... | collective-permute-start | bytes 405512 | tf_op jit(solution)/shard_map/ppermute | solution.py:281
  19.4 0.0 collective-permute-start.8
  19.4 1.5 %collective-permute-start.9 = (f32[256,128]{1,0:T(8,128)S(1)}, f32[256,128]{1,0:T(8,128)S(1)}, u32[]{:S(2)}, u32[]{:S(2)}) collective-permute-start(f32[256,128]{1,0:T(8,128)S(1)} %get-tuple-element.47), channel_id=1, source_target_pairs={{0,16},{8,24},{16,0},{24,8},{1,17},{9,25},{17,1},{25,9},{2,18},{10... | collective-permute-start | bytes 393224 | tf_op jit(solution)/shard_map/ppermute | solution.py:281
  21.0 0.3 %collective-permute-start.10 = (f32[256,128]{1,0:T(8,128)S(1)}, f32[256,128]{1,0:T(8,128)S(1)}, u32[]{:S(2)}, u32[]{:S(2)}) collective-permute-start(f32[256,128]{1,0:T(8,128)S(1)} %get-tuple-element.48), channel_id=1, source_target_pairs={{0,24},{8,16},{16,8},{24,0},{1,25},{9,17},{17,9},{25,1},{2,26},{10... | collective-permute-start | bytes 393224 | tf_op jit(solution)/shard_map/ppermute | solution.py:281
  21.3 0.8 %shard_map.105 = (f32[768,128]{1,0:T(8,128)S(1)}, bf16[512,768]{1,0:T(8,128)(2,1)S(1)}, bf16[768,256]{1,0:T(8,128)(2,1)S(1)}, bf16[768,256]{1,0:T(8,128)(2,1)S(1)}) custom-call(f32[264,128]{1,0:T(8,128)S(1)} %shard_map.104.msg_ref.own_ref, f32[64,256]{1,0:T(8,128)S(1)} %get-tuple-element.29.fact_ref, f32[64,256]{1,0:T(8,128)S(1)} %collective-permute-done.3.refs_5_.peer_ref, ...), custom_call_target="tpu_custom_call" | custom-call | flops 500000000 | bytes 100000 | tf_op jit(solution)/shard_map/pallas_call | solution.py:269
  22.1 0.8 %collective-permute-done.4.msg_ref = f32[264,128]{1,0:T(8,128)S(1)} collective-permute-done((f32[264,128]{1,0:T(8,128)S(1)}, f32[264,128]{1,0:T(8,128)S(1)}, u32[]{:S(2)}, u32[]{:S(2)}) %collective-permute-start.4) | collective-permute-done | bytes 135200 | tf_op jit(solution)/shard_map/ppermute | solution.py:281
  22.9 0.7 %shard_map.106 = (f32[136,128]{1,0:T(8,128)S(1)}, f32[136,128]{1,0:T(8,128)S(1)}, f32[136,128]{1,0:T(8,128)S(1)}, f32[136,128]{1,0:T(8,128)S(1)}) custom-call(f32[264,128]{1,0:T(8,128)S(1)} %collective-permute-done.4.msg_ref, bf16[768,256]{1,0:T(8,128)(2,1)S(1)} %get-tuple-element.31.high_ref, bf16[768,256]{1,0:T(8,128)(2,1)S(1)} %get-tuple-element.32.low_ref, ...), custom_call_target="tpu_custom_call" | custom-call | flops 500000000 | bytes 100000 | tf_op jit(solution)/shard_map/pallas_call | solution.py:269
  23.5 2.9 %collective-permute-start.5 = (f32[136,128]{1,0:T(8,128)S(1)}, f32[136,128]{1,0:T(8,128)S(1)}, u32[]{:S(2)}, u32[]{:S(2)}) collective-permute-start(f32[136,128]{1,0:T(8,128)S(1)} %get-tuple-element.40), channel_id=1, source_target_pairs={{0,4},{1,5},{2,6},{3,7},{4,0},{5,1},{6,2},{7,3},{8,12},{9,13},{10,... | collective-permute-start | bytes 208904 | tf_op jit(solution)/shard_map/ppermute | solution.py:281
  26.4 1.4 %collective-permute-start.6 = (f32[136,128]{1,0:T(8,128)S(1)}, f32[136,128]{1,0:T(8,128)S(1)}, u32[]{:S(2)}, u32[]{:S(2)}) collective-permute-start(f32[136,128]{1,0:T(8,128)S(1)} %get-tuple-element.41), channel_id=1, source_target_pairs={{0,6},{1,7},{2,4},{3,5},{4,2},{5,3},{6,0},{7,1},{8,14},{9,15},{10,... | collective-permute-start | bytes 208904 | tf_op jit(solution)/shard_map/ppermute | solution.py:281
  27.8 0.0 collective-permute-done.8.refs_5_
  27.8 0.2 collective-permute-start.7
  28.0 0.0 collective-permute-done.9.refs_6_
  28.0 0.0 collective-permute-done.10.refs_7_
  28.0 2.6 %shard_map.108 = f32[256,256]{1,0:T(8,128)} custom-call(f32[264,128]{1,0:T(8,128)S(1)} %get-tuple-element.27.refs_0_, f32[264,128]{1,0:T(8,128)S(1)} %collective-permute-done.refs_1_, f32[264,128]{1,0:T(8,128)S(1)} %collective-permute-done.1.refs_2_, f32[264,128]{1,0:T(8,128)S(1)} %collective-permute-done.2.refs_3_, ...), custom_call_target="tpu_custom_call" | custom-call | flops 2000000000 | bytes 100000 | tf_op jit(solution)/shard_map/pallas_call | solution.py:269
  30.6 0.0 collective-permute-done.5.refs_1_
  30.6 2.0 %collective-permute-done.6.refs_2_ = f32[136,128]{1,0:T(8,128)S(1)} collective-permute-done((f32[136,128]{1,0:T(8,128)S(1)}, f32[136,128]{1,0:T(8,128)S(1)}, u32[]{:S(2)}, u32[]{:S(2)}) %collective-permute-start.6) | collective-permute-done | bytes 69664 | tf_op jit(solution)/shard_map/ppermute | solution.py:281
  32.6 0.2 collective-permute-done.7.refs_3_
  32.8 1.2 %shard_map.107 = (f32[1,128]{1,0:T(1,128)}, f32[128,2048]{1,0:T(8,128)}) custom-call(bf16[128,2048]{1,0:T(8,128)(2,1)S(1)} %get-tuple-element.26.member_ref, f32[136,128]{1,0:T(8,128)S(1)} %get-tuple-element.39.refs_0_, f32[136,128]{1,0:T(8,128)S(1)} %collective-permute-done.5.refs_1_, f32[136,128]{1,0:T(8,128)S(1)} %collective-permute-done.6.refs_2_, ...), custom_call_target="tpu_custom_call" | custom-call | flops 500000000 | bytes 100000 | tf_op jit(solution)/shard_map/pallas_call | solution.py:269
Async XLA Ops:
  6.0 6.7 %collective-permute-start.1 = (f32[264,128]{1,0:T(8,128)S(1)}, f32[264,128]{1,0:T(8,128)S(1)}, u32[]{:S(2)}, u32[]{:S(2)}) collective-permute-start(f32[264,128]{1,0:T(8,128)S(1)} %get-tuple-element.27.refs_0_), channel_id=1, source_target_pairs={{0,16},{8,24},{16,0},{24,8},{1,17},{9,25},{17,1},{25,9},{2,18},{10... | collective-permute-start | bytes 405512 | tf_op jit(solution)/shard_map/ppermute | solution.py:281
  9.1 8.1 %collective-permute-start = (f32[264,128]{1,0:T(8,128)S(1)}, f32[264,128]{1,0:T(8,128)S(1)}, u32[]{:S(2)}, u32[]{:S(2)}) collective-permute-start(f32[264,128]{1,0:T(8,128)S(1)} %get-tuple-element.27.refs_0_), channel_id=1, source_target_pairs={{0,8},{8,0},{16,24},{24,16},{1,9},{9,1},{17,25},{25,17},{2,10},{10... | collective-permute-start | bytes 405512 | tf_op jit(solution)/shard_map/ppermute | solution.py:281
  12.7 4.5 %collective-permute-start.2 = (f32[264,128]{1,0:T(8,128)S(1)}, f32[264,128]{1,0:T(8,128)S(1)}, u32[]{:S(2)}, u32[]{:S(2)}) collective-permute-start(f32[264,128]{1,0:T(8,128)S(1)} %collective-permute-done.1.refs_2_), channel_id=1, source_target_pairs={{0,8},{8,0},{16,24},{24,16},{1,9},{9,1},{17,25},{25,17},{2,10},{10... | collective-permute-start | bytes 405512 | tf_op jit(solution)/shard_map/ppermute | solution.py:281
  12.7 4.5 %collective-permute-start.3 = (f32[64,256]{1,0:T(8,128)S(1)}, f32[64,256]{1,0:T(8,128)S(1)}, u32[]{:S(2)}, u32[]{:S(2)}) collective-permute-start(f32[64,256]{1,0:T(8,128)S(1)} %get-tuple-element.29.fact_ref), channel_id=1, source_target_pairs={{0,1},{1,0},{2,3},{3,2},{4,5},{5,4},{6,7},{7,6},{8,9},{9,8},{10,11... | collective-permute-start | bytes 196616 | tf_op jit(solution)/shard_map/ppermute | solution.py:281
  17.7 5.2 %collective-permute-start.4 = (f32[264,128]{1,0:T(8,128)S(1)}, f32[264,128]{1,0:T(8,128)S(1)}, u32[]{:S(2)}, u32[]{:S(2)}) collective-permute-start(f32[264,128]{1,0:T(8,128)S(1)} %shard_map.104.msg_ref.own_ref), channel_id=1, source_target_pairs={{0,1},{1,0},{2,3},{3,2},{4,5},{5,4},{6,7},{7,6},{8,9},{9,8},{10,11... | collective-permute-start | bytes 405512 | tf_op jit(solution)/shard_map/ppermute | solution.py:281
  19.4 8.3 %collective-permute-start.8 = (f32[256,128]{1,0:T(8,128)S(1)}, f32[256,128]{1,0:T(8,128)S(1)}, u32[]{:S(2)}, u32[]{:S(2)}) collective-permute-start(f32[256,128]{1,0:T(8,128)S(1)} %get-tuple-element.46), channel_id=1, source_target_pairs={{0,8},{8,0},{16,24},{24,16},{1,9},{9,1},{17,25},{25,17},{2,10},{10... | collective-permute-start | bytes 393224 | tf_op jit(solution)/shard_map/ppermute | solution.py:281
  19.4 8.6 %collective-permute-start.9 = (f32[256,128]{1,0:T(8,128)S(1)}, f32[256,128]{1,0:T(8,128)S(1)}, u32[]{:S(2)}, u32[]{:S(2)}) collective-permute-start(f32[256,128]{1,0:T(8,128)S(1)} %get-tuple-element.47), channel_id=1, source_target_pairs={{0,16},{8,24},{16,0},{24,8},{1,17},{9,25},{17,1},{25,9},{2,18},{10... | collective-permute-start | bytes 393224 | tf_op jit(solution)/shard_map/ppermute | solution.py:281
  21.0 7.0 %collective-permute-start.10 = (f32[256,128]{1,0:T(8,128)S(1)}, f32[256,128]{1,0:T(8,128)S(1)}, u32[]{:S(2)}, u32[]{:S(2)}) collective-permute-start(f32[256,128]{1,0:T(8,128)S(1)} %get-tuple-element.48), channel_id=1, source_target_pairs={{0,24},{8,16},{16,8},{24,0},{1,25},{9,17},{17,9},{25,1},{2,26},{10... | collective-permute-start | bytes 393224 | tf_op jit(solution)/shard_map/ppermute | solution.py:281
  23.5 7.1 %collective-permute-start.5 = (f32[136,128]{1,0:T(8,128)S(1)}, f32[136,128]{1,0:T(8,128)S(1)}, u32[]{:S(2)}, u32[]{:S(2)}) collective-permute-start(f32[136,128]{1,0:T(8,128)S(1)} %get-tuple-element.40), channel_id=1, source_target_pairs={{0,4},{1,5},{2,6},{3,7},{4,0},{5,1},{6,2},{7,3},{8,12},{9,13},{10,... | collective-permute-start | bytes 208904 | tf_op jit(solution)/shard_map/ppermute | solution.py:281
  26.4 6.2 %collective-permute-start.6 = (f32[136,128]{1,0:T(8,128)S(1)}, f32[136,128]{1,0:T(8,128)S(1)}, u32[]{:S(2)}, u32[]{:S(2)}) collective-permute-start(f32[136,128]{1,0:T(8,128)S(1)} %get-tuple-element.41), channel_id=1, source_target_pairs={{0,6},{1,7},{2,4},{3,5},{4,2},{5,3},{6,0},{7,1},{8,14},{9,15},{10,... | collective-permute-start | bytes 208904 | tf_op jit(solution)/shard_map/ppermute | solution.py:281
  27.8 5.1 %collective-permute-start.7 = (f32[136,128]{1,0:T(8,128)S(1)}, f32[136,128]{1,0:T(8,128)S(1)}, u32[]{:S(2)}, u32[]{:S(2)}) collective-permute-start(f32[136,128]{1,0:T(8,128)S(1)} %get-tuple-element.42), channel_id=1, source_target_pairs={{0,2},{1,3},{2,0},{3,1},{4,6},{5,7},{6,4},{7,5},{8,10},{9,11},{10,... | collective-permute-start | bytes 208904 | tf_op jit(solution)/shard_map/ppermute | solution.py:281

commit v6 on v5

--- a/solution.py
+++ b/solution.py
@@ -137,7 +137,8 @@
         highs, lows = [], []
         for step in group:
             coef_high, coef_low = split(coef_buf[step])
-            folded = nn(coef_high, turned_member) + nn(coef_low, turned_member)
+            both = nn(jnp.concatenate([coef_high, coef_low], axis=0), turned_member)
+            folded = both[:BLOCK] + both[BLOCK:]
             folded_refs[step // per][pl.ds((step % per) * BLOCK, BLOCK), :] = folded
             high, low = split(folded)
             highs.append(high)
@@ -168,51 +169,65 @@
     return info[0:1, :], info[1:2, :], info[2:3, :]
 
 
-def second_kernel(n_trade, *refs):
-    blocks, (side_ref, _, msg_ref) = refs[:n_trade], refs[n_trade:]
+def net_kernel(n_blocks, *refs):
+    blocks, own_ref, *total, out_ref = refs[:n_blocks], *refs[n_blocks:]
     trade = lax.axis_index("trade")
-    scen, sets = blocks[0].shape[0] - INFO, blocks[0].shape[1]
+    sets = own_ref.shape[1]
     (high, low), columns = blocks_of(blocks)
-    party, thr, wgt = info_of(blocks[0])
+    party, _, _ = info_of(own_ref)
     mine = (iota((1, sets), 1) + trade * sets).astype(f32)
     right = jnp.concatenate([same_as(columns, party), same_as(columns, mine)], axis=1)
     netted = nn(high, right) + nn(low, right)
-    msg_ref[:scen, :] = wgt * jax.nn.sigmoid(netted[:, :sets] - thr)
-    soft = jax.nn.softplus(netted[:, sets:] - side_ref[0:1, :])
+    out_ref[...] = total[0][...] + netted if total else netted
+
+
+def second_kernel(n_blocks, *refs):
+    *ins, side_ref, _, msg_ref, net_ref = refs
+    net_kernel(n_blocks, *ins, net_ref)
+    own_ref = ins[n_blocks]
+    scen, sets = own_ref.shape[0] - INFO, own_ref.shape[1]
+    _, thr, wgt = info_of(own_ref)
+    msg_ref[:scen, :] = wgt * jax.nn.sigmoid(net_ref[:, :sets] - thr)
+    soft = jax.nn.softplus(net_ref[:, sets:] - side_ref[0:1, :])
     msg_ref[scen:, :] = jnp.broadcast_to(
         jnp.sum(soft, axis=0, keepdims=True) * side_ref[1:2, :], (INFO, sets)
     )
 
 
-def response(table, msg_ref):
-    return pair_nn(table, split(msg_ref[: msg_ref.shape[0] - INFO, :]))
-
-
-def middle_kernel(n_scen, msg_ref, fact_ref, peer_ref, key_ref, grid_ref, chosen_ref, high_ref, low_ref, column_ref):
+def choose_kernel(n_scen, key_ref, chosen_ref, column_ref):
     me = lax.axis_index("scen")
     lines = key_ref.shape[0]
     chunk = lines * BLOCK // n_scen
     for i in range(lines):
         column_ref[i * BLOCK : (i + 1) * BLOCK, :] = column(key_ref[i : i + 1, :])
-    rows = grid_ref.shape[0]
     for j in range(n_scen // 2):
         here = column_ref[pl.ds(pl.multiple_of((me ^ (2 * j)) * chunk, chunk), chunk), :].astype(jnp.int32)
-        for i in range(rows // BLOCK):
+        for i in range(chosen_ref.shape[1] // BLOCK):
             chosen_ref[j * chunk : (j + 1) * chunk, i * BLOCK : (i + 1) * BLOCK] = one_hot(
                 here == iota(here.shape, 1) + i * BLOCK
             )
-    grid_ref[...] = response(split(basis(fact_ref[...])), msg_ref)
-    high_ref[...], low_ref[...] = split(basis(peer_ref[...]))
-
-
-def third_kernel(msg_ref, high_ref, low_ref, own_ref, grid_ref, chosen_ref, *chunk_refs):
-    chunk = chosen_ref.shape[0] // len(chunk_refs)
-    both = jnp.concatenate(split(grid_ref[...] + response((high_ref[...], low_ref[...]), msg_ref)), axis=1)
-    scen, sets = msg_ref.shape[0] - INFO, msg_ref.shape[1]
+
+
+def middle_kernel(msg_ref, fact_ref, peer_ref, chosen_ref, part_ref, high_ref, low_ref):
+    adj = split(msg_ref[: msg_ref.shape[0] - INFO, :])
+    sets = msg_ref.shape[1]
+    chosen = chosen_ref[...]
+    grid = pair_nn(split(basis(fact_ref[...])), adj)
+    part = nn(chosen, jnp.concatenate(split(grid), axis=1))
+    part_ref[...] = part[:, :sets] + part[:, sets:]
+    high, low = split(basis(peer_ref[...]))
+    high_ref[...] = nn(chosen, high).astype(bf16)
+    low_ref[...] = nn(chosen, low).astype(bf16)
+
+
+def third_kernel(msg_ref, own_ref, part_ref, high_ref, low_ref, *chunk_refs):
+    chunk = part_ref.shape[0] // len(chunk_refs)
+    scen = msg_ref.shape[0] - INFO
+    adj = split(msg_ref[:scen, :])
     xva = msg_ref[scen:, :] + own_ref[scen:, :]
     for j, ref in enumerate(chunk_refs):
-        part = nn(chosen_ref[j * chunk : (j + 1) * chunk, :], both)
-        ref[:chunk, :] = part[:, :sets] + part[:, sets:]
+        rows = slice(j * chunk, (j + 1) * chunk)
+        ref[:chunk, :] = part_ref[rows, :] + pair_nn((high_ref[rows, :], low_ref[rows, :]), adj)
         ref[chunk:, :] = xva
 
 
@@ -330,20 +345,38 @@
     for k in range(2, n_trade, 2):
         blocks[k + 1] = send(blocks[k], "trade", 1)
     peer_fact = send(fact, "scen", 1)
+    (chosen,) = call(
+        functools.partial(choose_kernel, n_scen),
+        [vmem((width // 2, grid), bf16)],
+        [VMEM],
+        [key],
+        [vmem((width, BLOCK), f32)],
+        limit=8 << 20,
+    )
+    total = []
+    for here in (blocks[:2], blocks[2::2]):
+        total = call(
+            functools.partial(net_kernel, len(here)),
+            [vmem((scen, 2 * sets), f32)],
+            [VMEM] * (len(here) + 1 + len(total)),
+            [*here, expo, *total],
+            limit=8 << 20,
+        )
+    here = blocks[3::2]
     (msg,) = call(
-        functools.partial(second_kernel, n_trade),
+        functools.partial(second_kernel, len(here)),
         [vmem((scen + INFO, sets), f32)],
-        [VMEM] * (n_trade + 2),
-        [*blocks, side, peer_fact],
+        [VMEM] * (len(here) + 4),
+        [*here, expo, *total, side, peer_fact],
+        [vmem((scen, 2 * sets), f32)],
         limit=8 << 20,
     )
     peer = send(msg, "scen", 1)
-    half, chosen, *peer_table = call(
-        functools.partial(middle_kernel, n_scen),
-        [vmem((grid, sets), f32), vmem((width // 2, grid), bf16)] + [vmem((grid, scen), bf16)] * 2,
+    middle = call(
+        middle_kernel,
+        [vmem((width // 2, sets), f32)] + [vmem((width // 2, scen), bf16)] * 2,
         [VMEM] * 4,
-        [msg, fact, peer_fact, key],
-        [vmem((width, BLOCK), f32)],
+        [msg, fact, peer_fact, chosen],
         limit=8 << 20,
     )
     msg, *later = lax.optimization_barrier((msg, *folded[1:]))
@@ -351,8 +384,8 @@
     chunks = call(
         third_kernel,
         [vmem((chunk + INFO, sets), f32)] * (n_scen // 2),
-        [VMEM] * 6,
-        [peer, *peer_table, msg, half, chosen],
+        [VMEM] * 5,
+        [peer, msg, *middle],
         limit=8 << 20,
     )
     chunks = [chunks[0]] + [

time: 34.2 us -> 33.9 us (level)
  waiting for transfers between devices: 9.39 us -> 7.96 us
  Pallas kernels: 11.1 us -> 12.2 us
    ppermute x11, waiting for transfers between devices: 9.39 us -> 7.96 us  [send(): lax.ppermute(value, axis, [(i, i ^ k) for i in range(lax.axis_size(axis))])]
    pallas_call x6 -> x9, Pallas kernels: 11.1 us -> 12.2 us  [call(): pl.pallas_call(kernel, out_shape=out_shape, in_specs=in_specs, out_specs=...]
  transfers between devices with their start and end apart: 11 -> 11, of which waited for: 5 -> 6; matrix products, arithmetic and copies ran while one was open for 0% -> 0% of each run, Pallas kernels for 12% -> 16%
where the time goes in v6:
time: 33.9 us; the launch traced here: 33.8 us
  starting transfers between devices  12.9 us (38%)
  Pallas kernels  12.2 us (36%)
  waiting for transfers between devices  7.96 us (23%)
  between operations  0.71 us (2%)
    ppermute x11, starting transfers between devices, send(): lax.ppermute(value, axis, [(i, i ^ k) for i in range(lax.axis_size(axis))])  12.9 us
    pallas_call x9, Pallas kernels, call(): pl.pallas_call(kernel, out_shape=out_shape, in_specs=in_specs, out_specs=...  12.2 us
    ppermute x11, waiting for transfers between devices, send(): lax.ppermute(value, axis, [(i, i ^ k) for i in range(lax.axis_size(axis))])  7.96 us
  transfers between devices with their start and end apart: 11, of which 6 were waited for; matrix products, arithmetic and copies ran while one was open for 0% of the time, Pallas kernels for 16%

profile of v6, /device:TPU:0, one launch (start us, length us, event | category | flops | bytes accessed | tf_op | source)
XLA Modules:
  0.0 33.8 jit_solution(6983450134516073512)
XLA Ops:
  0.6 5.3 %shard_map.103 = (f32[256,128]{1,0:T(8,128)S(1)}, f32[256,128]{1,0:T(8,128)S(1)}, f32[256,128]{1,0:T(8,128)S(1)}, f32[256,128]{1,0:T(8,128)S(1)}, f32[264,128]{1...) custom-call(f32[64,256]{1,0:T(8,128)} %bitcast.8, ...), custom_call_target="tpu_custom_call" | custom-call | flops 500000000 | bytes 100000 | tf_op jit(solution)/shard_map/pallas_call | solution.py:284
  6.0 3.1 %collective-permute-start = (f32[264,128]{1,0:T(8,128)S(1)}, f32[264,128]{1,0:T(8,128)S(1)}, u32[]{:S(2)}, u32[]{:S(2)}) collective-permute-start(f32[264,128]{1,0:T(8,128)S(1)} %get-tuple-element.26.refs_0_.refs_2_.refs_1_), channel_id=1, source_target_pairs={{0,16},{8,24},{16,0},{24,8},{1,17},{9,25},{17,1},{25,9},{2,18},{10... | collective-permute-start | bytes 405512 | tf_op jit(solution)/shard_map/ppermute | solution.py:296
  9.0 0.0 collective-permute-start.2
  9.0 3.6 %collective-permute-done.refs_0_.refs_2_ = f32[264,128]{1,0:T(8,128)S(1)} collective-permute-done((f32[264,128]{1,0:T(8,128)S(1)}, f32[264,128]{1,0:T(8,128)S(1)}, u32[]{:S(2)}, u32[]{:S(2)}) %collective-permute-start) | collective-permute-done | bytes 135200 | tf_op jit(solution)/shard_map/ppermute | solution.py:296
  12.6 0.0 collective-permute-start.1
  12.6 1.7 %collective-permute-start.3 = (f32[64,256]{1,0:T(8,128)S(1)}, f32[64,256]{1,0:T(8,128)S(1)}, u32[]{:S(2)}, u32[]{:S(2)}) collective-permute-start(f32[64,256]{1,0:T(8,128)S(1)} %get-tuple-element.28.fact_ref), channel_id=1, source_target_pairs={{0,1},{1,0},{2,3},{3,2},{4,5},{5,4},{6,7},{7,6},{8,9},{9,8},{10,11... | collective-permute-start | bytes 196616 | tf_op jit(solution)/shard_map/ppermute | solution.py:296
  14.3 0.0 collective-permute-done.2.refs_1_
  14.3 0.3 shard_map.104.refs_2_
  14.7 0.3 shard_map.105.refs_2_
  15.0 2.2 %collective-permute-done.3.refs_4_.peer_ref = f32[64,256]{1,0:T(8,128)S(1)} collective-permute-done((f32[64,256]{1,0:T(8,128)S(1)}, f32[64,256]{1,0:T(8,128)S(1)}, u32[]{:S(2)}, u32[]{:S(2)}) %collective-permute-start.3) | collective-permute-done | bytes 65568 | tf_op jit(solution)/shard_map/ppermute | solution.py:296
  17.1 0.0 collective-permute-done.1.refs_0_.refs_3_
  17.1 0.4 %shard_map.106.msg_ref.own_ref = f32[264,128]{1,0:T(8,128)S(1)} custom-call(f32[264,128]{1,0:T(8,128)S(1)} %collective-permute-done.1.refs_0_.refs_3_, f32[264,128]{1,0:T(8,128)S(1)} %get-tuple-element.26.refs_0_.refs_2_.refs_1_, f32[256,256]{1,0:T(8,128)S(1)} %shard_map.105.refs_2_, f32[8,128]{1,0:T(8,128)S(1)} %get-tuple-element.27.refs_3_, ...), custom_call_target="tpu_custom_call" | custom-call | flops 500000000 | bytes 100000 | tf_op jit(solution)/shard_map/pallas_call | solution.py:284
  17.5 1.8 %collective-permute-start.4 = (f32[264,128]{1,0:T(8,128)S(1)}, f32[264,128]{1,0:T(8,128)S(1)}, u32[]{:S(2)}, u32[]{:S(2)}) collective-permute-start(f32[264,128]{1,0:T(8,128)S(1)} %shard_map.106.msg_ref.own_ref), channel_id=1, source_target_pairs={{0,1},{1,0},{2,3},{3,2},{4,5},{5,4},{6,7},{7,6},{8,9},{9,8},{10,11... | collective-permute-start | bytes 405512 | tf_op jit(solution)/shard_map/ppermute | solution.py:296
  19.3 0.5 %collective-permute-start.10 = (f32[256,128]{1,0:T(8,128)S(1)}, f32[256,128]{1,0:T(8,128)S(1)}, u32[]{:S(2)}, u32[]{:S(2)}) collective-permute-start(f32[256,128]{1,0:T(8,128)S(1)} %get-tuple-element.46), channel_id=1, source_target_pairs={{0,24},{8,16},{16,8},{24,0},{1,25},{9,17},{17,9},{25,1},{2,26},{10... | collective-permute-start | bytes 393224 | tf_op jit(solution)/shard_map/ppermute | solution.py:296
  19.8 1.1 %collective-permute-start.8 = (f32[256,128]{1,0:T(8,128)S(1)}, f32[256,128]{1,0:T(8,128)S(1)}, u32[]{:S(2)}, u32[]{:S(2)}) collective-permute-start(f32[256,128]{1,0:T(8,128)S(1)} %get-tuple-element.44), channel_id=1, source_target_pairs={{0,8},{8,0},{16,24},{24,16},{1,9},{9,1},{17,25},{25,17},{2,10},{10... | collective-permute-start | bytes 393224 | tf_op jit(solution)/shard_map/ppermute | solution.py:296
  20.9 0.5 %collective-permute-start.9 = (f32[256,128]{1,0:T(8,128)S(1)}, f32[256,128]{1,0:T(8,128)S(1)}, u32[]{:S(2)}, u32[]{:S(2)}) collective-permute-start(f32[256,128]{1,0:T(8,128)S(1)} %get-tuple-element.45), channel_id=1, source_target_pairs={{0,16},{8,24},{16,0},{24,8},{1,17},{9,25},{17,1},{25,9},{2,18},{10... | collective-permute-start | bytes 393224 | tf_op jit(solution)/shard_map/ppermute | solution.py:296
  21.4 0.4 %shard_map.107.chosen_ref = bf16[512,768]{1,0:T(8,128)(2,1)S(1)} custom-call(s32[8,128]{1,0:T(8,128)S(1)} %get-tuple-element.33.key_ref), custom_call_target="tpu_custom_call" | custom-call | flops 500000000 | bytes 100000 | tf_op jit(solution)/shard_map/pallas_call | solution.py:284
  21.8 1.4 %shard_map.108 = (f32[512,128]{1,0:T(8,128)S(1)}, bf16[512,256]{1,0:T(8,128)(2,1)S(1)}, bf16[512,256]{1,0:T(8,128)(2,1)S(1)}) custom-call(f32[264,128]{1,0:T(8,128)S(1)} %shard_map.106.msg_ref.own_ref, f32[64,256]{1,0:T(8,128)S(1)} %get-tuple-element.28.fact_ref, f32[64,256]{1,0:T(8,128)S(1)} %collective-permute-done.3.refs_4_.peer_ref, ...), custom_call_target="tpu_custom_call" | custom-call | flops 500000000 | bytes 100000 | tf_op jit(solution)/shard_map/pallas_call | solution.py:284
  23.2 0.0 collective-permute-done.4.msg_ref
  23.2 0.3 shard_map.109
  23.5 2.6 %collective-permute-start.5 = (f32[136,128]{1,0:T(8,128)S(1)}, f32[136,128]{1,0:T(8,128)S(1)}, u32[]{:S(2)}, u32[]{:S(2)}) collective-permute-start(f32[136,128]{1,0:T(8,128)S(1)} %get-tuple-element.38), channel_id=1, source_target_pairs={{0,4},{1,5},{2,6},{3,7},{4,0},{5,1},{6,2},{7,3},{8,12},{9,13},{10,... | collective-permute-start | bytes 208904 | tf_op jit(solution)/shard_map/ppermute | solution.py:296
  26.1 1.3 %collective-permute-start.6 = (f32[136,128]{1,0:T(8,128)S(1)}, f32[136,128]{1,0:T(8,128)S(1)}, u32[]{:S(2)}, u32[]{:S(2)}) collective-permute-start(f32[136,128]{1,0:T(8,128)S(1)} %get-tuple-element.39), channel_id=1, source_target_pairs={{0,6},{1,7},{2,4},{3,5},{4,2},{5,3},{6,0},{7,1},{8,14},{9,15},{10,... | collective-permute-start | bytes 208904 | tf_op jit(solution)/shard_map/ppermute | solution.py:296
  27.5 0.0 collective-permute-done.10.refs_7_
  27.5 0.2 collective-permute-start.7
  27.7 0.0 collective-permute-done.8.refs_5_
  27.7 0.1 collective-permute-done.9.refs_6_
  27.9 2.6 %shard_map.111 = f32[256,256]{1,0:T(8,128)} custom-call(f32[264,128]{1,0:T(8,128)S(1)} %get-tuple-element.26.refs_0_.refs_2_.refs_1_, f32[264,128]{1,0:T(8,128)S(1)} %collective-permute-done.2.refs_1_, f32[264,128]{1,0:T(8,128)S(1)} %collective-permute-done.refs_0_.refs_2_, f32[264,128]{1,0:T(8,128)S(1)} %collective-permute-done.1.refs_0_.refs_3_, ...), custom_call_target="tpu_custom_call" | custom-call | flops 2000000000 | bytes 100000 | tf_op jit(solution)/shard_map/pallas_call | solution.py:284
  30.5 0.5 %collective-permute-done.5.refs_1_ = f32[136,128]{1,0:T(8,128)S(1)} collective-permute-done((f32[136,128]{1,0:T(8,128)S(1)}, f32[136,128]{1,0:T(8,128)S(1)}, u32[]{:S(2)}, u32[]{:S(2)}) %collective-permute-start.5) | collective-permute-done | bytes 69664 | tf_op jit(solution)/shard_map/ppermute | solution.py:296
  31.0 1.3 %collective-permute-done.6.refs_2_ = f32[136,128]{1,0:T(8,128)S(1)} collective-permute-done((f32[136,128]{1,0:T(8,128)S(1)}, f32[136,128]{1,0:T(8,128)S(1)}, u32[]{:S(2)}, u32[]{:S(2)}) %collective-permute-start.6) | collective-permute-done | bytes 69664 | tf_op jit(solution)/shard_map/ppermute | solution.py:296
  32.4 0.2 collective-permute-done.7.refs_3_
  32.6 1.2 %shard_map.110 = (f32[1,128]{1,0:T(1,128)}, f32[128,2048]{1,0:T(8,128)}) custom-call(bf16[128,2048]{1,0:T(8,128)(2,1)S(1)} %get-tuple-element.25.member_ref, f32[136,128]{1,0:T(8,128)S(1)} %get-tuple-element.37.refs_0_, f32[136,128]{1,0:T(8,128)S(1)} %collective-permute-done.5.refs_1_, f32[136,128]{1,0:T(8,128)S(1)} %collective-permute-done.6.refs_2_, ...), custom_call_target="tpu_custom_call" | custom-call | flops 500000000 | bytes 100000 | tf_op jit(solution)/shard_map/pallas_call | solution.py:284
Async XLA Ops:
  6.0 6.6 %collective-permute-start = (f32[264,128]{1,0:T(8,128)S(1)}, f32[264,128]{1,0:T(8,128)S(1)}, u32[]{:S(2)}, u32[]{:S(2)}) collective-permute-start(f32[264,128]{1,0:T(8,128)S(1)} %get-tuple-element.26.refs_0_.refs_2_.refs_1_), channel_id=1, source_target_pairs={{0,16},{8,24},{16,0},{24,8},{1,17},{9,25},{17,1},{25,9},{2,18},{10... | collective-permute-start | bytes 405512 | tf_op jit(solution)/shard_map/ppermute | solution.py:296
  9.0 5.3 %collective-permute-start.2 = (f32[264,128]{1,0:T(8,128)S(1)}, f32[264,128]{1,0:T(8,128)S(1)}, u32[]{:S(2)}, u32[]{:S(2)}) collective-permute-start(f32[264,128]{1,0:T(8,128)S(1)} %get-tuple-element.26.refs_0_.refs_2_.refs_1_), channel_id=1, source_target_pairs={{0,8},{8,0},{16,24},{24,16},{1,9},{9,1},{17,25},{25,17},{2,10},{10... | collective-permute-start | bytes 405512 | tf_op jit(solution)/shard_map/ppermute | solution.py:296
  12.6 4.5 %collective-permute-start.1 = (f32[264,128]{1,0:T(8,128)S(1)}, f32[264,128]{1,0:T(8,128)S(1)}, u32[]{:S(2)}, u32[]{:S(2)}) collective-permute-start(f32[264,128]{1,0:T(8,128)S(1)} %collective-permute-done.refs_0_.refs_2_), channel_id=1, source_target_pairs={{0,8},{8,0},{16,24},{24,16},{1,9},{9,1},{17,25},{25,17},{2,10},{10... | collective-permute-start | bytes 405512 | tf_op jit(solution)/shard_map/ppermute | solution.py:296
  12.6 4.5 %collective-permute-start.3 = (f32[64,256]{1,0:T(8,128)S(1)}, f32[64,256]{1,0:T(8,128)S(1)}, u32[]{:S(2)}, u32[]{:S(2)}) collective-permute-start(f32[64,256]{1,0:T(8,128)S(1)} %get-tuple-element.28.fact_ref), channel_id=1, source_target_pairs={{0,1},{1,0},{2,3},{3,2},{4,5},{5,4},{6,7},{7,6},{8,9},{9,8},{10,11... | collective-permute-start | bytes 196616 | tf_op jit(solution)/shard_map/ppermute | solution.py:296
  17.5 5.7 %collective-permute-start.4 = (f32[264,128]{1,0:T(8,128)S(1)}, f32[264,128]{1,0:T(8,128)S(1)}, u32[]{:S(2)}, u32[]{:S(2)}) collective-permute-start(f32[264,128]{1,0:T(8,128)S(1)} %shard_map.106.msg_ref.own_ref), channel_id=1, source_target_pairs={{0,1},{1,0},{2,3},{3,2},{4,5},{5,4},{6,7},{7,6},{8,9},{9,8},{10,11... | collective-permute-start | bytes 405512 | tf_op jit(solution)/shard_map/ppermute | solution.py:296
  19.3 8.2 %collective-permute-start.10 = (f32[256,128]{1,0:T(8,128)S(1)}, f32[256,128]{1,0:T(8,128)S(1)}, u32[]{:S(2)}, u32[]{:S(2)}) collective-permute-start(f32[256,128]{1,0:T(8,128)S(1)} %get-tuple-element.46), channel_id=1, source_target_pairs={{0,24},{8,16},{16,8},{24,0},{1,25},{9,17},{17,9},{25,1},{2,26},{10... | collective-permute-start | bytes 393224 | tf_op jit(solution)/shard_map/ppermute | solution.py:296
  19.8 8.0 %collective-permute-start.8 = (f32[256,128]{1,0:T(8,128)S(1)}, f32[256,128]{1,0:T(8,128)S(1)}, u32[]{:S(2)}, u32[]{:S(2)}) collective-permute-start(f32[256,128]{1,0:T(8,128)S(1)} %get-tuple-element.44), channel_id=1, source_target_pairs={{0,8},{8,0},{16,24},{24,16},{1,9},{9,1},{17,25},{25,17},{2,10},{10... | collective-permute-start | bytes 393224 | tf_op jit(solution)/shard_map/ppermute | solution.py:296
  20.9 7.0 %collective-permute-start.9 = (f32[256,128]{1,0:T(8,128)S(1)}, f32[256,128]{1,0:T(8,128)S(1)}, u32[]{:S(2)}, u32[]{:S(2)}) collective-permute-start(f32[256,128]{1,0:T(8,128)S(1)} %get-tuple-element.45), channel_id=1, source_target_pairs={{0,16},{8,24},{16,0},{24,8},{1,17},{9,25},{17,1},{25,9},{2,18},{10... | collective-permute-start | bytes 393224 | tf_op jit(solution)/shard_map/ppermute | solution.py:296
  23.5 7.5 %collective-permute-start.5 = (f32[136,128]{1,0:T(8,128)S(1)}, f32[136,128]{1,0:T(8,128)S(1)}, u32[]{:S(2)}, u32[]{:S(2)}) collective-permute-start(f32[136,128]{1,0:T(8,128)S(1)} %get-tuple-element.38), channel_id=1, source_target_pairs={{0,4},{1,5},{2,6},{3,7},{4,0},{5,1},{6,2},{7,3},{8,12},{9,13},{10,... | collective-permute-start | bytes 208904 | tf_op jit(solution)/shard_map/ppermute | solution.py:296
  26.1 6.2 %collective-permute-start.6 = (f32[136,128]{1,0:T(8,128)S(1)}, f32[136,128]{1,0:T(8,128)S(1)}, u32[]{:S(2)}, u32[]{:S(2)}) collective-permute-start(f32[136,128]{1,0:T(8,128)S(1)} %get-tuple-element.39), channel_id=1, source_target_pairs={{0,6},{1,7},{2,4},{3,5},{4,2},{5,3},{6,0},{7,1},{8,14},{9,15},{10,... | collective-permute-start | bytes 208904 | tf_op jit(solution)/shard_map/ppermute | solution.py:296
  27.5 5.1 %collective-permute-start.7 = (f32[136,128]{1,0:T(8,128)S(1)}, f32[136,128]{1,0:T(8,128)S(1)}, u32[]{:S(2)}, u32[]{:S(2)}) collective-permute-start(f32[136,128]{1,0:T(8,128)S(1)} %get-tuple-element.40), channel_id=1, source_target_pairs={{0,2},{1,3},{2,0},{3,1},{4,6},{5,7},{6,4},{7,5},{8,10},{9,11},{10,... | collective-permute-start | bytes 208904 | tf_op jit(solution)/shard_map/ppermute | solution.py:296

commit v7 on v6

--- a/solution.py
+++ b/solution.py
@@ -379,18 +379,15 @@
         [msg, fact, peer_fact, chosen],
         limit=8 << 20,
     )
-    msg, *later = lax.optimization_barrier((msg, *folded[1:]))
+    msg, *later = lax.optimization_barrier((msg, *folded[2:]))
+    later = [folded[1], *later]
     moved = [folded[0]] + [send(later[k - 1], "trade", k) for k in range(1, n_trade)]
     chunks = call(
-        third_kernel,
-        [vmem((chunk + INFO, sets), f32)] * (n_scen // 2),
-        [VMEM] * 5,
-        [peer, msg, *middle],
-        limit=8 << 20,
+        third_kernel, [vmem((chunk + INFO, sets), f32)] * (n_scen // 2), [VMEM] * 5, [peer, msg, *middle], limit=8 << 20
     )
     chunks = [chunks[0]] + [
         send(chunks[j], "scen", 2 * j)
-        for j in [*range(n_scen // 4, n_scen // 2), *range(1, n_scen // 4)]
+        for j in [*range(n_scen // 2 - 1, n_scen // 4, -1), *range(1, n_scen // 4), *range(n_scen // 4, n_scen // 4 + 1)]
     ]
     (feature_sens,) = call(
         functools.partial(feature_kernel, n_trade),

time: 33.9 us -> 34.2 us (level)
  transfers between devices with their start and end apart: 11 -> 11, of which waited for: 6 -> 4; matrix products, arithmetic and copies ran while one was open for 0% -> 0% of each run, Pallas kernels for 16% -> 16%
where the time goes in v7:
time: 34.2 us; the launch traced here: 34 us
  starting transfers between devices  13.1 us (38%)
  Pallas kernels  12.2 us (36%)
  waiting for transfers between devices  7.97 us (23%)
  between operations  0.71 us (2%)
    ppermute x11, starting transfers between devices, send(): lax.ppermute(value, axis, [(i, i ^ k) for i in range(lax.axis_size(axis))])  13.1 us
    pallas_call x9, Pallas kernels, call(): pl.pallas_call(kernel, out_shape=out_shape, in_specs=in_specs, out_specs=...  12.2 us
    ppermute x11, waiting for transfers between devices, send(): lax.ppermute(value, axis, [(i, i ^ k) for i in range(lax.axis_size(axis))])  7.97 us
  transfers between devices with their start and end apart: 11, of which 4 were waited for; matrix products, arithmetic and copies ran while one was open for 0% of the time, Pallas kernels for 16%

profile of v7, /device:TPU:0, one launch (start us, length us, event | category | flops | bytes accessed | tf_op | source)
XLA Modules:
  0.0 34.0 jit_solution(2288037433810314586)
XLA Ops:
  0.6 5.3 %shard_map.103 = (f32[256,128]{1,0:T(8,128)S(1)}, f32[256,128]{1,0:T(8,128)S(1)}, f32[256,128]{1,0:T(8,128)S(1)}, f32[256,128]{1,0:T(8,128)S(1)}, f32[264,128]{1...) custom-call(f32[64,256]{1,0:T(8,128)} %bitcast.8, ...), custom_call_target="tpu_custom_call" | custom-call | flops 500000000 | bytes 100000 | tf_op jit(solution)/shard_map/pallas_call | solution.py:284
  6.0 3.1 %collective-permute-start = (f32[264,128]{1,0:T(8,128)S(1)}, f32[264,128]{1,0:T(8,128)S(1)}, u32[]{:S(2)}, u32[]{:S(2)}) collective-permute-start(f32[264,128]{1,0:T(8,128)S(1)} %get-tuple-element.25.refs_0_.refs_2_.refs_1_), channel_id=1, source_target_pairs={{0,16},{8,24},{16,0},{24,8},{1,17},{9,25},{17,1},{25,9},{2,18},{10... | collective-permute-start | bytes 405512 | tf_op jit(solution)/shard_map/ppermute | solution.py:296
  9.0 0.0 collective-permute-start.2
  9.0 3.6 %collective-permute-done.refs_0_.refs_2_ = f32[264,128]{1,0:T(8,128)S(1)} collective-permute-done((f32[264,128]{1,0:T(8,128)S(1)}, f32[264,128]{1,0:T(8,128)S(1)}, u32[]{:S(2)}, u32[]{:S(2)}) %collective-permute-start) | collective-permute-done | bytes 135200 | tf_op jit(solution)/shard_map/ppermute | solution.py:296
  12.6 0.0 collective-permute-start.1
  12.6 1.7 %collective-permute-start.3 = (f32[64,256]{1,0:T(8,128)S(1)}, f32[64,256]{1,0:T(8,128)S(1)}, u32[]{:S(2)}, u32[]{:S(2)}) collective-permute-start(f32[64,256]{1,0:T(8,128)S(1)} %get-tuple-element.27.fact_ref), channel_id=1, source_target_pairs={{0,1},{1,0},{2,3},{3,2},{4,5},{5,4},{6,7},{7,6},{8,9},{9,8},{10,11... | collective-permute-start | bytes 196616 | tf_op jit(solution)/shard_map/ppermute | solution.py:296
  14.3 0.0 collective-permute-done.2.refs_1_
  14.3 0.3 shard_map.104.refs_2_
  14.7 0.3 shard_map.105.refs_2_
  15.0 2.2 %collective-permute-done.3.refs_4_.peer_ref = f32[64,256]{1,0:T(8,128)S(1)} collective-permute-done((f32[64,256]{1,0:T(8,128)S(1)}, f32[64,256]{1,0:T(8,128)S(1)}, u32[]{:S(2)}, u32[]{:S(2)}) %collective-permute-start.3) | collective-permute-done | bytes 65568 | tf_op jit(solution)/shard_map/ppermute | solution.py:296
  17.1 0.0 collective-permute-done.1.refs_0_.refs_3_
  17.1 0.4 %shard_map.106.msg_ref.own_ref = f32[264,128]{1,0:T(8,128)S(1)} custom-call(f32[264,128]{1,0:T(8,128)S(1)} %collective-permute-done.1.refs_0_.refs_3_, f32[264,128]{1,0:T(8,128)S(1)} %get-tuple-element.25.refs_0_.refs_2_.refs_1_, f32[256,256]{1,0:T(8,128)S(1)} %shard_map.105.refs_2_, f32[8,128]{1,0:T(8,128)S(1)} %get-tuple-element.26.refs_3_, ...), custom_call_target="tpu_custom_call" | custom-call | flops 500000000 | bytes 100000 | tf_op jit(solution)/shard_map/pallas_call | solution.py:284
  17.5 1.8 %collective-permute-start.4 = (f32[264,128]{1,0:T(8,128)S(1)}, f32[264,128]{1,0:T(8,128)S(1)}, u32[]{:S(2)}, u32[]{:S(2)}) collective-permute-start(f32[264,128]{1,0:T(8,128)S(1)} %shard_map.106.msg_ref.own_ref), channel_id=1, source_target_pairs={{0,1},{1,0},{2,3},{3,2},{4,5},{5,4},{6,7},{7,6},{8,9},{9,8},{10,11... | collective-permute-start | bytes 405512 | tf_op jit(solution)/shard_map/ppermute | solution.py:296
  19.3 0.0 collective-permute-start.8
  19.3 1.6 %collective-permute-start.10 = (f32[256,128]{1,0:T(8,128)S(1)}, f32[256,128]{1,0:T(8,128)S(1)}, u32[]{:S(2)}, u32[]{:S(2)}) collective-permute-start(f32[256,128]{1,0:T(8,128)S(1)} %get-tuple-element.44), channel_id=1, source_target_pairs={{0,24},{8,16},{16,8},{24,0},{1,25},{9,17},{17,9},{25,1},{2,26},{10... | collective-permute-start | bytes 393224 | tf_op jit(solution)/shard_map/ppermute | solution.py:296
  20.9 0.5 %collective-permute-start.9 = (f32[256,128]{1,0:T(8,128)S(1)}, f32[256,128]{1,0:T(8,128)S(1)}, u32[]{:S(2)}, u32[]{:S(2)}) collective-permute-start(f32[256,128]{1,0:T(8,128)S(1)} %get-tuple-element.43), channel_id=1, source_target_pairs={{0,16},{8,24},{16,0},{24,8},{1,17},{9,25},{17,1},{25,9},{2,18},{10... | collective-permute-start | bytes 393224 | tf_op jit(solution)/shard_map/ppermute | solution.py:296
  21.4 0.4 %shard_map.107.chosen_ref = bf16[512,768]{1,0:T(8,128)(2,1)S(1)} custom-call(s32[8,128]{1,0:T(8,128)S(1)} %get-tuple-element.31.key_ref), custom_call_target="tpu_custom_call" | custom-call | flops 500000000 | bytes 100000 | tf_op jit(solution)/shard_map/pallas_call | solution.py:284
  21.8 1.4 %shard_map.108 = (f32[512,128]{1,0:T(8,128)S(1)}, bf16[512,256]{1,0:T(8,128)(2,1)S(1)}, bf16[512,256]{1,0:T(8,128)(2,1)S(1)}) custom-call(f32[264,128]{1,0:T(8,128)S(1)} %shard_map.106.msg_ref.own_ref, f32[64,256]{1,0:T(8,128)S(1)} %get-tuple-element.27.fact_ref, f32[64,256]{1,0:T(8,128)S(1)} %collective-permute-done.3.refs_4_.peer_ref, ...), custom_call_target="tpu_custom_call" | custom-call | flops 500000000 | bytes 100000 | tf_op jit(solution)/shard_map/pallas_call | solution.py:284
  23.2 0.0 collective-permute-done.4.msg_ref
  23.2 0.3 shard_map.109
  23.5 3.7 %collective-permute-start.5 = (f32[136,128]{1,0:T(8,128)S(1)}, f32[136,128]{1,0:T(8,128)S(1)}, u32[]{:S(2)}, u32[]{:S(2)}) collective-permute-start(f32[136,128]{1,0:T(8,128)S(1)} %get-tuple-element.36), channel_id=1, source_target_pairs={{0,6},{1,7},{2,4},{3,5},{4,2},{5,3},{6,0},{7,1},{8,14},{9,15},{10,... | collective-permute-start | bytes 208904 | tf_op jit(solution)/shard_map/ppermute | solution.py:296
  27.2 0.0 collective-permute-start.6
  27.2 0.0 collective-permute-done.8.refs_5_
  27.2 0.8 %collective-permute-start.7 = (f32[136,128]{1,0:T(8,128)S(1)}, f32[136,128]{1,0:T(8,128)S(1)}, u32[]{:S(2)}, u32[]{:S(2)}) collective-permute-start(f32[136,128]{1,0:T(8,128)S(1)} %get-tuple-element.38), channel_id=1, source_target_pairs={{0,4},{1,5},{2,6},{3,7},{4,0},{5,1},{6,2},{7,3},{8,12},{9,13},{10,... | collective-permute-start | bytes 208904 | tf_op jit(solution)/shard_map/ppermute | solution.py:296
  28.0 0.0 collective-permute-done.10.refs_7_
  28.0 0.0 collective-permute-done.9.refs_6_
  28.0 2.6 %shard_map.111 = f32[256,256]{1,0:T(8,128)} custom-call(f32[264,128]{1,0:T(8,128)S(1)} %get-tuple-element.25.refs_0_.refs_2_.refs_1_, f32[264,128]{1,0:T(8,128)S(1)} %collective-permute-done.2.refs_1_, f32[264,128]{1,0:T(8,128)S(1)} %collective-permute-done.refs_0_.refs_2_, f32[264,128]{1,0:T(8,128)S(1)} %collective-permute-done.1.refs_0_.refs_3_, ...), custom_call_target="tpu_custom_call" | custom-call | flops 2000000000 | bytes 100000 | tf_op jit(solution)/shard_map/pallas_call | solution.py:284
  30.6 0.0 collective-permute-done.5.refs_1_
  30.6 1.5 %collective-permute-done.6.refs_2_ = f32[136,128]{1,0:T(8,128)S(1)} collective-permute-done((f32[136,128]{1,0:T(8,128)S(1)}, f32[136,128]{1,0:T(8,128)S(1)}, u32[]{:S(2)}, u32[]{:S(2)}) %collective-permute-start.6) | collective-permute-done | bytes 69664 | tf_op jit(solution)/shard_map/ppermute | solution.py:296
  32.1 0.7 %collective-permute-done.7.refs_3_ = f32[136,128]{1,0:T(8,128)S(1)} collective-permute-done((f32[136,128]{1,0:T(8,128)S(1)}, f32[136,128]{1,0:T(8,128)S(1)}, u32[]{:S(2)}, u32[]{:S(2)}) %collective-permute-start.7) | collective-permute-done | bytes 69664 | tf_op jit(solution)/shard_map/ppermute | solution.py:296
  32.8 1.2 %shard_map.110 = (f32[1,128]{1,0:T(1,128)}, f32[128,2048]{1,0:T(8,128)}) custom-call(bf16[128,2048]{1,0:T(8,128)(2,1)S(1)} %get-tuple-element.24.member_ref, f32[136,128]{1,0:T(8,128)S(1)} %get-tuple-element.35.refs_0_, f32[136,128]{1,0:T(8,128)S(1)} %collective-permute-done.5.refs_1_, f32[136,128]{1,0:T(8,128)S(1)} %collective-permute-done.6.refs_2_, ...), custom_call_target="tpu_custom_call" | custom-call | flops 500000000 | bytes 100000 | tf_op jit(solution)/shard_map/pallas_call | solution.py:284
Async XLA Ops:
  6.0 6.6 %collective-permute-start = (f32[264,128]{1,0:T(8,128)S(1)}, f32[264,128]{1,0:T(8,128)S(1)}, u32[]{:S(2)}, u32[]{:S(2)}) collective-permute-start(f32[264,128]{1,0:T(8,128)S(1)} %get-tuple-element.25.refs_0_.refs_2_.refs_1_), channel_id=1, source_target_pairs={{0,16},{8,24},{16,0},{24,8},{1,17},{9,25},{17,1},{25,9},{2,18},{10... | collective-permute-start | bytes 405512 | tf_op jit(solution)/shard_map/ppermute | solution.py:296
  9.0 5.3 %collective-permute-start.2 = (f32[264,128]{1,0:T(8,128)S(1)}, f32[264,128]{1,0:T(8,128)S(1)}, u32[]{:S(2)}, u32[]{:S(2)}) collective-permute-start(f32[264,128]{1,0:T(8,128)S(1)} %get-tuple-element.25.refs_0_.refs_2_.refs_1_), channel_id=1, source_target_pairs={{0,8},{8,0},{16,24},{24,16},{1,9},{9,1},{17,25},{25,17},{2,10},{10... | collective-permute-start | bytes 405512 | tf_op jit(solution)/shard_map/ppermute | solution.py:296
  12.6 4.5 %collective-permute-start.1 = (f32[264,128]{1,0:T(8,128)S(1)}, f32[264,128]{1,0:T(8,128)S(1)}, u32[]{:S(2)}, u32[]{:S(2)}) collective-permute-start(f32[264,128]{1,0:T(8,128)S(1)} %collective-permute-done.refs_0_.refs_2_), channel_id=1, source_target_pairs={{0,8},{8,0},{16,24},{24,16},{1,9},{9,1},{17,25},{25,17},{2,10},{10... | collective-permute-start | bytes 405512 | tf_op jit(solution)/shard_map/ppermute | solution.py:296
  12.6 4.5 %collective-permute-start.3 = (f32[64,256]{1,0:T(8,128)S(1)}, f32[64,256]{1,0:T(8,128)S(1)}, u32[]{:S(2)}, u32[]{:S(2)}) collective-permute-start(f32[64,256]{1,0:T(8,128)S(1)} %get-tuple-element.27.fact_ref), channel_id=1, source_target_pairs={{0,1},{1,0},{2,3},{3,2},{4,5},{5,4},{6,7},{7,6},{8,9},{9,8},{10,11... | collective-permute-start | bytes 196616 | tf_op jit(solution)/shard_map/ppermute | solution.py:296
  17.5 5.7 %collective-permute-start.4 = (f32[264,128]{1,0:T(8,128)S(1)}, f32[264,128]{1,0:T(8,128)S(1)}, u32[]{:S(2)}, u32[]{:S(2)}) collective-permute-start(f32[264,128]{1,0:T(8,128)S(1)} %shard_map.106.msg_ref.own_ref), channel_id=1, source_target_pairs={{0,1},{1,0},{2,3},{3,2},{4,5},{5,4},{6,7},{7,6},{8,9},{9,8},{10,11... | collective-permute-start | bytes 405512 | tf_op jit(solution)/shard_map/ppermute | solution.py:296
  19.3 7.9 %collective-permute-start.8 = (f32[256,128]{1,0:T(8,128)S(1)}, f32[256,128]{1,0:T(8,128)S(1)}, u32[]{:S(2)}, u32[]{:S(2)}) collective-permute-start(f32[256,128]{1,0:T(8,128)S(1)} %get-tuple-element.42), channel_id=1, source_target_pairs={{0,8},{8,0},{16,24},{24,16},{1,9},{9,1},{17,25},{25,17},{2,10},{10... | collective-permute-start | bytes 393224 | tf_op jit(solution)/shard_map/ppermute | solution.py:296
  19.3 8.7 %collective-permute-start.10 = (f32[256,128]{1,0:T(8,128)S(1)}, f32[256,128]{1,0:T(8,128)S(1)}, u32[]{:S(2)}, u32[]{:S(2)}) collective-permute-start(f32[256,128]{1,0:T(8,128)S(1)} %get-tuple-element.44), channel_id=1, source_target_pairs={{0,24},{8,16},{16,8},{24,0},{1,25},{9,17},{17,9},{25,1},{2,26},{10... | collective-permute-start | bytes 393224 | tf_op jit(solution)/shard_map/ppermute | solution.py:296
  20.9 7.1 %collective-permute-start.9 = (f32[256,128]{1,0:T(8,128)S(1)}, f32[256,128]{1,0:T(8,128)S(1)}, u32[]{:S(2)}, u32[]{:S(2)}) collective-permute-start(f32[256,128]{1,0:T(8,128)S(1)} %get-tuple-element.43), channel_id=1, source_target_pairs={{0,16},{8,24},{16,0},{24,8},{1,17},{9,25},{17,1},{25,9},{2,18},{10... | collective-permute-start | bytes 393224 | tf_op jit(solution)/shard_map/ppermute | solution.py:296
  23.5 7.1 %collective-permute-start.5 = (f32[136,128]{1,0:T(8,128)S(1)}, f32[136,128]{1,0:T(8,128)S(1)}, u32[]{:S(2)}, u32[]{:S(2)}) collective-permute-start(f32[136,128]{1,0:T(8,128)S(1)} %get-tuple-element.36), channel_id=1, source_target_pairs={{0,6},{1,7},{2,4},{3,5},{4,2},{5,3},{6,0},{7,1},{8,14},{9,15},{10,... | collective-permute-start | bytes 208904 | tf_op jit(solution)/shard_map/ppermute | solution.py:296
  27.2 4.9 %collective-permute-start.6 = (f32[136,128]{1,0:T(8,128)S(1)}, f32[136,128]{1,0:T(8,128)S(1)}, u32[]{:S(2)}, u32[]{:S(2)}) collective-permute-start(f32[136,128]{1,0:T(8,128)S(1)} %get-tuple-element.37), channel_id=1, source_target_pairs={{0,2},{1,3},{2,0},{3,1},{4,6},{5,7},{6,4},{7,5},{8,10},{9,11},{10,... | collective-permute-start | bytes 208904 | tf_op jit(solution)/shard_map/ppermute | solution.py:296
  27.2 5.6 %collective-permute-start.7 = (f32[136,128]{1,0:T(8,128)S(1)}, f32[136,128]{1,0:T(8,128)S(1)}, u32[]{:S(2)}, u32[]{:S(2)}) collective-permute-start(f32[136,128]{1,0:T(8,128)S(1)} %get-tuple-element.38), channel_id=1, source_target_pairs={{0,4},{1,5},{2,6},{3,7},{4,0},{5,1},{6,2},{7,3},{8,12},{9,13},{10,... | collective-permute-start | bytes 208904 | tf_op jit(solution)/shard_map/ppermute | solution.py:296

commit v8 on v7

--- a/solution.py
+++ b/solution.py
@@ -117,6 +117,7 @@
     member = jnp.where(set_ref[...] - me * sets == iota((sets, cols), 0), f32(1), f32(0))
     member_out[...] = member.astype(bf16)
     turned_member = jnp.transpose(member).astype(bf16)
+    twice = jnp.concatenate([turned_member, turned_member], axis=0)
     fact_out[...] = fact_ref[...]
     table = split(jnp.transpose(basis(fact_ref[...])))
     key_out[...] = factor_ref[...] + nfac * (degree_ref[...] - 1)
@@ -137,8 +138,7 @@
         highs, lows = [], []
         for step in group:
             coef_high, coef_low = split(coef_buf[step])
-            both = nn(jnp.concatenate([coef_high, coef_low], axis=0), turned_member)
-            folded = both[:BLOCK] + both[BLOCK:]
+            folded = nn(jnp.concatenate([coef_high, coef_low], axis=1), twice)
             folded_refs[step // per][pl.ds((step % per) * BLOCK, BLOCK), :] = folded
             high, low = split(folded)
             highs.append(high)
@@ -379,15 +379,14 @@
         [msg, fact, peer_fact, chosen],
         limit=8 << 20,
     )
-    msg, *later = lax.optimization_barrier((msg, *folded[2:]))
-    later = [folded[1], *later]
+    msg, *later = lax.optimization_barrier((msg, *folded[1:]))
     moved = [folded[0]] + [send(later[k - 1], "trade", k) for k in range(1, n_trade)]
     chunks = call(
         third_kernel, [vmem((chunk + INFO, sets), f32)] * (n_scen // 2), [VMEM] * 5, [peer, msg, *middle], limit=8 << 20
     )
     chunks = [chunks[0]] + [
         send(chunks[j], "scen", 2 * j)
-        for j in [*range(n_scen // 2 - 1, n_scen // 4, -1), *range(1, n_scen // 4), *range(n_scen // 4, n_scen // 4 + 1)]
+        for j in [*range(n_scen // 4, n_scen // 2), *range(1, n_scen // 4)]
     ]
     (feature_sens,) = call(
         functools.partial(feature_kernel, n_trade),

time: 34.2 us -> 34 us (level)
  transfers between devices with their start and end apart: 11 -> 11, of which waited for: 4 -> 6; matrix products, arithmetic and copies ran while one was open for 0% -> 0% of each run, Pallas kernels for 16% -> 16%
where the time goes in v8:
time: 34 us; the launch traced here: 33.8 us
  starting transfers between devices  12.9 us (38%)
  Pallas kernels  12.2 us (36%)
  waiting for transfers between devices  8.04 us (24%)
  between operations  0.71 us (2%)
    ppermute x11, starting transfers between devices, send(): lax.ppermute(value, axis, [(i, i ^ k) for i in range(lax.axis_size(axis))])  12.9 us
    pallas_call x9, Pallas kernels, call(): pl.pallas_call(kernel, out_shape=out_shape, in_specs=in_specs, out_specs=...  12.2 us
    ppermute x11, waiting for transfers between devices, send(): lax.ppermute(value, axis, [(i, i ^ k) for i in range(lax.axis_size(axis))])  8.04 us
  transfers between devices with their start and end apart: 11, of which 6 were waited for; matrix products, arithmetic and copies ran while one was open for 0% of the time, Pallas kernels for 16%

profile of v8, /device:TPU:0, one launch (start us, length us, event | category | flops | bytes accessed | tf_op | source)
XLA Modules:
  0.0 33.8 jit_solution(3270422062129405250)
XLA Ops:
  0.6 5.4 %shard_map.103 = (f32[256,128]{1,0:T(8,128)S(1)}, f32[256,128]{1,0:T(8,128)S(1)}, f32[256,128]{1,0:T(8,128)S(1)}, f32[256,128]{1,0:T(8,128)S(1)}, f32[264,128]{1...) custom-call(f32[64,256]{1,0:T(8,128)} %bitcast.8, ...), custom_call_target="tpu_custom_call" | custom-call | flops 500000000 | bytes 100000 | tf_op jit(solution)/shard_map/pallas_call | solution.py:284
  6.0 3.0 %collective-permute-start = (f32[264,128]{1,0:T(8,128)S(1)}, f32[264,128]{1,0:T(8,128)S(1)}, u32[]{:S(2)}, u32[]{:S(2)}) collective-permute-start(f32[264,128]{1,0:T(8,128)S(1)} %get-tuple-element.26.refs_0_.refs_2_.refs_1_), channel_id=1, source_target_pairs={{0,16},{8,24},{16,0},{24,8},{1,17},{9,25},{17,1},{25,9},{2,18},{10... | collective-permute-start | bytes 405512 | tf_op jit(solution)/shard_map/ppermute | solution.py:296
  9.0 0.0 collective-permute-start.2
  9.0 3.6 %collective-permute-done.refs_0_.refs_2_ = f32[264,128]{1,0:T(8,128)S(1)} collective-permute-done((f32[264,128]{1,0:T(8,128)S(1)}, f32[264,128]{1,0:T(8,128)S(1)}, u32[]{:S(2)}, u32[]{:S(2)}) %collective-permute-start) | collective-permute-done | bytes 135200 | tf_op jit(solution)/shard_map/ppermute | solution.py:296
  12.6 0.0 collective-permute-start.1
  12.6 1.7 %collective-permute-start.3 = (f32[64,256]{1,0:T(8,128)S(1)}, f32[64,256]{1,0:T(8,128)S(1)}, u32[]{:S(2)}, u32[]{:S(2)}) collective-permute-start(f32[64,256]{1,0:T(8,128)S(1)} %get-tuple-element.28.fact_ref), channel_id=1, source_target_pairs={{0,1},{1,0},{2,3},{3,2},{4,5},{5,4},{6,7},{7,6},{8,9},{9,8},{10,11... | collective-permute-start | bytes 196616 | tf_op jit(solution)/shard_map/ppermute | solution.py:296
  14.3 0.0 collective-permute-done.2.refs_1_
  14.3 0.3 shard_map.104.refs_2_
  14.7 0.3 shard_map.105.refs_2_
  15.0 2.2 %collective-permute-done.3.refs_4_.peer_ref = f32[64,256]{1,0:T(8,128)S(1)} collective-permute-done((f32[64,256]{1,0:T(8,128)S(1)}, f32[64,256]{1,0:T(8,128)S(1)}, u32[]{:S(2)}, u32[]{:S(2)}) %collective-permute-start.3) | collective-permute-done | bytes 65568 | tf_op jit(solution)/shard_map/ppermute | solution.py:296
  17.2 0.0 collective-permute-done.1.refs_0_.refs_3_
  17.2 0.4 %shard_map.106.msg_ref.own_ref = f32[264,128]{1,0:T(8,128)S(1)} custom-call(f32[264,128]{1,0:T(8,128)S(1)} %collective-permute-done.1.refs_0_.refs_3_, f32[264,128]{1,0:T(8,128)S(1)} %get-tuple-element.26.refs_0_.refs_2_.refs_1_, f32[256,256]{1,0:T(8,128)S(1)} %shard_map.105.refs_2_, f32[8,128]{1,0:T(8,128)S(1)} %get-tuple-element.27.refs_3_, ...), custom_call_target="tpu_custom_call" | custom-call | flops 500000000 | bytes 100000 | tf_op jit(solution)/shard_map/pallas_call | solution.py:284
  17.5 1.8 %collective-permute-start.4 = (f32[264,128]{1,0:T(8,128)S(1)}, f32[264,128]{1,0:T(8,128)S(1)}, u32[]{:S(2)}, u32[]{:S(2)}) collective-permute-start(f32[264,128]{1,0:T(8,128)S(1)} %shard_map.106.msg_ref.own_ref), channel_id=1, source_target_pairs={{0,1},{1,0},{2,3},{3,2},{4,5},{5,4},{6,7},{7,6},{8,9},{9,8},{10,11... | collective-permute-start | bytes 405512 | tf_op jit(solution)/shard_map/ppermute | solution.py:296
  19.3 0.5 %collective-permute-start.10 = (f32[256,128]{1,0:T(8,128)S(1)}, f32[256,128]{1,0:T(8,128)S(1)}, u32[]{:S(2)}, u32[]{:S(2)}) collective-permute-start(f32[256,128]{1,0:T(8,128)S(1)} %get-tuple-element.46), channel_id=1, source_target_pairs={{0,24},{8,16},{16,8},{24,0},{1,25},{9,17},{17,9},{25,1},{2,26},{10... | collective-permute-start | bytes 393224 | tf_op jit(solution)/shard_map/ppermute | solution.py:296
  19.8 1.1 %collective-permute-start.8 = (f32[256,128]{1,0:T(8,128)S(1)}, f32[256,128]{1,0:T(8,128)S(1)}, u32[]{:S(2)}, u32[]{:S(2)}) collective-permute-start(f32[256,128]{1,0:T(8,128)S(1)} %get-tuple-element.44), channel_id=1, source_target_pairs={{0,8},{8,0},{16,24},{24,16},{1,9},{9,1},{17,25},{25,17},{2,10},{10... | collective-permute-start | bytes 393224 | tf_op jit(solution)/shard_map/ppermute | solution.py:296
  20.9 0.5 %collective-permute-start.9 = (f32[256,128]{1,0:T(8,128)S(1)}, f32[256,128]{1,0:T(8,128)S(1)}, u32[]{:S(2)}, u32[]{:S(2)}) collective-permute-start(f32[256,128]{1,0:T(8,128)S(1)} %get-tuple-element.45), channel_id=1, source_target_pairs={{0,16},{8,24},{16,0},{24,8},{1,17},{9,25},{17,1},{25,9},{2,18},{10... | collective-permute-start | bytes 393224 | tf_op jit(solution)/shard_map/ppermute | solution.py:296
  21.4 0.4 %shard_map.107.chosen_ref = bf16[512,768]{1,0:T(8,128)(2,1)S(1)} custom-call(s32[8,128]{1,0:T(8,128)S(1)} %get-tuple-element.33.key_ref), custom_call_target="tpu_custom_call" | custom-call | flops 500000000 | bytes 100000 | tf_op jit(solution)/shard_map/pallas_call | solution.py:284
  21.8 1.4 %shard_map.108 = (f32[512,128]{1,0:T(8,128)S(1)}, bf16[512,256]{1,0:T(8,128)(2,1)S(1)}, bf16[512,256]{1,0:T(8,128)(2,1)S(1)}) custom-call(f32[264,128]{1,0:T(8,128)S(1)} %shard_map.106.msg_ref.own_ref, f32[64,256]{1,0:T(8,128)S(1)} %get-tuple-element.28.fact_ref, f32[64,256]{1,0:T(8,128)S(1)} %collective-permute-done.3.refs_4_.peer_ref, ...), custom_call_target="tpu_custom_call" | custom-call | flops 500000000 | bytes 100000 | tf_op jit(solution)/shard_map/pallas_call | solution.py:284
  23.2 0.0 collective-permute-done.4.msg_ref
  23.2 0.3 shard_map.109
  23.5 2.7 %collective-permute-start.5 = (f32[136,128]{1,0:T(8,128)S(1)}, f32[136,128]{1,0:T(8,128)S(1)}, u32[]{:S(2)}, u32[]{:S(2)}) collective-permute-start(f32[136,128]{1,0:T(8,128)S(1)} %get-tuple-element.38), channel_id=1, source_target_pairs={{0,4},{1,5},{2,6},{3,7},{4,0},{5,1},{6,2},{7,3},{8,12},{9,13},{10,... | collective-permute-start | bytes 208904 | tf_op jit(solution)/shard_map/ppermute | solution.py:296
  26.2 1.3 %collective-permute-start.6 = (f32[136,128]{1,0:T(8,128)S(1)}, f32[136,128]{1,0:T(8,128)S(1)}, u32[]{:S(2)}, u32[]{:S(2)}) collective-permute-start(f32[136,128]{1,0:T(8,128)S(1)} %get-tuple-element.39), channel_id=1, source_target_pairs={{0,6},{1,7},{2,4},{3,5},{4,2},{5,3},{6,0},{7,1},{8,14},{9,15},{10,... | collective-permute-start | bytes 208904 | tf_op jit(solution)/shard_map/ppermute | solution.py:296
  27.5 0.0 collective-permute-done.10.refs_7_
  27.5 0.2 collective-permute-start.7
  27.7 0.0 collective-permute-done.8.refs_5_
  27.7 0.2 collective-permute-done.9.refs_6_
  27.9 2.6 %shard_map.111 = f32[256,256]{1,0:T(8,128)} custom-call(f32[264,128]{1,0:T(8,128)S(1)} %get-tuple-element.26.refs_0_.refs_2_.refs_1_, f32[264,128]{1,0:T(8,128)S(1)} %collective-permute-done.2.refs_1_, f32[264,128]{1,0:T(8,128)S(1)} %collective-permute-done.refs_0_.refs_2_, f32[264,128]{1,0:T(8,128)S(1)} %collective-permute-done.1.refs_0_.refs_3_, ...), custom_call_target="tpu_custom_call" | custom-call | flops 2000000000 | bytes 100000 | tf_op jit(solution)/shard_map/pallas_call | solution.py:284
  30.5 0.5 %collective-permute-done.5.refs_1_ = f32[136,128]{1,0:T(8,128)S(1)} collective-permute-done((f32[136,128]{1,0:T(8,128)S(1)}, f32[136,128]{1,0:T(8,128)S(1)}, u32[]{:S(2)}, u32[]{:S(2)}) %collective-permute-start.5) | collective-permute-done | bytes 69664 | tf_op jit(solution)/shard_map/ppermute | solution.py:296
  31.0 1.5 %collective-permute-done.6.refs_2_ = f32[136,128]{1,0:T(8,128)S(1)} collective-permute-done((f32[136,128]{1,0:T(8,128)S(1)}, f32[136,128]{1,0:T(8,128)S(1)}, u32[]{:S(2)}, u32[]{:S(2)}) %collective-permute-start.6) | collective-permute-done | bytes 69664 | tf_op jit(solution)/shard_map/ppermute | solution.py:296
  32.4 0.2 collective-permute-done.7.refs_3_
  32.6 1.2 %shard_map.110 = (f32[1,128]{1,0:T(1,128)}, f32[128,2048]{1,0:T(8,128)}) custom-call(bf16[128,2048]{1,0:T(8,128)(2,1)S(1)} %get-tuple-element.25.member_ref, f32[136,128]{1,0:T(8,128)S(1)} %get-tuple-element.37.refs_0_, f32[136,128]{1,0:T(8,128)S(1)} %collective-permute-done.5.refs_1_, f32[136,128]{1,0:T(8,128)S(1)} %collective-permute-done.6.refs_2_, ...), custom_call_target="tpu_custom_call" | custom-call | flops 500000000 | bytes 100000 | tf_op jit(solution)/shard_map/pallas_call | solution.py:284
Async XLA Ops:
  6.0 6.7 %collective-permute-start = (f32[264,128]{1,0:T(8,128)S(1)}, f32[264,128]{1,0:T(8,128)S(1)}, u32[]{:S(2)}, u32[]{:S(2)}) collective-permute-start(f32[264,128]{1,0:T(8,128)S(1)} %get-tuple-element.26.refs_0_.refs_2_.refs_1_), channel_id=1, source_target_pairs={{0,16},{8,24},{16,0},{24,8},{1,17},{9,25},{17,1},{25,9},{2,18},{10... | collective-permute-start | bytes 405512 | tf_op jit(solution)/shard_map/ppermute | solution.py:296
  9.0 5.3 %collective-permute-start.2 = (f32[264,128]{1,0:T(8,128)S(1)}, f32[264,128]{1,0:T(8,128)S(1)}, u32[]{:S(2)}, u32[]{:S(2)}) collective-permute-start(f32[264,128]{1,0:T(8,128)S(1)} %get-tuple-element.26.refs_0_.refs_2_.refs_1_), channel_id=1, source_target_pairs={{0,8},{8,0},{16,24},{24,16},{1,9},{9,1},{17,25},{25,17},{2,10},{10... | collective-permute-start | bytes 405512 | tf_op jit(solution)/shard_map/ppermute | solution.py:296
  12.6 4.5 %collective-permute-start.1 = (f32[264,128]{1,0:T(8,128)S(1)}, f32[264,128]{1,0:T(8,128)S(1)}, u32[]{:S(2)}, u32[]{:S(2)}) collective-permute-start(f32[264,128]{1,0:T(8,128)S(1)} %collective-permute-done.refs_0_.refs_2_), channel_id=1, source_target_pairs={{0,8},{8,0},{16,24},{24,16},{1,9},{9,1},{17,25},{25,17},{2,10},{10... | collective-permute-start | bytes 405512 | tf_op jit(solution)/shard_map/ppermute | solution.py:296
  12.6 4.5 %collective-permute-start.3 = (f32[64,256]{1,0:T(8,128)S(1)}, f32[64,256]{1,0:T(8,128)S(1)}, u32[]{:S(2)}, u32[]{:S(2)}) collective-permute-start(f32[64,256]{1,0:T(8,128)S(1)} %get-tuple-element.28.fact_ref), channel_id=1, source_target_pairs={{0,1},{1,0},{2,3},{3,2},{4,5},{5,4},{6,7},{7,6},{8,9},{9,8},{10,11... | collective-permute-start | bytes 196616 | tf_op jit(solution)/shard_map/ppermute | solution.py:296
  17.5 5.7 %collective-permute-start.4 = (f32[264,128]{1,0:T(8,128)S(1)}, f32[264,128]{1,0:T(8,128)S(1)}, u32[]{:S(2)}, u32[]{:S(2)}) collective-permute-start(f32[264,128]{1,0:T(8,128)S(1)} %shard_map.106.msg_ref.own_ref), channel_id=1, source_target_pairs={{0,1},{1,0},{2,3},{3,2},{4,5},{5,4},{6,7},{7,6},{8,9},{9,8},{10,11... | collective-permute-start | bytes 405512 | tf_op jit(solution)/shard_map/ppermute | solution.py:296
  19.3 8.3 %collective-permute-start.10 = (f32[256,128]{1,0:T(8,128)S(1)}, f32[256,128]{1,0:T(8,128)S(1)}, u32[]{:S(2)}, u32[]{:S(2)}) collective-permute-start(f32[256,128]{1,0:T(8,128)S(1)} %get-tuple-element.46), channel_id=1, source_target_pairs={{0,24},{8,16},{16,8},{24,0},{1,25},{9,17},{17,9},{25,1},{2,26},{10... | collective-permute-start | bytes 393224 | tf_op jit(solution)/shard_map/ppermute | solution.py:296
  19.8 8.0 %collective-permute-start.8 = (f32[256,128]{1,0:T(8,128)S(1)}, f32[256,128]{1,0:T(8,128)S(1)}, u32[]{:S(2)}, u32[]{:S(2)}) collective-permute-start(f32[256,128]{1,0:T(8,128)S(1)} %get-tuple-element.44), channel_id=1, source_target_pairs={{0,8},{8,0},{16,24},{24,16},{1,9},{9,1},{17,25},{25,17},{2,10},{10... | collective-permute-start | bytes 393224 | tf_op jit(solution)/shard_map/ppermute | solution.py:296
  20.9 7.0 %collective-permute-start.9 = (f32[256,128]{1,0:T(8,128)S(1)}, f32[256,128]{1,0:T(8,128)S(1)}, u32[]{:S(2)}, u32[]{:S(2)}) collective-permute-start(f32[256,128]{1,0:T(8,128)S(1)} %get-tuple-element.45), channel_id=1, source_target_pairs={{0,16},{8,24},{16,0},{24,8},{1,17},{9,25},{17,1},{25,9},{2,18},{10... | collective-permute-start | bytes 393224 | tf_op jit(solution)/shard_map/ppermute | solution.py:296
  23.5 7.4 %collective-permute-start.5 = (f32[136,128]{1,0:T(8,128)S(1)}, f32[136,128]{1,0:T(8,128)S(1)}, u32[]{:S(2)}, u32[]{:S(2)}) collective-permute-start(f32[136,128]{1,0:T(8,128)S(1)} %get-tuple-element.38), channel_id=1, source_target_pairs={{0,4},{1,5},{2,6},{3,7},{4,0},{5,1},{6,2},{7,3},{8,12},{9,13},{10,... | collective-permute-start | bytes 208904 | tf_op jit(solution)/shard_map/ppermute | solution.py:296
  26.2 6.2 %collective-permute-start.6 = (f32[136,128]{1,0:T(8,128)S(1)}, f32[136,128]{1,0:T(8,128)S(1)}, u32[]{:S(2)}, u32[]{:S(2)}) collective-permute-start(f32[136,128]{1,0:T(8,128)S(1)} %get-tuple-element.39), channel_id=1, source_target_pairs={{0,6},{1,7},{2,4},{3,5},{4,2},{5,3},{6,0},{7,1},{8,14},{9,15},{10,... | collective-permute-start | bytes 208904 | tf_op jit(solution)/shard_map/ppermute | solution.py:296
  27.5 5.1 %collective-permute-start.7 = (f32[136,128]{1,0:T(8,128)S(1)}, f32[136,128]{1,0:T(8,128)S(1)}, u32[]{:S(2)}, u32[]{:S(2)}) collective-permute-start(f32[136,128]{1,0:T(8,128)S(1)} %get-tuple-element.40), channel_id=1, source_target_pairs={{0,2},{1,3},{2,0},{3,1},{4,6},{5,7},{6,4},{7,5},{8,10},{9,11},{10,... | collective-permute-start | bytes 208904 | tf_op jit(solution)/shard_map/ppermute | solution.py:296
